TPU v7x, 128 devices: a whole 4x4x4 slice. The times are simulated.
128 devices in a mesh: skyx: 8 (over y, core), skyy: 16 (over x, z).
Axes of the slice: x: 4, y: 4, z: 4, core: 2. Of those that a mesh axis runs over, the one named last changes fastest.
Arguments:
- image: bfloat16 [8192, 16, 512], P(('skyx', 'skyy')), may hold values from -6 to 6
- inverse_var: bfloat16 [8192, 16, 512], P(('skyx', 'skyy')), may hold values from 0.099609375 to 1
- patch_of: int32 [8192, 1], replicated, may hold values from 0 to 127; in each aligned block of 64 rows (0 to 63, 64 to 127, ...) no two rows name the same one
- row_of: int32 [8192], replicated, may hold values from 0 to 3
- valid: int32 [8192], replicated, may hold values 0 or 1
- coef_index: int32 [128], replicated, may hold values from 0 to 63
- coef_table: float32 [64, 20], replicated, may hold values from -1.25 to 1.25
- basis_across: float32 [20, 41], replicated, may hold values from -1 to 1
- basis_down: float32 [20, 41], replicated, may hold values from -1 to 1
Outputs:
- coadd: float32 [1024, 4096], P('skyy', 'skyx')
- weight_sum: float32 [1024, 4096], P('skyy', 'skyx')
Inputs may be any that keep to these rules, and one draw needn't show every extreme that they name: `patch_of`: within the 64 blocks of one exposure (the rows of one device) no patch appears twice.
All inputs are finite; a program needn't handle non-finite values.
Results may differ from a plain program's by a relative error of at most 0.0065.
Values may be sent and summed in bfloat16 or wider, within the bound.
No kernel may reach another device: no remote copies, remote signals or barrier semaphores. Data moves between devices by JAX's collectives and lax.ppermute only.
A program may use at most 192 MiB of HBM per device.

v0:
```python
import jax
import jax.numpy as jnp
from jax import lax
from jax.sharding import PartitionSpec as P

RS = 4


group_blocks = 8


def from_behind(value, axis, steps):
    count = lax.axis_size(axis)
    initial, last = (max(0, -steps), min(count, count - steps))
    return lax.ppermute(value, axis, [(source, source + steps) for source in range(initial, last)])


def band_pair(basis_across):
    margin = (basis_across.shape[1] - 1) // 2
    rows_in = jnp.arange(128, dtype=jnp.int32)[:, None]
    cols_out = jnp.arange(128, dtype=jnp.int32)[None, :]
    offset_now = cols_out - rows_in
    offset_prev = cols_out + 128 - rows_in
    inside_now = (offset_now >= 0) & (offset_now <= 2 * margin)
    inside_prev = (offset_prev >= 0) & (offset_prev <= 2 * margin)
    band_now = jnp.where(
        inside_now[None], jnp.take(basis_across, jnp.clip(offset_now, 0, 2 * margin), axis=1), 0.0
    )
    band_prev = jnp.where(
        inside_prev[None], jnp.take(basis_across, jnp.clip(offset_prev, 0, 2 * margin), axis=1), 0.0
    )
    return (band_now.astype(jnp.bfloat16), band_prev.astype(jnp.bfloat16))


def vertical_mix(basis_down, coeffs, row_count):
    margin = (basis_down.shape[1] - 1) // 2
    rows_out = jnp.arange(row_count + 2 * margin, dtype=jnp.int32)[:, None]
    rows_in = jnp.arange(row_count, dtype=jnp.int32)[None, :]
    offset = rows_out - rows_in
    inside = (offset >= 0) & (offset <= 2 * margin)
    picked = jnp.where(
        inside[None], jnp.take(basis_down, jnp.clip(offset, 0, 2 * margin), axis=1), 0.0
    )
    mixed_taps = coeffs[:, :, None, None] * picked[None]
    mixed_taps = jnp.transpose(mixed_taps, (0, 2, 1, 3))
    return mixed_taps.reshape(mixed_taps.shape[0], row_count + 2 * margin, -1).astype(jnp.bfloat16)


def convolve(planes, coeffs, bands, basis_down, out_width):
    block_count, row_count, block_width = planes.shape
    band_now, band_prev = bands
    tile_count = out_width // 128
    padded = jnp.pad(planes, ((0, 0), (0, 0), (128, out_width - block_width)))
    tiles = padded.reshape(block_count, row_count, tile_count + 1, 128)
    swept_rows = jnp.einsum(
        "krti,cio->kcrto", tiles[:, :, 1:], band_now, preferred_element_type=jnp.float32
    )
    swept_rows = swept_rows + jnp.einsum(
        "krti,cio->kcrto", tiles[:, :, :tile_count], band_prev, preferred_element_type=jnp.float32
    )
    swept_rows = swept_rows.astype(jnp.bfloat16).reshape(block_count, -1, out_width)
    mixer_taps = vertical_mix(basis_down, coeffs, row_count)
    return jnp.einsum(
        "kyj,kjx->kyx", mixer_taps, swept_rows, preferred_element_type=jnp.float32
    ).astype(jnp.bfloat16)


def deliver(first_plane, second_plane):
    return (
        lax.all_to_all(first_plane, ("skyx", "skyy"), split_axis=0, concat_axis=0, tiled=True),
        lax.all_to_all(second_plane, ("skyx", "skyy"), split_axis=0, concat_axis=0, tiled=True),
    )


def route_planes(route_onehot, planes):
    return jnp.einsum(
        "kd,krx->drx", route_onehot, planes, preferred_element_type=jnp.float32
    ).astype(jnp.bfloat16)


def body(
    image, inverse_var, patch_of, row_of, valid, coef_index, coef_table, basis_across, basis_down
):
    devices = lax.axis_size("skyx") * lax.axis_size("skyy")
    block_count, row_count, block_width = image.shape
    margin = (basis_across.shape[1] - 1) // 2
    out_width = (block_width + 2 * margin + 127) // 128 * 128
    patch_rows = RS * row_count
    my_patch = lax.axis_index("skyx") * lax.axis_size("skyy") + lax.axis_index("skyy")
    first_row = my_patch * block_count
    my_valid = lax.dynamic_slice_in_dim(valid, first_row, block_count)
    my_targets = lax.dynamic_slice_in_dim(patch_of[:, 0], first_row, block_count)
    valid_flags = my_valid.astype(jnp.float32)[:, None, None]
    kept_planes = (valid_flags * inverse_var.astype(jnp.float32)).astype(jnp.bfloat16)
    weighted = (valid_flags * inverse_var.astype(jnp.float32) * image.astype(jnp.float32)).astype(
        jnp.bfloat16
    )
    choose = (
        coef_index[:, None] == jnp.arange(coef_table.shape[0], dtype=jnp.int32)[None, :]
    ).astype(jnp.float32)
    coeffs = jnp.dot(choose, coef_table, precision=lax.Precision.HIGHEST)
    bands = band_pair(basis_across)
    target_grid = patch_of[:, 0].reshape(devices, block_count)
    slot_grid = row_of.reshape(devices, block_count)
    hits = target_grid == my_patch
    has_block = jnp.any(hits, axis=1)
    slot_source = jnp.sum(jnp.where(hits, slot_grid, 0), axis=1)
    slot_onehot = (
        (slot_source[:, None] == jnp.arange(RS, dtype=jnp.int32)[None, :]) & has_block[:, None]
    ).astype(jnp.bfloat16)
    route_onehot = (my_targets[:, None] == jnp.arange(devices, dtype=jnp.int32)[None, :]).astype(
        jnp.bfloat16
    )
    kept_send = route_planes(route_onehot, kept_planes)
    weighted_send = route_planes(route_onehot, weighted)
    weighted_in, kept_in = deliver(weighted_send, kept_send)
    ranks = jnp.cumsum(has_block.astype(jnp.int32)) - 1
    live_count = jnp.sum(has_block.astype(jnp.int32))
    ranks = jnp.where(has_block, ranks, -1)
    turns = (live_count + group_blocks - 1) // group_blocks
    flat_in = weighted_in.reshape(devices, row_count * block_width)

    def add_group(turn, slot_state):
        wanted = turn * group_blocks + jnp.arange(group_blocks, dtype=jnp.int32)
        pick_table = wanted[:, None] == ranks[None, :]
        pick_bf = pick_table.astype(jnp.bfloat16)
        planes = jnp.dot(pick_bf, flat_in, preferred_element_type=jnp.float32).astype(jnp.bfloat16)
        planes = planes.reshape(group_blocks, row_count, block_width)
        group_coeffs = jnp.dot(
            pick_table.astype(jnp.float32), coeffs, precision=lax.Precision.HIGHEST
        )
        contrib = convolve(planes, group_coeffs, bands, basis_down, out_width)
        choose_slot = jnp.dot(pick_bf, slot_onehot, preferred_element_type=jnp.float32).astype(
            jnp.bfloat16
        )
        return slot_state + jnp.einsum(
            "gs,gyx->syx", choose_slot, contrib, preferred_element_type=jnp.float32
        )

    slot_sums = lax.fori_loop(
        0, turns, add_group, jnp.zeros((RS, row_count + 2 * margin, out_width), jnp.float32)
    )
    weight_sum = jnp.einsum(
        "ks,kyx->syx", slot_onehot, kept_in, preferred_element_type=jnp.float32
    ).reshape(patch_rows, block_width)
    extended = jnp.zeros((patch_rows + 2 * margin, out_width), jnp.float32)
    for slot_index in range(RS):
        extended = extended.at[
            slot_index * row_count : slot_index * row_count + row_count + 2 * margin
        ].add(slot_sums[slot_index])
    from_below = from_behind(extended[:margin], "skyy", -1)
    from_above = from_behind(extended[patch_rows + margin :], "skyy", 1)
    middle = extended[margin : margin + patch_rows]
    middle = middle.at[patch_rows - margin :].add(from_below)
    middle = middle.at[:margin].add(from_above)
    right_start = min(block_width + margin, out_width - 128)
    right_offset = block_width + margin - right_start
    from_right = from_behind(middle[:, :128], "skyx", -1)
    from_left = from_behind(middle[:, right_start : right_start + 128], "skyx", 1)
    coadd = middle[:, margin : margin + block_width]
    coadd = coadd.at[:, block_width - margin :].add(from_right[:, :margin])
    coadd = coadd.at[:, :margin].add(from_left[:, right_offset : right_offset + margin])
    return (coadd, weight_sum)


def solution(mesh):
    placed = (
        P(("skyx", "skyy"), None, None),
        P(("skyx", "skyy"), None, None),
        P(),
        P(),
        P(),
        P(),
        P(),
        P(),
        P(),
    )
    return jax.shard_map(
        body,
        mesh=mesh,
        in_specs=placed,
        out_specs=(P("skyy", "skyx"), P("skyy", "skyx")),
        check_vma=False,
    )
```

profile of v0, /device:TPU:3, one launch (start us, length us, event | category | flops | bytes accessed | tf_op | source)
XLA Modules:
  0.0 635.0 jit_solution(1939807506144688844)
XLA Ops:
  2.1 1.9 fusion.39
  5.7 2.5 copy.51
  8.3 10.8 %all-to-all-start = ((bf16[128,16,512]{2,1,0:T(8,128)(2,1)}), bf16[128,16,512]{2,1,0:T(8,128)(2,1)S(1)}, u32[]{:S(2)}, u32[]{:S(2)}) async-start(bf16[128,16,512]{2,1,0:T(8,128)(2,1)} %copy.51), calls=%async_computation | async-start | bytes 4194304 | tf_op jit(solution)/shard_map/all_to_all | solution.py:70
  19.9 3.0 convolution_convert_fusion.3
  24.5 4.1 copy.64
  28.6 57.5 %gather_fusion.1 = bf16[16384,20]{1,0:T(8,128)(2,1)} fusion(bf16[20,41]{0,1:T(8,128)(2,1)S(1)} %copy.53, s32[16384]{0:T(1024)S(1)} %bitcast_clamp_fusion.1), kind=kCustom, calls=%fused_computation.clone | custom fusion | bytes 1376256 | tf_op jit(solution)/shard_map/jit(_take)/gather | solution.py:27
  86.1 3.9 copy.54
  90.1 57.5 %gather_fusion.2 = bf16[16384,20]{1,0:T(8,128)(2,1)} fusion(bf16[20,41]{0,1:T(8,128)(2,1)S(1)} %copy.53, s32[16384]{0:T(1024)S(1)} %bitcast_clamp_fusion), kind=kCustom, calls=%fused_computation.2.clone | custom fusion | bytes 1376256 | tf_op jit(solution)/shard_map/jit(_take)/gather | solution.py:30
  147.6 3.9 copy.56
  154.1 10.2 %all-to-all-start.1 = ((bf16[128,16,512]{2,1,0:T(8,128)(2,1)}), bf16[128,16,512]{2,1,0:T(8,128)(2,1)}, u32[]{:S(2)}, u32[]{:S(2)}) async-start(bf16[128,16,512]{2,1,0:T(8,128)(2,1)} %copy.64), calls=%async_computation.1 | async-start | bytes 4194304 | tf_op jit(solution)/shard_map/all_to_all | solution.py:71
  164.3 3.1 copy.52
  167.4 4.1 copy.58
  172.4 189.4 %while.21 = (s32[]{:T(128)}, f32[4,56,640]{2,0,1:T(4,128)}, s32[]{:T(128)}, s32[128]{0:T(128)S(1)}, f32[128,20]{0,1:T(8,128)S(1)}, /*index=5*/f32[20,41]{0,1:T(8...) while((s32[]{:T(128)}, f32[4,56,640]{2,0,1:T(4,128)}, ...), condition=%wide.region_5.7_spmd.clone, body=%wide.region_4.6_spmd.clone.sunk | while | flops 1045801472 | bytes 41292440 | solution.py:140
  172.9 2.0 convolution_convert_fusion.7
  175.4 1.9 gather_fusion
  177.7 2.1 fusion.107
  179.8 2.1 fusion.108
  181.9 6.3 copy.96
  188.2 7.0 %reshape.454 = bf16[8,320,640]{2,1,0:T(8,128)(2,1)S(1)} reshape(bf16[8,20,16,5,128]{4,3,2,1,0:T(8,128)(2,1)} %copy.96) | data formatting | bytes 6553600 | tf_op jit(solution)/shard_map/while/body/reshape | solution.py:61
  196.8 2.7 convolution_add_fusion.2
  200.0 2.0 convolution_convert_fusion.7
  202.4 1.9 gather_fusion
  204.8 2.1 fusion.107
  206.9 2.1 fusion.108
  209.0 6.3 copy.96
  215.3 7.0 %reshape.454 = bf16[8,320,640]{2,1,0:T(8,128)(2,1)S(1)} reshape(bf16[8,20,16,5,128]{4,3,2,1,0:T(8,128)(2,1)} %copy.96) | data formatting | bytes 6553600 | tf_op jit(solution)/shard_map/while/body/reshape | solution.py:61
  223.9 2.7 convolution_add_fusion.2
  227.0 2.0 convolution_convert_fusion.7
  229.5 1.9 gather_fusion
  231.8 2.1 fusion.107
  233.9 2.1 fusion.108
  236.0 6.3 copy.96
  242.4 7.0 %reshape.454 = bf16[8,320,640]{2,1,0:T(8,128)(2,1)S(1)} reshape(bf16[8,20,16,5,128]{4,3,2,1,0:T(8,128)(2,1)} %copy.96) | data formatting | bytes 6553600 | tf_op jit(solution)/shard_map/while/body/reshape | solution.py:61
  250.9 2.7 convolution_add_fusion.2
  254.1 2.0 convolution_convert_fusion.7
  258.9 2.1 fusion.107
  261.0 2.1 fusion.108
  263.1 6.3 copy.96
  269.4 7.0 %reshape.454 = bf16[8,320,640]{2,1,0:T(8,128)(2,1)S(1)} reshape(bf16[8,20,16,5,128]{4,3,2,1,0:T(8,128)(2,1)} %copy.96) | data formatting | bytes 6553600 | tf_op jit(solution)/shard_map/while/body/reshape | solution.py:61
  278.0 2.7 convolution_add_fusion.2
  281.1 2.0 convolution_convert_fusion.7
  285.9 2.1 fusion.107
  288.0 2.1 fusion.108
  290.1 6.3 copy.96
  296.5 7.0 %reshape.454 = bf16[8,320,640]{2,1,0:T(8,128)(2,1)S(1)} reshape(bf16[8,20,16,5,128]{4,3,2,1,0:T(8,128)(2,1)} %copy.96) | data formatting | bytes 6553600 | tf_op jit(solution)/shard_map/while/body/reshape | solution.py:61
  305.0 2.7 convolution_add_fusion.2
  308.2 2.0 convolution_convert_fusion.7
  313.0 2.1 fusion.107
  315.1 2.1 fusion.108
  317.2 6.3 copy.96
  323.5 7.0 %reshape.454 = bf16[8,320,640]{2,1,0:T(8,128)(2,1)S(1)} reshape(bf16[8,20,16,5,128]{4,3,2,1,0:T(8,128)(2,1)} %copy.96) | data formatting | bytes 6553600 | tf_op jit(solution)/shard_map/while/body/reshape | solution.py:61
  332.1 2.7 convolution_add_fusion.2
  335.2 2.0 convolution_convert_fusion.7
  340.0 2.1 fusion.107
  342.1 2.1 fusion.108
  344.2 6.3 copy.96
  350.6 7.0 %reshape.454 = bf16[8,320,640]{2,1,0:T(8,128)(2,1)S(1)} reshape(bf16[8,20,16,5,128]{4,3,2,1,0:T(8,128)(2,1)} %copy.96) | data formatting | bytes 6553600 | tf_op jit(solution)/shard_map/while/body/reshape | solution.py:61
  359.1 2.7 convolution_add_fusion.2
  363.1 248.4 %collective-permute-start = (f32[20,640]{1,0:T(8,128)S(1)}, f32[20,640]{1,0:T(8,128)S(1)}, u32[]{:S(2)}, u32[]{:S(2)}) collective-permute-start(f32[20,640]{1,0:T(8,128)S(1)} %slice.238), channel_id=1, source_target_pairs={{1,0},{2,1},{3,2},{4,3},{5,4},{6,5},{7,6},{8,7},{9,8},{10,9},{11,1... | collective-permute-start | bytes 153608 | tf_op jit(solution)/shard_map/ppermute | solution.py:15
  612.8 1.9 collective-permute-start.1
  615.8 5.3 collective-permute-done.1
  621.7 2.5 collective-permute-start.2
  624.3 3.9 fusion.37
  628.9 3.3 collective-permute-start.3
  (180 shorter events, 43.8 us)
Async XLA Ops:
  0.6 151.0 %copy-start = (f32[64,20]{0,1:T(8,128)S(1)}, f32[64,20]{0,1:T(8,128)}, u32[]{:S(2)}) copy-start(f32[64,20]{0,1:T(8,128)} %param.35) | copy-start | bytes 15364
  8.3 10.9 %copy-start.3 = (s32[8192,1]{0,1:T(1,128)S(1)}, s32[8192,1]{0,1:T(1,128)}, u32[]{:S(2)}) copy-start(s32[8192,1]{0,1:T(1,128)} %param.31) | copy-start | bytes 98308
  8.3 145.8 %all-to-all-start = ((bf16[128,16,512]{2,1,0:T(8,128)(2,1)}), bf16[128,16,512]{2,1,0:T(8,128)(2,1)S(1)}, u32[]{:S(2)}, u32[]{:S(2)}) async-start(bf16[128,16,512]{2,1,0:T(8,128)(2,1)} %copy.51), calls=%async_computation | async-start | bytes 4194304 | tf_op jit(solution)/shard_map/all_to_all | solution.py:70
  19.2 5.0 copy-start.4
  19.2 5.1 copy-start.5
  19.2 5.2 copy-start.2
  147.6 4.1 copy-start.6
  154.1 470.2 %all-to-all-start.1 = ((bf16[128,16,512]{2,1,0:T(8,128)(2,1)}), bf16[128,16,512]{2,1,0:T(8,128)(2,1)}, u32[]{:S(2)}, u32[]{:S(2)}) async-start(bf16[128,16,512]{2,1,0:T(8,128)(2,1)} %copy.64), calls=%async_computation.1 | async-start | bytes 4194304 | tf_op jit(solution)/shard_map/all_to_all | solution.py:71
  363.1 249.7 %collective-permute-start = (f32[20,640]{1,0:T(8,128)S(1)}, f32[20,640]{1,0:T(8,128)S(1)}, u32[]{:S(2)}, u32[]{:S(2)}) collective-permute-start(f32[20,640]{1,0:T(8,128)S(1)} %slice.238), channel_id=1, source_target_pairs={{1,0},{2,1},{3,2},{4,3},{5,4},{6,5},{7,6},{8,7},{9,8},{10,9},{11,1... | collective-permute-start | bytes 153608 | tf_op jit(solution)/shard_map/ppermute | solution.py:15
  612.8 8.3 %collective-permute-start.1 = (f32[20,640]{1,0:T(8,128)S(1)}, f32[20,640]{1,0:T(8,128)S(1)}, u32[]{:S(2)}, u32[]{:S(2)}) collective-permute-start(f32[20,640]{1,0:T(8,128)S(1)} %get-tuple-element.318), channel_id=1, source_target_pairs={{0,1},{1,2},{2,3},{3,4},{4,5},{5,6},{6,7},{7,8},{8,9},{9,10},{10,1... | collective-permute-start | bytes 153608 | tf_op jit(solution)/shard_map/ppermute | solution.py:15
  621.7 10.5 %collective-permute-start.2 = (f32[64,128]{1,0:T(8,128)S(1)}, f32[64,128]{1,0:T(8,128)S(1)}, u32[]{:S(2)}, u32[]{:S(2)}) collective-permute-start(f32[64,128]{1,0:T(8,128)S(1)} %get-tuple-element.317), channel_id=1, source_target_pairs={{16,0},{32,16},{48,32},{64,48},{80,64},{96,80},{112,96},{17,1},{33... | collective-permute-start | bytes 98312 | tf_op jit(solution)/shard_map/ppermute | solution.py:15
  628.9 4.3 collective-permute-start.3
  634.3 0.7 copy-start.1
where the time goes:
time: 640 us; the launch traced here: 635 us
  starting transfers between devices  277 us (43%)
  local copies, waits for them, and re-layouts  257 us (40%)
  matrix products  83.2 us (13%)
  other arithmetic  8.11 us (1%)
  waiting for transfers between devices  7.08 us (1%)
    ppermute x4, starting transfers between devices, from_behind(): lax.ppermute(value, axis, [(source, source + steps) for source in range(i...  256 us
    gather x2, local copies, waits for them, and re-layouts, band_pair(): jnp.take(basis_across, jnp.clip(offset_prev, 0, 2 * margin), axis=1)  61.4 us
    gather x2, local copies, waits for them, and re-layouts, band_pair(): jnp.take(basis_across, jnp.clip(offset_now, 0, 2 * margin), axis=1)  61.4 us
    reshape x7, local copies, waits for them, and re-layouts, convolve(): swept_rows.astype(jnp.bfloat16).reshape(block_count, -1, out_width)  48.8 us
    convert_element_type x7, local copies, waits for them, and re-layouts, convolve(): swept_rows.astype(jnp.bfloat16).reshape(block_count, -1, out_width)  44.4 us
    dot_general x7, matrix products, add_group(): jnp.einsum('gs,gyx->syx', choose_slot, contrib, preferred_element_type=jn...  18.6 us
    gather x14, local copies, waits for them, and re-layouts, vertical_mix(): jnp.take(basis_down, jnp.clip(offset, 0, 2 * margin), axis=1)  15.3 us
    dot_general x7, matrix products, convolve(): jnp.einsum('krti,cio->kcrto', tiles[:, :, :tile_count], band_prev, prefer...  14.7 us
  transfers between devices with their start and end apart: 6, of which 3 were waited for; matrix products, arithmetic and copies ran while one was open for 53% of the time, Pallas kernels for 0%

commit v1 on v0

v1 whole, which is shorter than its diff:
```python
import functools

import jax
import jax.numpy as jnp
from jax import lax
from jax.experimental import pallas as pl
from jax.experimental.pallas import tpu as pltpu
from jax.sharding import PartitionSpec as P

RS = 4
LANES = 128
BOTH = ("skyx", "skyy")


def from_behind(value, axis, steps):
    count = lax.axis_size(axis)
    initial, last = (max(0, -steps), min(count, count - steps))
    return lax.ppermute(value, axis, [(source, source + steps) for source in range(initial, last)])


def pack_kernel(group, targets, valid, *refs):
    *planes, out, block_of = refs
    step = pl.program_id(0)
    blocks = targets.shape[0]

    @pl.when(step == 0)
    def _():
        @pl.loop(0, block_of.shape[0])
        def _(patch):
            block_of[patch] = -1

        @pl.loop(0, blocks)
        def _(block):
            block_of[targets[block]] = block

    @pl.loop(0, group)
    def _(offset):
        block = block_of[step * group + offset]
        at = jnp.maximum(block, 0)
        factor = jnp.where(block >= 0, valid[at], 0).astype(jnp.float32)
        value = factor * planes[0][at].astype(jnp.float32)
        for plane in planes[1:]:
            value = value * plane[at].astype(jnp.float32)
        out[offset] = value.astype(out.dtype)


def pack(devices, targets, valid, *planes):
    blocks, rows, width = planes[0].shape
    group = 16
    return pl.pallas_call(
        functools.partial(pack_kernel, group),
        out_shape=jax.ShapeDtypeStruct((devices, rows, width), jnp.bfloat16),
        grid_spec=pltpu.PrefetchScalarGridSpec(
            num_scalar_prefetch=2,
            grid=(devices // group,),
            in_specs=[
                pl.BlockSpec((blocks, rows, width), lambda step, *_: (0, 0, 0), pipeline_mode=pl.Buffered(1))
                for _ in planes
            ],
            out_specs=pl.BlockSpec((group, rows, width), lambda step, *_: (step, 0, 0)),
            scratch_shapes=[pltpu.SMEM((devices,), jnp.int32)],
        ),
        cost_estimate=pl.CostEstimate(
            flops=devices * rows * width,
            bytes_accessed=2 * (len(planes) * blocks + devices) * rows * width,
            transcendentals=0,
        ),
        name="pack",
    )(targets, valid, *planes)


def coadd_kernel(flux, choose, down, across, out, wide, channels, mixed):
    sources, rows, width = flux.shape
    count, ext, _ = down.shape
    tiles = out.shape[1] // LANES
    pieces = width // LANES
    for piece in range(pieces):
        lanes = pl.ds(piece * LANES, LANES)
        wide[piece] = flux[:, :, lanes].reshape(sources * rows, LANES).astype(jnp.float32)
    table = choose[...]
    for pair in range(rows // 2):
        halves = []
        for half in range(2):
            at = pl.ds(2 * pair + half, sources, stride=rows)
            row = [wide[piece, at, :].astype(jnp.bfloat16) for piece in range(pieces)]
            halves.append(jnp.concatenate(row, axis=1))
        summed = jnp.dot(table, jnp.concatenate(halves, axis=0), preferred_element_type=jnp.float32)
        channels[:, pair * 8 : pair * 8 + 8, :] = summed.reshape(count, 8, width)
    zeros = jnp.zeros((ext, LANES), jnp.bfloat16)
    for c in range(count):
        mixed[c, :, :LANES] = zeros
        mixed[c, :, LANES + width :] = zeros
        mixed[c, :, LANES : LANES + width] = jnp.dot(
            down[c], channels[c].astype(jnp.bfloat16), preferred_element_type=jnp.float32
        ).astype(jnp.bfloat16)
    total = jnp.zeros((tiles * ext, LANES), jnp.float32)
    for c in range(count):
        windows = jnp.concatenate([mixed[c, :, LANES * t : LANES * t + 2 * LANES] for t in range(tiles)], axis=0)
        total = total + jnp.dot(windows, across[c], preferred_element_type=jnp.float32)
    for t in range(tiles):
        out[:, t * LANES : (t + 1) * LANES] = total[t * ext : (t + 1) * ext]


def convolve_sum(flux, choose, down, across, out_width):
    sources, rows, width = flux.shape
    count, ext, _ = down.shape
    tiles = out_width // LANES
    return pl.pallas_call(
        coadd_kernel,
        out_shape=jax.ShapeDtypeStruct((ext, out_width), jnp.float32),
        in_specs=[pl.BlockSpec(memory_space=pltpu.VMEM)] * 4,
        out_specs=pl.BlockSpec(memory_space=pltpu.VMEM),
        scratch_shapes=[
            pltpu.VMEM((width // LANES, sources * rows, LANES), jnp.float32),
            pltpu.VMEM((count, RS * rows, width), jnp.float32),
            pltpu.VMEM((count, ext, (tiles + 1) * LANES), jnp.bfloat16),
        ],
        compiler_params=pltpu.CompilerParams(vmem_limit_bytes=40 << 20),
        cost_estimate=pl.CostEstimate(
            flops=2 * count * ext * out_width * 2 * LANES,
            bytes_accessed=2 * sources * rows * width + 4 * ext * out_width,
            transcendentals=0,
        ),
        name="convolve_sum",
    )(flux, choose, down, across)


def weight_kernel(slots, kept, out):
    step = pl.program_id(0)
    group, rows, _ = kept.shape

    @pl.when(step == 0)
    def _():
        out[...] = jnp.zeros_like(out)

    @pl.loop(0, group)
    def _(offset):
        slot = slots[step * group + offset]

        @pl.when(slot >= 0)
        def _():
            at = pl.ds(pl.multiple_of(slot * rows, rows), rows)
            out[at, :] += kept[offset].astype(jnp.float32)


def place_weights(slots, kept):
    sources, rows, width = kept.shape
    group = 32
    return pl.pallas_call(
        weight_kernel,
        out_shape=jax.ShapeDtypeStruct((RS * rows, width), jnp.float32),
        grid_spec=pltpu.PrefetchScalarGridSpec(
            num_scalar_prefetch=1,
            grid=(sources // group,),
            in_specs=[pl.BlockSpec((group, rows, width), lambda step, *_: (step, 0, 0))],
            out_specs=pl.BlockSpec((RS * rows, width), lambda step, *_: (0, 0)),
        ),
        cost_estimate=pl.CostEstimate(
            flops=sources * rows * width,
            bytes_accessed=2 * sources * rows * width,
            transcendentals=0,
        ),
        name="place_weights",
    )(slots, kept)


def spread(taps, offset):
    picked = jnp.zeros((taps.shape[0],) + offset.shape, jnp.float32)
    shape = (-1,) + (1,) * offset.ndim
    for tap in range(taps.shape[1]):
        picked = jnp.where(offset[None] == tap, taps[:, tap].reshape(shape), picked)
    return picked.astype(jnp.bfloat16)


def body(
    image, inverse_var, patch_of, row_of, valid, coef_index, coef_table, basis_across, basis_down
):
    devices = lax.axis_size("skyx") * lax.axis_size("skyy")
    block_count, row_count, block_width = image.shape
    channels = basis_across.shape[0]
    margin = (basis_across.shape[1] - 1) // 2
    out_width = (block_width + 2 * margin + 127) // 128 * 128
    patch_rows = RS * row_count
    ext = (patch_rows + 2 * margin + 15) // 16 * 16
    my_patch = lax.axis_index("skyx") * lax.axis_size("skyy") + lax.axis_index("skyy")
    first_row = my_patch * block_count
    patches = patch_of[:, 0]
    my_valid = lax.dynamic_slice_in_dim(valid, first_row, block_count)
    my_targets = lax.dynamic_slice_in_dim(patches, first_row, block_count)

    weighted_in = lax.all_to_all(
        pack(devices, my_targets, my_valid, inverse_var, image), BOTH, split_axis=0, concat_axis=0, tiled=True
    )
    kept_in = lax.all_to_all(
        pack(devices, my_targets, my_valid, inverse_var), BOTH, split_axis=0, concat_axis=0, tiled=True
    )

    choose = (
        coef_index[:, None] == jnp.arange(coef_table.shape[0], dtype=jnp.int32)[None, :]
    ).astype(jnp.float32)
    coeffs = jnp.dot(choose, coef_table, precision=lax.Precision.HIGHEST)
    target_grid = patches.reshape(devices, block_count)
    slot_grid = row_of.reshape(devices, block_count)
    hits = target_grid == my_patch
    slot = jnp.max(jnp.where(hits, slot_grid, -1), axis=1)
    in_slot = slot[None, :] == jnp.arange(RS, dtype=jnp.int32)[:, None]
    one = jnp.where(in_slot[None], coeffs.T[:, None, :], 0.0)
    none = jnp.zeros_like(one)
    table = jnp.concatenate(
        [jnp.concatenate([one, none], axis=2), jnp.concatenate([none, one], axis=2)], axis=1
    ).reshape(channels * 2 * RS, 2 * devices).astype(jnp.bfloat16)
    places = jnp.arange(patch_rows, dtype=jnp.int32)
    row_at = (places % RS) * row_count + places // RS
    down = spread(basis_down, jnp.arange(ext, dtype=jnp.int32)[:, None] - row_at[None, :])
    across = spread(
        basis_across,
        jnp.arange(LANES, dtype=jnp.int32)[None, :] + LANES - jnp.arange(2 * LANES, dtype=jnp.int32)[:, None],
    )
    extended = convolve_sum(weighted_in, table, down, across, out_width)

    from_below = from_behind(extended[:margin], "skyy", -1)
    from_above = from_behind(extended[patch_rows + margin : patch_rows + 2 * margin], "skyy", 1)
    middle = extended[margin : margin + patch_rows]
    middle = middle.at[patch_rows - margin :].add(from_below)
    middle = middle.at[:margin].add(from_above)
    right_start = min(block_width + margin, out_width - 128)
    right_offset = block_width + margin - right_start
    from_right = from_behind(middle[:, :128], "skyx", -1)
    from_left = from_behind(middle[:, right_start : right_start + 128], "skyx", 1)
    coadd = middle[:, margin : margin + block_width]
    coadd = coadd.at[:, block_width - margin :].add(from_right[:, :margin])
    coadd = coadd.at[:, :margin].add(from_left[:, right_offset : right_offset + margin])
    weight_sum = place_weights(slot, kept_in)
    return (coadd, weight_sum)


def solution(mesh):
    placed = (P(BOTH, None, None), P(BOTH, None, None), P(), P(), P(), P(), P(), P(), P())
    return jax.shard_map(
        body,
        mesh=mesh,
        in_specs=placed,
        out_specs=(P("skyy", "skyx"), P("skyy", "skyx")),
        check_vma=False,
    )
```

time: 640 us -> 101 us (0.16)
  local copies, waits for them, and re-layouts: 257 us -> 10.1 us
  starting transfers between devices: 277 us -> 33.3 us
  matrix products: 83.2 us -> 0.23 us
  Pallas kernels: 0 us -> 22 us
  other arithmetic: 8.11 us -> 25 us
    ppermute x4, starting transfers between devices: 256 us -> 13.6 us  [from_behind(): lax.ppermute(value, axis, [(source, source + steps) for source in range(i...]
    gather x18 -> x0, local copies, waits for them, and re-layouts: 138 us -> none  [the longest x2 61.4 us: band_pair(): jnp.take(basis_across, jnp.clip(offset_prev, 0, 2 * margin), axis=1)]
    dot_general x45 -> x0, matrix products: 83 us -> none  [the longest x7 18.6 us: add_group(): jnp.einsum('gs,gyx->syx', choose_slot, contrib, preferred_element_type=jn...]
    convert_element_type x10 -> x0, local copies, waits for them, and re-layouts: 51.2 us -> none  [the longest x7 44.4 us: convolve(): swept_rows.astype(jnp.bfloat16).reshape(block_count, -1, out_width)]
    reshape x21 -> x0, local copies, waits for them, and re-layouts: 50.8 us -> none  [the longest x7 48.8 us: convolve(): swept_rows.astype(jnp.bfloat16).reshape(block_count, -1, out_width)]
    pallas_call x0 -> x4, Pallas kernels: none -> 22 us  [the longest x2 12.2 us: pack(): pl.pallas_call(functools.partial(pack_kernel, group), out_shape=jax.Shape...]
    convert_element_type x5 -> x3, other arithmetic: 4.78 us -> 20.6 us  [the longest x2 20.6 us: spread(): return picked.astype(jnp.bfloat16)]
  transfers between devices with their start and end apart: 6 -> 6, of which waited for: 3 -> 4; matrix products, arithmetic and copies ran while one was open for 53% -> 31% of each run, Pallas kernels for 0% -> 16%
where the time goes in v1:
time: 101 us; the launch traced here: 100 us
  starting transfers between devices  33.3 us (33%)
  other arithmetic  25 us (25%)
  Pallas kernels  22 us (22%)
  local copies, waits for them, and re-layouts  10.1 us (10%)
  waiting for transfers between devices  8.35 us (8%)
  between operations  1.27 us (1%)
    convert_element_type x2, other arithmetic, spread(): return picked.astype(jnp.bfloat16)  20.6 us
    ppermute x4, starting transfers between devices, from_behind(): lax.ppermute(value, axis, [(source, source + steps) for source in range(i...  13.6 us
    pallas_call x2, Pallas kernels, pack(): pl.pallas_call(functools.partial(pack_kernel, group), out_shape=jax.Shape...  12.2 us
    all_to_all x1, starting transfers between devices, body(): lax.all_to_all(pack(devices, my_targets, my_valid, inverse_var, image), B...  10.8 us
    all_to_all x1, starting transfers between devices, body(): lax.all_to_all(pack(devices, my_targets, my_valid, inverse_var), BOTH, sp...  8.8 us
    ppermute x4, waiting for transfers between devices, from_behind(): lax.ppermute(value, axis, [(source, source + steps) for source in range(i...  6.91 us
    pallas_call x1, Pallas kernels, place_weights(): pl.pallas_call(weight_kernel, out_shape=jax.ShapeDtypeStruct((RS * rows,...  4.93 us
    pallas_call x1, Pallas kernels, convolve_sum(): pl.pallas_call(coadd_kernel, out_shape=jax.ShapeDtypeStruct((ext, out_wid...  4.84 us
  transfers between devices with their start and end apart: 6, of which 4 were waited for; matrix products, arithmetic and copies ran while one was open for 31% of the time, Pallas kernels for 16%

profile of v1, /device:TPU:3, one launch (start us, length us, event | category | flops | bytes accessed | tf_op | source)
XLA Modules:
  0.0 100.3 jit_solution(9400369962842697351)
XLA Ops:
  0.6 0.0 copy-start
  0.7 1.2 %dynamic-slice_bitcast_fusion.targets = s32[64]{0:T(128)} fusion(s32[8192,1]{0,1:T(1,128)} %param.19, s32[]{:T(128)S(6)} %select_n.440), kind=kLoop, calls=%fused_computation.194 | loop fusion | bytes 516 | tf_op jit(solution)/shard_map/dynamic_slice | solution.py:189
  1.9 1.3 %dynamic_slice.10.valid = s32[64]{0:T(128)} dynamic-slice(s32[8192]{0:T(1024)} %param.21, s32[]{:T(128)S(6)} %select_n.440), dynamic_slice_sizes={64} | dynamic-slice | bytes 516 | tf_op jit(solution)/shard_map/dynamic_slice | solution.py:188
  3.2 6.2 %pack.2 = bf16[128,16,512]{2,1,0:T(8,128)(2,1)} custom-call(s32[64]{0:T(128)} %dynamic-slice_bitcast_fusion.targets, s32[64]{0:T(128)} %dynamic_slice.10.valid, bf16[64,16,512]{2,1,0:T(8,128)(2,1)} %refs_0_.3, bf16[64,16,512]{2,1,0:T(8,128)(2,1)} %refs_1_.1), custom_call_target="tpu_custom_call" | custom-call | flops 1048576 | bytes 4194304 | tf_op jit(solution)/shard_map/pack/pallas_call | solution.py:50
  9.4 0.0 copy-start.29
  9.4 10.8 %all-to-all-start = ((bf16[128,16,512]{2,1,0:T(8,128)(2,1)}), bf16[128,16,512]{2,1,0:T(8,128)(2,1)S(1)}, u32[]{:S(2)}, u32[]{:S(2)}) async-start(bf16[128,16,512]{2,1,0:T(8,128)(2,1)} %pack.2), calls=%async_computation | async-start | bytes 4194304 | tf_op jit(solution)/shard_map/all_to_all | solution.py:191
  20.3 0.1 compare_reduce_fusion
  20.4 0.2 slice_reduce_fusion.79
  20.6 1.1 %slice_reduce_fusion.81 = (bf16[20]{0:T(256)(128)(2,1)S(1)}, bf16[20]{0:T(256)(128)(2,1)S(1)}, bf16[20]{0:T(256)(128)(2,1)S(1)}, bf16[20]{0:T(256)(128)(2,1)S(1)...) fusion(f32[20,41]{1,0:T(8,128)S(1)} %copy-done.1), kind=kLoop, calls=%fused_computation.183 | loop fusion | bytes 2280 | tf_op jit(solution)/shard_map/slice | solution.py:171
  21.7 1.1 %slice_reduce_fusion.80 = (bf16[20]{0:T(256)(128)(2,1)}, bf16[20]{0:T(256)(128)(2,1)}, bf16[20]{0:T(256)(128)(2,1)}, bf16[20]{0:T(256)(128)(2,1)}, bf16[20]{0:T(...) fusion(f32[20,41]{1,0:T(8,128)S(1)} %copy-done.1), kind=kLoop, calls=%fused_computation.182 | loop fusion | bytes 2280 | tf_op jit(solution)/shard_map/slice | solution.py:171
  22.8 0.6 fusion.88
  23.4 0.7 slice_reduce_fusion.38
  24.1 1.1 %slice_reduce_fusion.40 = (bf16[20]{0:T(256)(128)(2,1)}, bf16[20]{0:T(256)(128)(2,1)}, bf16[20]{0:T(256)(128)(2,1)}, bf16[20]{0:T(256)(128)(2,1)}, bf16[20]{0:T(...) fusion(f32[20,41]{1,0:T(8,128)S(1)} %copy-done.2), kind=kLoop, calls=%fused_computation.142 | loop fusion | bytes 2280 | tf_op jit(solution)/shard_map/slice | solution.py:171
  25.1 0.1 eq.945
  25.2 0.1 reshape.1883
  25.3 0.1 select_reduce_fusion.slots
  25.4 0.0 copy-done
  25.5 0.0 copy-done.29
  25.5 0.2 convolution_bitcast_fusion
  25.8 6.0 %pack.3 = bf16[128,16,512]{2,1,0:T(8,128)(2,1)} custom-call(s32[64]{0:T(128)} %dynamic-slice_bitcast_fusion.targets, s32[64]{0:T(128)} %dynamic_slice.10.valid, bf16[64,16,512]{2,1,0:T(8,128)(2,1)} %refs_0_.3), custom_call_target="tpu_custom_call" | custom-call | flops 1048576 | bytes 3145728 | tf_op jit(solution)/shard_map/pack/pallas_call | solution.py:50
  31.8 0.0 copy-start.10
  31.8 0.0 copy-start.11
  31.8 0.0 copy-start.12
  31.8 0.0 copy-start.13
  31.8 0.0 copy-start.14
  31.8 0.0 copy-start.15
  31.8 0.0 copy-start.16
  31.8 0.0 copy-start.17
  31.8 0.0 copy-start.18
  31.8 0.0 copy-start.19
  31.9 0.0 copy-start.20
  31.9 0.0 copy-start.21
  31.9 0.0 copy-start.22
  31.9 0.0 copy-start.23
  31.9 0.0 copy-start.24
  31.9 0.0 copy-start.25
  31.9 0.0 copy-start.26
  31.9 0.5 slice_reduce_fusion.39
  32.5 1.0 fusion.42
  33.7 13.8 %select_convert_fusion.across = bf16[20,256,128]{2,1,0:T(8,128)(2,1)S(1)} fusion(bf16[20]{0:T(256)(128)(2,1)S(1)} %copy-done.8, bf16[20]{0:T(256)(128)(2,1)S(1)} %copy-done.9, bf16[20]{0:T(256)(128)(2,1)S(1)} %copy-done.11, bf16[20]{0:T(256)(128)(2,1)S(1)} %copy-done.12, bf16[20]{0:T(256)(128)(2,1)S(1)} %copy-done.13, bf16[20]{0:T(256)(128)(2,1)S(1)} %copy-done.14, ...), kind=kLoop, calls=%fused_computation | loop fusion | flops 26869760 | bytes 2655848 | tf_op jit(solution)/shard_map/convert_element_type | solution.py:172
  47.5 1.4 %all-to-all-done.flux = bf16[128,16,512]{2,1,0:T(8,128)(2,1)S(1)} async-done(((bf16[128,16,512]{2,1,0:T(8,128)(2,1)}), bf16[128,16,512]{2,1,0:T(8,128)(2,1)S(1)}, u32[]{:S(2)}, u32[]{:S(2)}) %all-to-all-start) | async-done | bytes 2097184 | tf_op jit(solution)/shard_map/all_to_all | solution.py:191
  48.9 8.8 %all-to-all-start.1 = ((bf16[128,16,512]{2,1,0:T(8,128)(2,1)}), bf16[128,16,512]{2,1,0:T(8,128)(2,1)}, u32[]{:S(2)}, u32[]{:S(2)}) async-start(bf16[128,16,512]{2,1,0:T(8,128)(2,1)} %pack.3), calls=%async_computation.1 | async-start | bytes 4194304 | tf_op jit(solution)/shard_map/all_to_all | solution.py:194
  57.8 1.2 %fusion.85 = (pred[112,64]{1,0:T(8,128)(4,1)S(1)}, pred[112,64]{1,0:T(8,128)(4,1)S(1)}, pred[112,64]{1,0:T(8,128)(4,1)S(1)}, pred[112,64]{1,0:T(8,128)(4,1)S(1)}...) fusion(s32[64]{0:T(128)} %fusion.88), kind=kLoop, calls=%fused_computation.97 | loop fusion | flops 301056 | bytes 294144 | tf_op jit(solution)/shard_map/eq | solution.py:171
  59.0 6.8 %select_convert_fusion.1.down = bf16[20,112,64]{2,1,0:T(8,128)(2,1)S(1)} fusion(bf16[20]{0:T(256)(128)(2,1)S(1)} %get-tuple-element.130, bf16[20]{0:T(256)(128)(2,1)S(1)} %get-tuple-element.131, bf16[20]{0:T(256)(128)(2,1)S(1)} %get-tuple-element.92, bf16[20]{0:T(256)(128)(2,1)S(1)} %get-tuple-element.93, bf16[20]{0:T(256)(128)(2,1)S(1)} %get-tuple-element.94, ...), kind=kLoop, calls=%fused_computation.1 | loop fusion | flops 5877760 | bytes 582248 | tf_op jit(solution)/shard_map/convert_element_type | solution.py:172
  65.8 4.8 %convolve_sum.1 = f32[112,640]{1,0:T(8,128)S(1)} custom-call(bf16[128,16,512]{2,1,0:T(8,128)(2,1)S(1)} %all-to-all-done.flux, bf16[160,256]{1,0:T(8,128)(2,1)S(1)} %fusion.44.choose, bf16[20,112,64]{2,1,0:T(8,128)(2,1)S(1)} %select_convert_fusion.1.down, bf16[20,256,128]{2,1,0:T(8,128)(2,1)S(1)} %select_convert_fusion.across), custom_call_target="tpu_custom_call" | custom-call | flops 734003200 | bytes 2383872 | tf_op jit(solution)/shard_map/convolve_sum/pallas_call | solution.py:108
  70.6 5.0 %collective-permute-start = (f32[20,640]{1,0:T(8,128)S(1)}, f32[20,640]{1,0:T(8,128)S(1)}, u32[]{:S(2)}, u32[]{:S(2)}) collective-permute-start(f32[20,640]{1,0:T(8,128)S(1)} %get-tuple-element.133), channel_id=1, source_target_pairs={{1,0},{2,1},{3,2},{4,3},{5,4},{6,5},{7,6},{8,7},{9,8},{10,9},{11,1... | collective-permute-start | bytes 153608 | tf_op jit(solution)/shard_map/ppermute | solution.py:18
  75.6 1.9 %collective-permute-start.1 = (f32[20,640]{1,0:T(8,128)S(1)}, f32[20,640]{1,0:T(8,128)S(1)}, u32[]{:S(2)}, u32[]{:S(2)}) collective-permute-start(f32[20,640]{1,0:T(8,128)S(1)} %get-tuple-element.132), channel_id=1, source_target_pairs={{0,1},{1,2},{2,3},{3,4},{4,5},{5,6},{6,7},{7,8},{8,9},{9,10},{10,1... | collective-permute-start | bytes 153608 | tf_op jit(solution)/shard_map/ppermute | solution.py:18
  77.6 6.3 %collective-permute-done = f32[20,640]{1,0:T(8,128)S(1)} collective-permute-done((f32[20,640]{1,0:T(8,128)S(1)}, f32[20,640]{1,0:T(8,128)S(1)}, u32[]{:S(2)}, u32[]{:S(2)}) %collective-permute-start) | collective-permute-done | bytes 51232 | tf_op jit(solution)/shard_map/ppermute | solution.py:18
  83.8 0.4 scatter-add.14
  84.2 0.1 collective-permute-done.1
  84.4 0.6 scatter-add.15
  85.0 3.6 %collective-permute-start.2 = (f32[64,128]{1,0:T(8,128)S(1)}, f32[64,128]{1,0:T(8,128)S(1)}, u32[]{:S(2)}, u32[]{:S(2)}) collective-permute-start(f32[64,128]{1,0:T(8,128)S(1)} %get-tuple-element.135), channel_id=1, source_target_pairs={{16,0},{32,16},{48,32},{64,48},{80,64},{96,80},{112,96},{17,1},{33... | collective-permute-start | bytes 98312 | tf_op jit(solution)/shard_map/ppermute | solution.py:18
  88.7 0.6 compare_reduce_fusion.1
  89.3 0.0 all-to-all-done.1.kept
  89.3 4.9 %place_weights.1 = f32[64,512]{1,0:T(8,128)} custom-call(s32[128]{0:T(128)} %copy-done.6, bf16[128,16,512]{2,1,0:T(8,128)(2,1)} %all-to-all-done.1.kept), custom_call_target="tpu_custom_call" | custom-call | flops 1048576 | bytes 2097152 | tf_op jit(solution)/shard_map/place_weights/pallas_call | solution.py:149
  94.2 0.1 slice.447
  94.3 3.1 %collective-permute-start.3 = (f32[64,128]{1,0:T(8,128)S(1)}, f32[64,128]{1,0:T(8,128)S(1)}, u32[]{:S(2)}, u32[]{:S(2)}) collective-permute-start(f32[64,128]{1,0:T(8,128)S(1)} %get-tuple-element.134), channel_id=1, source_target_pairs={{0,16},{16,32},{32,48},{48,64},{64,80},{80,96},{96,112},{1,17},{17... | collective-permute-start | bytes 98312 | tf_op jit(solution)/shard_map/ppermute | solution.py:18
  97.5 0.0 collective-permute-done.2
  97.5 0.5 scatter-add.16
  98.0 0.5 collective-permute-done.3
  98.5 0.7 add_select_fusion
  99.2 0.4 scatter-add.19
  99.6 0.0 copy-start.3
  99.6 0.6 copy-done.3
  (47 shorter events, 0.2 us)
Async XLA Ops:
  0.6 24.8 %copy-start = (f32[64,20]{0,1:T(8,128)S(1)}, f32[64,20]{0,1:T(8,128)}, u32[]{:S(2)}) copy-start(f32[64,20]{0,1:T(8,128)} %param.23) | copy-start | bytes 15364
  9.4 10.9 %copy-start.5 = (s32[8192,1]{0,1:T(1,128)S(1)}, s32[8192,1]{0,1:T(1,128)}, u32[]{:S(2)}) copy-start(s32[8192,1]{0,1:T(1,128)} %param.19) | copy-start | bytes 98308
  9.4 11.0 %copy-start.1 = (f32[20,41]{1,0:T(8,128)S(1)}, f32[20,41]{1,0:T(8,128)}, u32[]{:S(2)}) copy-start(f32[20,41]{1,0:T(8,128)} %param.25) | copy-start | bytes 9844
  9.4 14.0 %copy-start.2 = (f32[20,41]{1,0:T(8,128)S(1)}, f32[20,41]{1,0:T(8,128)}, u32[]{:S(2)}) copy-start(f32[20,41]{1,0:T(8,128)} %param.24) | copy-start | bytes 9844
  9.4 15.8 %copy-start.4 = (s32[8192]{0:T(1024)S(1)}, s32[8192]{0:T(1024)}, u32[]{:S(2)}) copy-start(s32[8192]{0:T(1024)} %param.20) | copy-start | bytes 98308
  9.4 16.1 %copy-start.29 = (s32[128]{0:T(128)S(1)}, s32[128]{0:T(128)}, u32[]{:S(2)}) copy-start(s32[128]{0:T(128)} %param.22) | copy-start | bytes 1540
  9.4 39.5 %all-to-all-start = ((bf16[128,16,512]{2,1,0:T(8,128)(2,1)}), bf16[128,16,512]{2,1,0:T(8,128)(2,1)S(1)}, u32[]{:S(2)}, u32[]{:S(2)}) async-start(bf16[128,16,512]{2,1,0:T(8,128)(2,1)} %pack.2), calls=%async_computation | async-start | bytes 4194304 | tf_op jit(solution)/shard_map/all_to_all | solution.py:191
  25.4 6.3 %copy-start.6 = (s32[128]{0:T(128)}, s32[128]{0:T(128)S(1)}, u32[]{:S(2)}) copy-start(s32[128]{0:T(128)S(1)} %select_reduce_fusion.slots) | copy-start | bytes 1540
  31.8 1.8 %copy-start.8 = (bf16[20]{0:T(256)(128)(2,1)S(1)}, bf16[20]{0:T(256)(128)(2,1)}, u32[]{:S(2)}) copy-start(bf16[20]{0:T(256)(128)(2,1)} %get-tuple-element.89) | copy-start | bytes 124
  31.8 1.8 %copy-start.9 = (bf16[20]{0:T(256)(128)(2,1)S(1)}, bf16[20]{0:T(256)(128)(2,1)}, u32[]{:S(2)}) copy-start(bf16[20]{0:T(256)(128)(2,1)} %get-tuple-element.90) | copy-start | bytes 124
  31.8 1.8 %copy-start.10 = (bf16[20]{0:T(256)(128)(2,1)S(1)}, bf16[20]{0:T(256)(128)(2,1)}, u32[]{:S(2)}) copy-start(bf16[20]{0:T(256)(128)(2,1)} %get-tuple-element.50) | copy-start | bytes 124
  31.8 1.8 %copy-start.11 = (bf16[20]{0:T(256)(128)(2,1)S(1)}, bf16[20]{0:T(256)(128)(2,1)}, u32[]{:S(2)}) copy-start(bf16[20]{0:T(256)(128)(2,1)} %get-tuple-element.51) | copy-start | bytes 124
  31.8 1.8 %copy-start.12 = (bf16[20]{0:T(256)(128)(2,1)S(1)}, bf16[20]{0:T(256)(128)(2,1)}, u32[]{:S(2)}) copy-start(bf16[20]{0:T(256)(128)(2,1)} %get-tuple-element.52) | copy-start | bytes 124
  31.8 1.8 %copy-start.13 = (bf16[20]{0:T(256)(128)(2,1)S(1)}, bf16[20]{0:T(256)(128)(2,1)}, u32[]{:S(2)}) copy-start(bf16[20]{0:T(256)(128)(2,1)} %get-tuple-element.53) | copy-start | bytes 124
  31.8 1.8 %copy-start.14 = (bf16[20]{0:T(256)(128)(2,1)S(1)}, bf16[20]{0:T(256)(128)(2,1)}, u32[]{:S(2)}) copy-start(bf16[20]{0:T(256)(128)(2,1)} %get-tuple-element.54) | copy-start | bytes 124
  31.8 1.8 %copy-start.15 = (bf16[20]{0:T(256)(128)(2,1)S(1)}, bf16[20]{0:T(256)(128)(2,1)}, u32[]{:S(2)}) copy-start(bf16[20]{0:T(256)(128)(2,1)} %get-tuple-element.55) | copy-start | bytes 124
  31.8 1.8 %copy-start.16 = (bf16[20]{0:T(256)(128)(2,1)S(1)}, bf16[20]{0:T(256)(128)(2,1)}, u32[]{:S(2)}) copy-start(bf16[20]{0:T(256)(128)(2,1)} %get-tuple-element.56) | copy-start | bytes 124
  31.8 1.8 %copy-start.17 = (bf16[20]{0:T(256)(128)(2,1)S(1)}, bf16[20]{0:T(256)(128)(2,1)}, u32[]{:S(2)}) copy-start(bf16[20]{0:T(256)(128)(2,1)} %get-tuple-element.57) | copy-start | bytes 124
  31.8 1.8 %copy-start.18 = (bf16[20]{0:T(256)(128)(2,1)S(1)}, bf16[20]{0:T(256)(128)(2,1)}, u32[]{:S(2)}) copy-start(bf16[20]{0:T(256)(128)(2,1)} %get-tuple-element.58) | copy-start | bytes 124
  31.8 1.8 %copy-start.19 = (bf16[20]{0:T(256)(128)(2,1)S(1)}, bf16[20]{0:T(256)(128)(2,1)}, u32[]{:S(2)}) copy-start(bf16[20]{0:T(256)(128)(2,1)} %get-tuple-element.59) | copy-start | bytes 124
  31.9 1.8 %copy-start.20 = (bf16[20]{0:T(256)(128)(2,1)S(1)}, bf16[20]{0:T(256)(128)(2,1)}, u32[]{:S(2)}) copy-start(bf16[20]{0:T(256)(128)(2,1)} %get-tuple-element.60) | copy-start | bytes 124
  31.9 1.8 %copy-start.21 = (bf16[20]{0:T(256)(128)(2,1)S(1)}, bf16[20]{0:T(256)(128)(2,1)}, u32[]{:S(2)}) copy-start(bf16[20]{0:T(256)(128)(2,1)} %get-tuple-element.61) | copy-start | bytes 124
  31.9 1.8 %copy-start.22 = (bf16[20]{0:T(256)(128)(2,1)S(1)}, bf16[20]{0:T(256)(128)(2,1)}, u32[]{:S(2)}) copy-start(bf16[20]{0:T(256)(128)(2,1)} %get-tuple-element.62) | copy-start | bytes 124
  31.9 1.8 %copy-start.23 = (bf16[20]{0:T(256)(128)(2,1)S(1)}, bf16[20]{0:T(256)(128)(2,1)}, u32[]{:S(2)}) copy-start(bf16[20]{0:T(256)(128)(2,1)} %get-tuple-element.63) | copy-start | bytes 124
  31.9 1.8 %copy-start.24 = (bf16[20]{0:T(256)(128)(2,1)S(1)}, bf16[20]{0:T(256)(128)(2,1)}, u32[]{:S(2)}) copy-start(bf16[20]{0:T(256)(128)(2,1)} %get-tuple-element.64) | copy-start | bytes 124
  31.9 1.8 %copy-start.25 = (bf16[20]{0:T(256)(128)(2,1)S(1)}, bf16[20]{0:T(256)(128)(2,1)}, u32[]{:S(2)}) copy-start(bf16[20]{0:T(256)(128)(2,1)} %get-tuple-element.65) | copy-start | bytes 124
  31.9 1.8 %copy-start.26 = (bf16[20]{0:T(256)(128)(2,1)S(1)}, bf16[20]{0:T(256)(128)(2,1)}, u32[]{:S(2)}) copy-start(bf16[20]{0:T(256)(128)(2,1)} %get-tuple-element.66) | copy-start | bytes 124
  31.9 1.8 %copy-start.27 = (bf16[20]{0:T(256)(128)(2,1)S(1)}, bf16[20]{0:T(256)(128)(2,1)}, u32[]{:S(2)}) copy-start(bf16[20]{0:T(256)(128)(2,1)} %get-tuple-element.67) | copy-start | bytes 124
  31.9 1.8 %copy-start.28 = (bf16[20]{0:T(256)(128)(2,1)S(1)}, bf16[20]{0:T(256)(128)(2,1)}, u32[]{:S(2)}) copy-start(bf16[20]{0:T(256)(128)(2,1)} %get-tuple-element.68) | copy-start | bytes 124
  47.5 11.5 %copy-start.7 = (bf16[20]{0:T(256)(128)(2,1)S(1)}, bf16[20]{0:T(256)(128)(2,1)}, u32[]{:S(2)}) copy-start(bf16[20]{0:T(256)(128)(2,1)} %get-tuple-element.100) | copy-start | bytes 124
  48.9 40.4 %all-to-all-start.1 = ((bf16[128,16,512]{2,1,0:T(8,128)(2,1)}), bf16[128,16,512]{2,1,0:T(8,128)(2,1)}, u32[]{:S(2)}, u32[]{:S(2)}) async-start(bf16[128,16,512]{2,1,0:T(8,128)(2,1)} %pack.3), calls=%async_computation.1 | async-start | bytes 4194304 | tf_op jit(solution)/shard_map/all_to_all | solution.py:194
  70.6 13.2 %collective-permute-start = (f32[20,640]{1,0:T(8,128)S(1)}, f32[20,640]{1,0:T(8,128)S(1)}, u32[]{:S(2)}, u32[]{:S(2)}) collective-permute-start(f32[20,640]{1,0:T(8,128)S(1)} %get-tuple-element.133), channel_id=1, source_target_pairs={{1,0},{2,1},{3,2},{4,3},{5,4},{6,5},{7,6},{8,7},{9,8},{10,9},{11,1... | collective-permute-start | bytes 153608 | tf_op jit(solution)/shard_map/ppermute | solution.py:18
  75.6 8.7 %collective-permute-start.1 = (f32[20,640]{1,0:T(8,128)S(1)}, f32[20,640]{1,0:T(8,128)S(1)}, u32[]{:S(2)}, u32[]{:S(2)}) collective-permute-start(f32[20,640]{1,0:T(8,128)S(1)} %get-tuple-element.132), channel_id=1, source_target_pairs={{0,1},{1,2},{2,3},{3,4},{4,5},{5,6},{6,7},{7,8},{8,9},{9,10},{10,1... | collective-permute-start | bytes 153608 | tf_op jit(solution)/shard_map/ppermute | solution.py:18
  85.0 12.4 %collective-permute-start.2 = (f32[64,128]{1,0:T(8,128)S(1)}, f32[64,128]{1,0:T(8,128)S(1)}, u32[]{:S(2)}, u32[]{:S(2)}) collective-permute-start(f32[64,128]{1,0:T(8,128)S(1)} %get-tuple-element.135), channel_id=1, source_target_pairs={{16,0},{32,16},{48,32},{64,48},{80,64},{96,80},{112,96},{17,1},{33... | collective-permute-start | bytes 98312 | tf_op jit(solution)/shard_map/ppermute | solution.py:18
  94.3 4.1 %collective-permute-start.3 = (f32[64,128]{1,0:T(8,128)S(1)}, f32[64,128]{1,0:T(8,128)S(1)}, u32[]{:S(2)}, u32[]{:S(2)}) collective-permute-start(f32[64,128]{1,0:T(8,128)S(1)} %get-tuple-element.134), channel_id=1, source_target_pairs={{0,16},{16,32},{32,48},{48,64},{64,80},{80,96},{96,112},{1,17},{17... | collective-permute-start | bytes 98312 | tf_op jit(solution)/shard_map/ppermute | solution.py:18
  99.6 0.7 copy-start.3

commit v2 on v1

v2 whole, which is shorter than its diff:
```python
import functools

import jax
import jax.numpy as jnp
from jax import lax
from jax.experimental import pallas as pl
from jax.experimental.pallas import tpu as pltpu
from jax.sharding import PartitionSpec as P

RS = 4
LANES = 128
BOTH = ("skyx", "skyy")


def from_behind(value, axis, steps):
    count = lax.axis_size(axis)
    initial, last = (max(0, -steps), min(count, count - steps))
    return lax.ppermute(value, axis, [(source, source + steps) for source in range(initial, last)])


def pack_kernel(planes, me, patch_of, valid, *refs):
    sources, refs = refs[:planes], refs[planes:]
    out, *rooms, packed, targets, usable, arrived, noted, sent = refs
    blocks = rooms[0].shape[0]
    chunks = arrived.shape[1]
    group = blocks // chunks

    def fetch(index, chunk):
        at = pl.ds(chunk * group, group)
        return pltpu.make_async_copy(sources[index].at[at], rooms[index].at[at], arrived.at[index, chunk])

    notes = [pltpu.make_async_copy(patch_of, targets, noted.at[0]), pltpu.make_async_copy(valid, usable, noted.at[1])]
    for note in notes:
        note.start()
    for chunk in range(chunks):
        for index in range(planes):
            fetch(index, chunk).start()
    packed[...] = jnp.zeros_like(packed)
    for note in notes:
        note.wait()
    first = me[0] * blocks
    for chunk in range(chunks):
        for index in range(planes):
            fetch(index, chunk).wait()
        for block in range(chunk * group, chunk * group + group):
            value = rooms[0][block]
            for room in rooms[1:]:
                value = value * room[block]
            place = targets[first + block]
            packed[place] = jnp.where(usable[first + block] != 0, value, jnp.zeros_like(value))
    pieces = sent.shape[0]
    share = packed.shape[0] // pieces
    copies = []
    for piece in range(pieces):
        at = pl.ds(piece * share, share)
        copies.append(pltpu.make_async_copy(packed.at[at], out.at[at], sent.at[piece]))
        copies[-1].start()
    for copy in copies:
        copy.wait()


def pack(devices, me, patch_of, valid, *planes):
    blocks, rows, width = planes[0].shape
    chunks, pieces = 4, 8
    return pl.pallas_call(
        functools.partial(pack_kernel, len(planes)),
        out_shape=jax.ShapeDtypeStruct((devices, rows, width), jnp.bfloat16),
        in_specs=[pl.BlockSpec(memory_space=pltpu.SMEM)] + [pl.BlockSpec(memory_space=pl.ANY)] * (2 + len(planes)),
        out_specs=pl.BlockSpec(memory_space=pl.ANY),
        scratch_shapes=[pltpu.VMEM((blocks, rows, width), jnp.bfloat16) for _ in planes]
        + [
            pltpu.VMEM((devices, rows, width), jnp.bfloat16),
            pltpu.SMEM(patch_of.shape, jnp.int32),
            pltpu.SMEM(valid.shape, jnp.int32),
            pltpu.SemaphoreType.DMA((len(planes), chunks)),
            pltpu.SemaphoreType.DMA((2,)),
            pltpu.SemaphoreType.DMA((pieces,)),
        ],
        cost_estimate=pl.CostEstimate(
            flops=devices * rows * width,
            bytes_accessed=2 * (len(planes) * blocks + devices) * rows * width,
            transcendentals=0,
        ),
        name="pack",
    )(me, patch_of, valid, *planes)


def table_kernel(across_taps, down_taps, row_at, across, down):
    count, ext, places = down.shape
    lane = lax.broadcasted_iota(jnp.int32, (LANES, LANES), 1)
    line = lax.broadcasted_iota(jnp.int32, (LANES, LANES), 0)
    order = (lax.broadcasted_iota(jnp.int32, (LANES, places), 0) == row_at[...]).astype(jnp.bfloat16)
    for c in range(count):
        turned = jnp.broadcast_to(across_taps[c : c + 1, :], (LANES, LANES))
        turned = pltpu.roll(turned, 0, 1, stride=1, stride_axis=0)
        across[c, LANES:, :] = jnp.where(lane >= line, turned, 0.0).astype(jnp.bfloat16)
        across[c, :LANES, :] = jnp.where(lane < line, turned, 0.0).astype(jnp.bfloat16)
        turned = jnp.broadcast_to(down_taps[c : c + 1, :], (LANES, LANES))
        turned = pltpu.roll(turned, 0, 1, stride=1, stride_axis=0)[:ext].astype(jnp.bfloat16)
        down[c] = jnp.dot(turned, order, preferred_element_type=jnp.float32).astype(jnp.bfloat16)


def band_tables(basis_across, basis_down, row_at, ext):
    channels, taps = basis_across.shape
    places = row_at.shape[1]
    across_taps = jnp.pad(basis_across, ((0, 0), (0, LANES - taps)))
    down_taps = jnp.concatenate(
        [basis_down[:, :1], jnp.zeros((channels, LANES - taps), jnp.float32), basis_down[:, :0:-1]], axis=1
    )
    return pl.pallas_call(
        table_kernel,
        out_shape=(
            jax.ShapeDtypeStruct((channels, 2 * LANES, LANES), jnp.bfloat16),
            jax.ShapeDtypeStruct((channels, ext, places), jnp.bfloat16),
        ),
        in_specs=[pl.BlockSpec(memory_space=pltpu.VMEM)] * 3,
        out_specs=(pl.BlockSpec(memory_space=pltpu.VMEM),) * 2,
        compiler_params=pltpu.CompilerParams(vmem_limit_bytes=8 << 20),
        name="band_tables",
    )(across_taps, down_taps, row_at)


def coadd_kernel(margin, flux, choose, down, across, inner, top, bottom, wide, channels, mixed):
    sources, rows, width = flux.shape
    count, ext, _ = down.shape
    pieces = width // LANES
    tiles = pieces + 1
    edge = top.shape[0]
    tall = inner.shape[0]
    for piece in range(pieces):
        lanes = pl.ds(piece * LANES, LANES)
        wide[piece] = flux[:, :, lanes].reshape(sources * rows, LANES).astype(jnp.float32)
    table = choose[...]
    for pair in range(rows // 2):
        halves = []
        for half in range(2):
            at = pl.ds(2 * pair + half, sources, stride=rows)
            row = [wide[piece, at, :].astype(jnp.bfloat16) for piece in range(pieces)]
            halves.append(jnp.concatenate(row, axis=1))
        summed = jnp.dot(table, jnp.concatenate(halves, axis=0), preferred_element_type=jnp.float32)
        channels[:, pair * 8 : pair * 8 + 8, :] = summed.reshape(count, 8, width)
    zeros = jnp.zeros((ext, LANES), jnp.bfloat16)
    for c in range(count):
        mixed[c, :, :LANES] = zeros
        mixed[c, :, LANES + width :] = zeros
        mixed[c, :, LANES : LANES + width] = jnp.dot(
            down[c], channels[c].astype(jnp.bfloat16), preferred_element_type=jnp.float32
        ).astype(jnp.bfloat16)
    total = jnp.zeros((tiles * ext, LANES), jnp.float32)
    for c in range(count):
        windows = jnp.concatenate([mixed[c, :, LANES * t : LANES * t + 2 * LANES] for t in range(tiles)], axis=0)
        total = total + jnp.dot(windows, across[c], preferred_element_type=jnp.float32)
    whole = jnp.concatenate([total[t * ext : (t + 1) * ext] for t in range(tiles)], axis=1)
    whole = pltpu.roll(whole, tiles * LANES - margin, 1)
    top[...] = whole[:edge]
    inner[...] = whole[edge : edge + tall]
    bottom[...] = whole[edge + tall :]


def convolve_sum(margin, flux, choose, down, across):
    sources, rows, width = flux.shape
    count, ext, _ = down.shape
    tiles = width // LANES + 1
    tall = RS * rows
    edge = (ext - tall) // 2
    sizes = [(tall, tiles * LANES), (edge, tiles * LANES), (edge, tiles * LANES)]
    return pl.pallas_call(
        functools.partial(coadd_kernel, margin),
        out_shape=tuple(jax.ShapeDtypeStruct(size, jnp.float32) for size in sizes),
        in_specs=[pl.BlockSpec(memory_space=pltpu.VMEM)] * 4,
        out_specs=(pl.BlockSpec(memory_space=pltpu.VMEM),) * len(sizes),
        scratch_shapes=[
            pltpu.VMEM((width // LANES, sources * rows, LANES), jnp.float32),
            pltpu.VMEM((count, RS * rows, width), jnp.float32),
            pltpu.VMEM((count, ext, (tiles + 1) * LANES), jnp.bfloat16),
        ],
        compiler_params=pltpu.CompilerParams(vmem_limit_bytes=20 << 20),
        cost_estimate=pl.CostEstimate(
            flops=2 * count * ext * tiles * LANES * 2 * LANES,
            bytes_accessed=2 * sources * rows * width + 4 * ext * tiles * LANES,
            transcendentals=0,
        ),
        name="convolve_sum",
    )(flux, choose, down, across)


def weight_kernel(row_in_patch, kept, out):
    sources, rows, width = kept.shape
    line = lax.broadcasted_iota(jnp.int32, (out.shape[0], sources * rows), 0)
    chosen = (line == row_in_patch[...]).astype(jnp.bfloat16)
    out[...] = jnp.dot(chosen, kept[...].reshape(sources * rows, width), preferred_element_type=jnp.float32)


def place_weights(row_in_patch, kept):
    sources, rows, width = kept.shape
    return pl.pallas_call(
        weight_kernel,
        out_shape=jax.ShapeDtypeStruct((RS * rows, width), jnp.float32),
        in_specs=[pl.BlockSpec(memory_space=pltpu.VMEM)] * 2,
        out_specs=pl.BlockSpec(memory_space=pltpu.VMEM),
        compiler_params=pltpu.CompilerParams(vmem_limit_bytes=8 << 20),
        cost_estimate=pl.CostEstimate(
            flops=2 * RS * rows * sources * rows * width,
            bytes_accessed=2 * sources * rows * width,
            transcendentals=0,
        ),
        name="place_weights",
    )(row_in_patch, kept)


def side_kernel(side, top, bottom, out):
    tall, _ = side.shape
    edge = top.shape[0]
    out[:edge, :] = side[:edge, :] + top[...]
    out[edge : tall - edge, :] = side[edge : tall - edge, :]
    out[tall - edge :, :] = side[tall - edge :, :] + bottom[...]


def add_beside(inner, top, bottom):
    tall, wide = inner.shape
    edge = top.shape[0]
    last = wide // LANES - 1
    return pl.pallas_call(
        side_kernel,
        out_shape=jax.ShapeDtypeStruct((tall, LANES), jnp.float32),
        grid=(1,),
        in_specs=[pl.BlockSpec((size, LANES), lambda step: (0, last)) for size in (tall, edge, edge)],
        out_specs=pl.BlockSpec((tall, LANES), lambda step: (0, 0)),
        compiler_params=pltpu.CompilerParams(vmem_limit_bytes=4 << 20),
        name="add_beside",
    )(inner, top, bottom)


def finish_kernel(margin, inner, top, bottom, left, right, out):
    tall, width = out.shape
    edge = top.shape[0]
    lane = lax.broadcasted_iota(jnp.int32, (1, LANES), 1)
    out[:edge, :] = inner[:edge, :width] + top[:, :width]
    out[edge : tall - edge, :] = inner[edge : tall - edge, :width]
    out[tall - edge :, :] = inner[tall - edge :, :width] + bottom[:, :width]
    out[:, :LANES] += jnp.where(lane < margin, left[...], 0.0)
    out[:, width - LANES :] += jnp.where(lane >= LANES - margin, right[...], 0.0)


def finish(margin, inner, top, bottom, left, right):
    tall, wide = inner.shape
    return pl.pallas_call(
        functools.partial(finish_kernel, margin),
        out_shape=jax.ShapeDtypeStruct((tall, wide - LANES), jnp.float32),
        in_specs=[pl.BlockSpec(memory_space=pltpu.VMEM)] * 5,
        out_specs=pl.BlockSpec(memory_space=pltpu.VMEM),
        compiler_params=pltpu.CompilerParams(vmem_limit_bytes=4 << 20),
        name="finish",
    )(inner, top, bottom, left, right)


def body(
    image, inverse_var, patch_of, row_of, valid, coef_index, coef_table, basis_across, basis_down
):
    devices = lax.axis_size("skyx") * lax.axis_size("skyy")
    block_count, row_count, block_width = image.shape
    channels = basis_across.shape[0]
    margin = (basis_across.shape[1] - 1) // 2
    patch_rows = RS * row_count
    columns, lines = lax.axis_size("skyx"), lax.axis_size("skyy")
    my_column, my_line = lax.axis_index("skyx"), lax.axis_index("skyy")
    my_patch = my_column * lines + my_line
    patches = patch_of[:, 0]
    me = my_patch.astype(jnp.int32).reshape(1)

    weighted = pack(devices, me, patches, valid, inverse_var, image)
    weighted_in = lax.all_to_all(weighted, BOTH, split_axis=0, concat_axis=0, tiled=True)
    kept = pack(devices, me, patches, valid, inverse_var)

    choose = (
        coef_index[:, None] == jnp.arange(coef_table.shape[0], dtype=jnp.int32)[None, :]
    ).astype(jnp.float32)
    coeffs = jnp.dot(choose, coef_table, precision=lax.Precision.HIGHEST)
    target_grid = patches.reshape(devices, block_count)
    slot_grid = row_of.reshape(devices, block_count)
    hits = target_grid == my_patch
    slot = jnp.max(jnp.where(hits, slot_grid, -1), axis=1)
    in_slot = slot[None, :] == jnp.arange(RS, dtype=jnp.int32)[:, None]
    one = jnp.where(in_slot[None], coeffs.T[:, None, :], 0.0)
    none = jnp.zeros_like(one)
    table = jnp.concatenate(
        [jnp.concatenate([one, none], axis=2), jnp.concatenate([none, one], axis=2)], axis=1
    ).reshape(channels * 2 * RS, 2 * devices).astype(jnp.bfloat16)
    places = jnp.arange(patch_rows, dtype=jnp.int32)
    edge = (margin + 7) // 8 * 8
    row_at = (places % RS) * row_count + places // RS + edge - margin
    across, down = band_tables(basis_across, basis_down, row_at[None, :], patch_rows + 2 * edge)
    received_rows = jnp.arange(row_count, dtype=jnp.int32)[None, :]
    row_in_patch = jnp.where(slot[:, None] >= 0, slot[:, None] * row_count + received_rows, -1)
    row_in_patch = row_in_patch.reshape(1, devices * row_count)
    kept, table, down, across, row_in_patch = lax.optimization_barrier((kept, table, down, across, row_in_patch))
    kept_in = lax.all_to_all(kept, BOTH, split_axis=0, concat_axis=0, tiled=True)
    inner, top, bottom = convolve_sum(margin, weighted_in, table, down, across)
    top, bottom = from_behind(bottom, "skyy", 1), from_behind(top, "skyy", -1)
    side = add_beside(inner, top, bottom)
    left, right = from_behind(side, "skyx", 1), from_behind(side, "skyx", -1)
    weight_sum = place_weights(row_in_patch, kept_in)
    coadd = finish(margin, inner, top, bottom, left, right)
    return (coadd, weight_sum)


def solution(mesh):
    placed = (P(BOTH, None, None), P(BOTH, None, None), P(), P(), P(), P(), P(), P(), P())
    return jax.shard_map(
        body,
        mesh=mesh,
        in_specs=placed,
        out_specs=(P("skyy", "skyx"), P("skyy", "skyx")),
        check_vma=False,
    )
```

time: 101 us -> 88.8 us (0.88)
  waiting for transfers between devices: 8.35 us -> 35.9 us
  other arithmetic: 25 us -> 0.49 us
  local copies, waits for them, and re-layouts: 10.1 us -> 3.06 us
  Pallas kernels: 22 us -> 15.8 us
  starting transfers between devices: 33.3 us -> 31.8 us
    all_to_all x2, waiting for transfers between devices: 1.44 us -> 22.5 us  [the longest x1 22.5 us: body(): lax.all_to_all(weighted, BOTH, split_axis=0, concat_axis=0, tiled=True)]
    convert_element_type x2 -> x0, other arithmetic: 20.6 us -> none  [spread(): return picked.astype(jnp.bfloat16)]
    ppermute x4, waiting for transfers between devices: 6.91 us -> 13.4 us  [from_behind(): lax.ppermute(value, axis, [(source, source + steps) for source in range(i...]
    slice x10 -> x1, local copies, waits for them, and re-layouts: 4.81 us -> 0.07 us  [band_tables(): basis_down[:, :0:-1]]
    pallas_call x3 -> x6, Pallas kernels: 17 us -> 13.1 us  [the longest x2 7 us: pack(): pl.pallas_call(functools.partial(pack_kernel, len(planes)), out_shape=jax...]
    dynamic_slice x2 -> x0, local copies, waits for them, and re-layouts: 2.51 us -> none  [the longest x1 1.27 us: body(): my_valid = lax.dynamic_slice_in_dim(valid, first_row, block_count)]
    pallas_call x1, Pallas kernels: 4.93 us -> 2.72 us  [place_weights(): pl.pallas_call(weight_kernel, out_shape=jax.ShapeDtypeStruct((RS * rows,...]
    eq x2 -> x0, other arithmetic: 2.19 us -> none  [spread(): picked = jnp.where(offset[None] == tap, taps[:, tap].reshape(shape), picked)]
  transfers between devices with their start and end apart: 6 -> 6, of which waited for: 4 -> 2; matrix products, arithmetic and copies ran while one was open for 31% -> 1% of each run, Pallas kernels for 16% -> 13%
where the time goes in v2:
time: 88.8 us; the launch traced here: 88.2 us
  waiting for transfers between devices  35.9 us (40%)
  starting transfers between devices  31.8 us (36%)
  Pallas kernels  15.8 us (18%)
  local copies, waits for them, and re-layouts  3.06 us (3%)
  between operations  0.93 us (1%)
    all_to_all x1, waiting for transfers between devices, body(): lax.all_to_all(weighted, BOTH, split_axis=0, concat_axis=0, tiled=True)  22.5 us
    ppermute x4, starting transfers between devices, from_behind(): lax.ppermute(value, axis, [(source, source + steps) for source in range(i...  14.3 us
    ppermute x4, waiting for transfers between devices, from_behind(): lax.ppermute(value, axis, [(source, source + steps) for source in range(i...  13.4 us
    all_to_all x1, starting transfers between devices, body(): lax.all_to_all(weighted, BOTH, split_axis=0, concat_axis=0, tiled=True)  10.8 us
    pallas_call x2, Pallas kernels, pack(): pl.pallas_call(functools.partial(pack_kernel, len(planes)), out_shape=jax...  7 us
    all_to_all x1, starting transfers between devices, body(): lax.all_to_all(kept, BOTH, split_axis=0, concat_axis=0, tiled=True)  6.61 us
    pallas_call x1, Pallas kernels, convolve_sum(): pl.pallas_call(functools.partial(coadd_kernel, margin), out_shape=tuple((...  4.91 us
    pallas_call x1, Pallas kernels, place_weights(): pl.pallas_call(weight_kernel, out_shape=jax.ShapeDtypeStruct((RS * rows,...  2.72 us
  transfers between devices with their start and end apart: 6, of which 2 were waited for; matrix products, arithmetic and copies ran while one was open for 1% of the time, Pallas kernels for 13%

profile of v2, /device:TPU:3, one launch (start us, length us, event | category | flops | bytes accessed | tf_op | source)
XLA Modules:
  0.0 88.2 jit_solution(12665105713163275508)
XLA Ops:
  0.6 0.0 copy-start
  0.7 3.5 %pack.2 = bf16[128,16,512]{2,1,0:T(8,128)(2,1)} custom-call(s32[1]{0:T(128)} %bitcast.me, s32[8192]{0:T(1024)} %bitcast.8, s32[8192]{0:T(1024)} %valid.3, bf16[64,16,512]{2,1,0:T(8,128)(2,1)} %refs_0_.3, bf16[64,16,512]{2,1,0:T(8,128)(2,1)} %refs_1_.1), custom_call_target="tpu_custom_call" | custom-call | flops 1048576 | bytes 4194304 | tf_op jit(solution)/shard_map/pack/pallas_call | solution.py:65
  4.2 0.0 copy-start.5
  4.2 0.0 copy-start.6
  4.2 0.0 copy-start.7
  4.2 0.0 copy-start.8
  4.2 10.8 %all-to-all-start = ((bf16[128,16,512]{2,1,0:T(8,128)(2,1)}), bf16[128,16,512]{2,1,0:T(8,128)(2,1)S(1)}, u32[]{:S(2)}, u32[]{:S(2)}) async-start(bf16[128,16,512]{2,1,0:T(8,128)(2,1)} %pack.2), calls=%async_computation | async-start | bytes 4194304 | tf_op jit(solution)/shard_map/all_to_all | solution.py:272
  15.1 0.0 copy-done.5
  15.1 0.0 copy-start.9
  15.1 0.1 compare_reduce_fusion
  15.2 0.1 eq.43
  15.3 0.0 copy-done.6
  15.3 0.1 slice.7
  15.4 0.1 rev.3
  15.5 0.0 copy-done.7
  15.5 0.1 reshape.141
  15.5 0.1 select_reduce_fusion
  15.7 0.1 add_select_fusion
  15.8 0.1 select_n.53.row_in_patch
  15.9 0.0 copy-done.8
  15.9 0.1 pad.10.clone
  16.0 0.1 pad_maximum_fusion.down_taps
  16.1 0.5 band_tables.1
  16.6 0.0 copy-start.3
  16.6 0.8 copy-done.3
  17.4 3.5 %pack.3 = bf16[128,16,512]{2,1,0:T(8,128)(2,1)} custom-call(s32[1]{0:T(128)} %bitcast.me, s32[8192]{0:T(1024)} %bitcast.9, s32[8192]{0:T(1024)} %valid.3, bf16[64,16,512]{2,1,0:T(8,128)(2,1)} %refs_0_.3), custom_call_target="tpu_custom_call" | custom-call | flops 1048576 | bytes 3145728 | tf_op jit(solution)/shard_map/pack/pallas_call | solution.py:65
  20.9 0.0 copy-done
  20.9 0.0 copy-done.9
  20.9 0.2 convolution_bitcast_fusion
  21.3 22.5 %all-to-all-done.flux = bf16[128,16,512]{2,1,0:T(8,128)(2,1)S(1)} async-done(((bf16[128,16,512]{2,1,0:T(8,128)(2,1)}), bf16[128,16,512]{2,1,0:T(8,128)(2,1)S(1)}, u32[]{:S(2)}, u32[]{:S(2)}) %all-to-all-start) | async-done | bytes 2097184 | tf_op jit(solution)/shard_map/all_to_all | solution.py:272
  43.8 6.6 %all-to-all-start.1 = ((bf16[128,16,512]{2,1,0:T(8,128)(2,1)}), bf16[128,16,512]{2,1,0:T(8,128)(2,1)}, u32[]{:S(2)}, u32[]{:S(2)}) async-start(bf16[128,16,512]{2,1,0:T(8,128)(2,1)} %pack.3), calls=%async_computation.1 | async-start | bytes 4194304 | tf_op jit(solution)/shard_map/all_to_all | solution.py:297
  50.4 0.0 copy-start.4
  50.4 1.1 %copy-done.4 = bf16[20,112,64]{2,1,0:T(8,128)(2,1)S(1)} copy-done((bf16[20,112,64]{2,1,0:T(8,128)(2,1)S(1)}, bf16[20,112,64]{2,1,0:T(8,128)(2,1)}, u32[]{:S(2)}) %copy-start.4) | copy-done | bytes 286744
  51.4 4.9 %convolve_sum.1 = (f32[64,640]{1,0:T(8,128)S(1)}, f32[24,640]{1,0:T(8,128)S(1)}, f32[24,640]{1,0:T(8,128)S(1)}) custom-call(bf16[128,16,512]{2,1,0:T(8,128)(2,1)S(1)} %all-to-all-done.flux, bf16[160,256]{1,0:T(8,128)(2,1)S(1)} %fusion.3.choose, bf16[20,112,64]{2,1,0:T(8,128)(2,1)S(1)} %copy-done.4, bf16[20,256,128]{2,1,0:T(8,128)(2,1)S(1)} %get-tuple-element.16.across), custom_call_target="tpu_custom_call" | custom-call | flops 734003200 | bytes 2383872 | tf_op jit(solution)/shard_map/convolve_sum/pallas_call | solution.py:167
  56.4 3.4 %collective-permute-start = (f32[24,640]{1,0:T(8,128)S(1)}, f32[24,640]{1,0:T(8,128)S(1)}, u32[]{:S(2)}, u32[]{:S(2)}) collective-permute-start(f32[24,640]{1,0:T(8,128)S(1)} %get-tuple-element.18), channel_id=1, source_target_pairs={{0,1},{1,2},{2,3},{3,4},{4,5},{5,6},{6,7},{7,8},{8,9},{9,10},{10,1... | collective-permute-start | bytes 184328 | tf_op jit(solution)/shard_map/ppermute | solution.py:18
  59.7 4.0 %collective-permute-start.1 = (f32[24,640]{1,0:T(8,128)S(1)}, f32[24,640]{1,0:T(8,128)S(1)}, u32[]{:S(2)}, u32[]{:S(2)}) collective-permute-start(f32[24,640]{1,0:T(8,128)S(1)} %get-tuple-element.19), channel_id=1, source_target_pairs={{1,0},{2,1},{3,2},{4,3},{5,4},{6,5},{7,6},{8,7},{9,8},{10,9},{11,1... | collective-permute-start | bytes 184328 | tf_op jit(solution)/shard_map/ppermute | solution.py:18
  63.8 13.4 %collective-permute-done.top = f32[24,640]{1,0:T(8,128)S(1)} collective-permute-done((f32[24,640]{1,0:T(8,128)S(1)}, f32[24,640]{1,0:T(8,128)S(1)}, u32[]{:S(2)}, u32[]{:S(2)}) %collective-permute-start) | collective-permute-done | bytes 61472 | tf_op jit(solution)/shard_map/ppermute | solution.py:18
  77.1 0.0 collective-permute-done.1.bottom
  77.1 0.0 copy-start.1
  77.2 0.7 copy-done.1
  77.8 3.6 %collective-permute-start.3 = (f32[64,128]{1,0:T(8,128)S(1)}, f32[64,128]{1,0:T(8,128)S(1)}, u32[]{:S(2)}, u32[]{:S(2)}) collective-permute-start(f32[64,128]{1,0:T(8,128)S(1)} %add_beside.1), channel_id=1, source_target_pairs={{16,0},{32,16},{48,32},{64,48},{80,64},{96,80},{112,96},{17,1},{33... | collective-permute-start | bytes 98312 | tf_op jit(solution)/shard_map/ppermute | solution.py:18
  81.4 0.0 copy-start.2
  81.5 3.3 %collective-permute-start.2 = (f32[64,128]{1,0:T(8,128)S(1)}, f32[64,128]{1,0:T(8,128)S(1)}, u32[]{:S(2)}, u32[]{:S(2)}) collective-permute-start(f32[64,128]{1,0:T(8,128)S(1)} %add_beside.1), channel_id=1, source_target_pairs={{0,16},{16,32},{32,48},{48,64},{64,80},{80,96},{96,112},{1,17},{17... | collective-permute-start | bytes 98312 | tf_op jit(solution)/shard_map/ppermute | solution.py:18
  84.8 0.0 all-to-all-done.1.kept
  84.8 2.7 %place_weights.1 = f32[64,512]{1,0:T(8,128)} custom-call(s32[1,2048]{1,0:T(1,128)S(1)} %select_n.53.row_in_patch, bf16[128,16,512]{2,1,0:T(8,128)(2,1)} %all-to-all-done.1.kept), custom_call_target="tpu_custom_call" | custom-call | flops 134217728 | bytes 2097152 | tf_op jit(solution)/shard_map/place_weights/pallas_call | solution.py:196
  87.5 0.0 collective-permute-done.3.right
  87.5 0.0 collective-permute-done.2.left
  87.5 0.0 copy-done.2
  87.5 0.7 finish.1
  (9 shorter events, 0.1 us)
Async XLA Ops:
  0.6 20.3 %copy-start = (f32[64,20]{0,1:T(8,128)S(1)}, f32[64,20]{0,1:T(8,128)}, u32[]{:S(2)}) copy-start(f32[64,20]{0,1:T(8,128)} %param.15) | copy-start | bytes 15364
  4.2 10.9 %copy-start.5 = (s32[8192,1]{0,1:T(1,128)S(1)}, s32[8192,1]{0,1:T(1,128)}, u32[]{:S(2)}) copy-start(s32[8192,1]{0,1:T(1,128)} %param.11) | copy-start | bytes 98308
  4.2 11.1 %copy-start.6 = (f32[20,41]{1,0:T(8,128)S(1)}, f32[20,41]{1,0:T(8,128)}, u32[]{:S(2)}) copy-start(f32[20,41]{1,0:T(8,128)} %param.17) | copy-start | bytes 9844
  4.2 11.3 %copy-start.7 = (s32[8192]{0:T(1024)S(1)}, s32[8192]{0:T(1024)}, u32[]{:S(2)}) copy-start(s32[8192]{0:T(1024)} %param.12) | copy-start | bytes 98308
  4.2 11.7 %copy-start.8 = (f32[20,41]{1,0:T(8,128)S(1)}, f32[20,41]{1,0:T(8,128)}, u32[]{:S(2)}) copy-start(f32[20,41]{1,0:T(8,128)} %param.16) | copy-start | bytes 9844
  4.2 39.5 %all-to-all-start = ((bf16[128,16,512]{2,1,0:T(8,128)(2,1)}), bf16[128,16,512]{2,1,0:T(8,128)(2,1)S(1)}, u32[]{:S(2)}, u32[]{:S(2)}) async-start(bf16[128,16,512]{2,1,0:T(8,128)(2,1)} %pack.2), calls=%async_computation | async-start | bytes 4194304 | tf_op jit(solution)/shard_map/all_to_all | solution.py:272
  15.1 5.8 %copy-start.9 = (s32[128]{0:T(128)S(1)}, s32[128]{0:T(128)}, u32[]{:S(2)}) copy-start(s32[128]{0:T(128)} %param.14) | copy-start | bytes 1540
  16.6 0.8 copy-start.3
  43.8 41.0 %all-to-all-start.1 = ((bf16[128,16,512]{2,1,0:T(8,128)(2,1)}), bf16[128,16,512]{2,1,0:T(8,128)(2,1)}, u32[]{:S(2)}, u32[]{:S(2)}) async-start(bf16[128,16,512]{2,1,0:T(8,128)(2,1)} %pack.3), calls=%async_computation.1 | async-start | bytes 4194304 | tf_op jit(solution)/shard_map/all_to_all | solution.py:297
  50.4 1.1 %copy-start.4 = (bf16[20,112,64]{2,1,0:T(8,128)(2,1)S(1)}, bf16[20,112,64]{2,1,0:T(8,128)(2,1)}, u32[]{:S(2)}) copy-start(bf16[20,112,64]{2,1,0:T(8,128)(2,1)} %copy-done.3) | copy-start | bytes 860164
  56.4 20.8 %collective-permute-start = (f32[24,640]{1,0:T(8,128)S(1)}, f32[24,640]{1,0:T(8,128)S(1)}, u32[]{:S(2)}, u32[]{:S(2)}) collective-permute-start(f32[24,640]{1,0:T(8,128)S(1)} %get-tuple-element.18), channel_id=1, source_target_pairs={{0,1},{1,2},{2,3},{3,4},{4,5},{5,6},{6,7},{7,8},{8,9},{9,10},{10,1... | collective-permute-start | bytes 184328 | tf_op jit(solution)/shard_map/ppermute | solution.py:18
  59.7 17.4 %collective-permute-start.1 = (f32[24,640]{1,0:T(8,128)S(1)}, f32[24,640]{1,0:T(8,128)S(1)}, u32[]{:S(2)}, u32[]{:S(2)}) collective-permute-start(f32[24,640]{1,0:T(8,128)S(1)} %get-tuple-element.19), channel_id=1, source_target_pairs={{1,0},{2,1},{3,2},{4,3},{5,4},{6,5},{7,6},{8,7},{9,8},{10,9},{11,1... | collective-permute-start | bytes 184328 | tf_op jit(solution)/shard_map/ppermute | solution.py:18
  77.1 0.7 copy-start.1
  77.8 9.7 %collective-permute-start.3 = (f32[64,128]{1,0:T(8,128)S(1)}, f32[64,128]{1,0:T(8,128)S(1)}, u32[]{:S(2)}, u32[]{:S(2)}) collective-permute-start(f32[64,128]{1,0:T(8,128)S(1)} %add_beside.1), channel_id=1, source_target_pairs={{16,0},{32,16},{48,32},{64,48},{80,64},{96,80},{112,96},{17,1},{33... | collective-permute-start | bytes 98312 | tf_op jit(solution)/shard_map/ppermute | solution.py:18
  81.4 6.1 %copy-start.2 = (f32[64,640]{1,0:T(8,128)S(1)}, f32[64,640]{1,0:T(8,128)}, u32[]{:S(2)}) copy-start(f32[64,640]{1,0:T(8,128)} %copy-done.1) | copy-start | bytes 491524
  81.5 6.1 %collective-permute-start.2 = (f32[64,128]{1,0:T(8,128)S(1)}, f32[64,128]{1,0:T(8,128)S(1)}, u32[]{:S(2)}, u32[]{:S(2)}) collective-permute-start(f32[64,128]{1,0:T(8,128)S(1)} %add_beside.1), channel_id=1, source_target_pairs={{0,16},{16,32},{32,48},{48,64},{64,80},{80,96},{96,112},{1,17},{17... | collective-permute-start | bytes 98312 | tf_op jit(solution)/shard_map/ppermute | solution.py:18

commit v3 on v2

--- a/solution.py
+++ b/solution.py
@@ -10,12 +10,6 @@
 RS = 4
 LANES = 128
 BOTH = ("skyx", "skyy")
-
-
-def from_behind(value, axis, steps):
-    count = lax.axis_size(axis)
-    initial, last = (max(0, -steps), min(count, count - steps))
-    return lax.ppermute(value, axis, [(source, source + steps) for source in range(initial, last)])
 
 
 def pack_kernel(planes, me, patch_of, valid, *refs):
@@ -81,6 +75,7 @@
             bytes_accessed=2 * (len(planes) * blocks + devices) * rows * width,
             transcendentals=0,
         ),
+        compiler_params=pltpu.CompilerParams(vmem_limit_bytes=63 << 20),
         name="pack",
     )(me, patch_of, valid, *planes)
 
@@ -120,16 +115,33 @@
     )(across_taps, down_taps, row_at)
 
 
-def coadd_kernel(margin, flux, choose, down, across, inner, top, bottom, wide, channels, mixed):
+def coadd_kernel(
+    margin, here, flux_far, choose, down_far, across_far, inner, first, second,
+    flux, down, across, wide, channels, mixed, arrived,
+):
     sources, rows, width = flux.shape
     count, ext, _ = down.shape
     pieces = width // LANES
     tiles = pieces + 1
-    edge = top.shape[0]
+    edge = first.shape[0]
     tall = inner.shape[0]
-    for piece in range(pieces):
-        lanes = pl.ds(piece * LANES, LANES)
-        wide[piece] = flux[:, :, lanes].reshape(sources * rows, LANES).astype(jnp.float32)
+    chunks = arrived.shape[0] - 2
+    share = sources // chunks
+    copies = []
+    for chunk in range(chunks):
+        some = pl.ds(chunk * share, share)
+        copies.append(pltpu.make_async_copy(flux_far.at[some], flux.at[some], arrived.at[chunk]))
+    copies.append(pltpu.make_async_copy(down_far, down, arrived.at[chunks]))
+    copies.append(pltpu.make_async_copy(across_far, across, arrived.at[chunks + 1]))
+    for copy in copies:
+        copy.start()
+    for chunk in range(chunks):
+        copies[chunk].wait()
+        some = pl.ds(chunk * share, share)
+        for piece in range(pieces):
+            lanes = pl.ds(piece * LANES, LANES)
+            block = flux[some, :, lanes].reshape(share * rows, LANES)
+            wide[piece, pl.ds(chunk * share * rows, share * rows), :] = block.astype(jnp.float32)
     table = choose[...]
     for pair in range(rows // 2):
         halves = []
@@ -139,6 +151,8 @@
             halves.append(jnp.concatenate(row, axis=1))
         summed = jnp.dot(table, jnp.concatenate(halves, axis=0), preferred_element_type=jnp.float32)
         channels[:, pair * 8 : pair * 8 + 8, :] = summed.reshape(count, 8, width)
+    copies[chunks].wait()
+    copies[chunks + 1].wait()
     zeros = jnp.zeros((ext, LANES), jnp.bfloat16)
     for c in range(count):
         mixed[c, :, :LANES] = zeros
@@ -152,12 +166,14 @@
         total = total + jnp.dot(windows, across[c], preferred_element_type=jnp.float32)
     whole = jnp.concatenate([total[t * ext : (t + 1) * ext] for t in range(tiles)], axis=1)
     whole = pltpu.roll(whole, tiles * LANES - margin, 1)
-    top[...] = whole[:edge]
     inner[...] = whole[edge : edge + tall]
-    bottom[...] = whole[edge + tall :]
-
-
-def convolve_sum(margin, flux, choose, down, across):
+    top, bottom = whole[:edge], whole[edge + tall :]
+    even = lax.rem(here[1], 2) == 0
+    first[...] = jnp.where(even, bottom, top)
+    second[...] = jnp.where(even, top, bottom)
+
+
+def convolve_sum(margin, at, flux, choose, down, across):
     sources, rows, width = flux.shape
     count, ext, _ = down.shape
     tiles = width // LANES + 1
@@ -167,12 +183,22 @@
     return pl.pallas_call(
         functools.partial(coadd_kernel, margin),
         out_shape=tuple(jax.ShapeDtypeStruct(size, jnp.float32) for size in sizes),
-        in_specs=[pl.BlockSpec(memory_space=pltpu.VMEM)] * 4,
+        in_specs=[
+            pl.BlockSpec(memory_space=pltpu.SMEM),
+            pl.BlockSpec(memory_space=pltpu.HBM),
+            pl.BlockSpec(memory_space=pltpu.VMEM),
+            pl.BlockSpec(memory_space=pltpu.HBM),
+            pl.BlockSpec(memory_space=pltpu.HBM),
+        ],
         out_specs=(pl.BlockSpec(memory_space=pltpu.VMEM),) * len(sizes),
         scratch_shapes=[
+            pltpu.VMEM(flux.shape, jnp.bfloat16),
+            pltpu.VMEM(down.shape, jnp.bfloat16),
+            pltpu.VMEM(across.shape, jnp.bfloat16),
             pltpu.VMEM((width // LANES, sources * rows, LANES), jnp.float32),
             pltpu.VMEM((count, RS * rows, width), jnp.float32),
             pltpu.VMEM((count, ext, (tiles + 1) * LANES), jnp.bfloat16),
+            pltpu.SemaphoreType.DMA((4 + 2,)),
         ],
         compiler_params=pltpu.CompilerParams(vmem_limit_bytes=20 << 20),
         cost_estimate=pl.CostEstimate(
@@ -181,7 +207,7 @@
             transcendentals=0,
         ),
         name="convolve_sum",
-    )(flux, choose, down, across)
+    )(at, flux, choose, down, across)
 
 
 def weight_kernel(row_in_patch, kept, out):
@@ -208,50 +234,60 @@
     )(row_in_patch, kept)
 
 
-def side_kernel(side, top, bottom, out):
-    tall, _ = side.shape
-    edge = top.shape[0]
-    out[:edge, :] = side[:edge, :] + top[...]
-    out[edge : tall - edge, :] = side[edge : tall - edge, :]
-    out[tall - edge :, :] = side[tall - edge :, :] + bottom[...]
-
-
-def add_beside(inner, top, bottom):
+def by_parity(place, first, second):
+    even = lax.rem(place, 2) == 0
+    return jnp.where(even, second, first), jnp.where(even, first, second)
+
+
+def side_kernel(at, inner, first, second, out):
     tall, wide = inner.shape
-    edge = top.shape[0]
-    last = wide // LANES - 1
+    edge = first.shape[0]
+    lanes = slice(wide - LANES, wide)
+    above, below = by_parity(at[1], first[:, lanes], second[:, lanes])
+    out[:edge, :] = inner[:edge, lanes] + above
+    out[edge : tall - edge, :] = inner[edge : tall - edge, lanes]
+    out[tall - edge :, :] = inner[tall - edge :, lanes] + below
+
+
+def add_beside(at, inner, first, second):
     return pl.pallas_call(
         side_kernel,
-        out_shape=jax.ShapeDtypeStruct((tall, LANES), jnp.float32),
-        grid=(1,),
-        in_specs=[pl.BlockSpec((size, LANES), lambda step: (0, last)) for size in (tall, edge, edge)],
-        out_specs=pl.BlockSpec((tall, LANES), lambda step: (0, 0)),
+        out_shape=jax.ShapeDtypeStruct((inner.shape[0], LANES), jnp.float32),
+        in_specs=[pl.BlockSpec(memory_space=pltpu.SMEM)] + [pl.BlockSpec(memory_space=pltpu.VMEM)] * 3,
+        out_specs=pl.BlockSpec(memory_space=pltpu.VMEM),
         compiler_params=pltpu.CompilerParams(vmem_limit_bytes=4 << 20),
         name="add_beside",
-    )(inner, top, bottom)
-
-
-def finish_kernel(margin, inner, top, bottom, left, right, out):
+    )(at, inner, first, second)
+
+
+def finish_kernel(margin, at, inner, first, second, near, far, out):
     tall, width = out.shape
-    edge = top.shape[0]
+    edge = first.shape[0]
+    above, below = by_parity(at[1], first[:, :width], second[:, :width])
+    out[:edge, :] = inner[:edge, :width] + above
+    out[edge : tall - edge, :] = inner[edge : tall - edge, :width]
+    out[tall - edge :, :] = inner[tall - edge :, :width] + below
     lane = lax.broadcasted_iota(jnp.int32, (1, LANES), 1)
-    out[:edge, :] = inner[:edge, :width] + top[:, :width]
-    out[edge : tall - edge, :] = inner[edge : tall - edge, :width]
-    out[tall - edge :, :] = inner[tall - edge :, :width] + bottom[:, :width]
-    out[:, :LANES] += jnp.where(lane < margin, left[...], 0.0)
-    out[:, width - LANES :] += jnp.where(lane >= LANES - margin, right[...], 0.0)
-
-
-def finish(margin, inner, top, bottom, left, right):
+    left, right = by_parity(at[0], near[...], far[...])
+    out[:, :LANES] += jnp.where(lane < margin, left, 0.0)
+    out[:, width - LANES :] += jnp.where(lane >= LANES - margin, right, 0.0)
+
+
+def finish(margin, at, inner, first, second, near, far):
     tall, wide = inner.shape
     return pl.pallas_call(
         functools.partial(finish_kernel, margin),
         out_shape=jax.ShapeDtypeStruct((tall, wide - LANES), jnp.float32),
-        in_specs=[pl.BlockSpec(memory_space=pltpu.VMEM)] * 5,
+        in_specs=[pl.BlockSpec(memory_space=pltpu.SMEM)] + [pl.BlockSpec(memory_space=pltpu.VMEM)] * 5,
         out_specs=pl.BlockSpec(memory_space=pltpu.VMEM),
         compiler_params=pltpu.CompilerParams(vmem_limit_bytes=4 << 20),
         name="finish",
-    )(inner, top, bottom, left, right)
+    )(at, inner, first, second, near, far)
+
+
+def swap(value, axis, first):
+    pairs = [(i, i + 1) for i in range(first, lax.axis_size(axis) - 1, 2)]
+    return lax.ppermute(value, axis, pairs + [(j, i) for i, j in pairs])
 
 
 def body(
@@ -295,12 +331,14 @@
     row_in_patch = row_in_patch.reshape(1, devices * row_count)
     kept, table, down, across, row_in_patch = lax.optimization_barrier((kept, table, down, across, row_in_patch))
     kept_in = lax.all_to_all(kept, BOTH, split_axis=0, concat_axis=0, tiled=True)
-    inner, top, bottom = convolve_sum(margin, weighted_in, table, down, across)
-    top, bottom = from_behind(bottom, "skyy", 1), from_behind(top, "skyy", -1)
-    side = add_beside(inner, top, bottom)
-    left, right = from_behind(side, "skyx", 1), from_behind(side, "skyx", -1)
+    at = jnp.stack([my_column, my_line]).astype(jnp.int32)
+    down, across = (pltpu.with_memory_space_constraint(x, pltpu.HBM) for x in (down, across))
+    inner, first, second = convolve_sum(margin, at, weighted_in, table, down, across)
+    first, second = swap(first, "skyy", 0), swap(second, "skyy", 1)
+    side = add_beside(at, inner, first, second)
+    near, far = swap(side, "skyx", 0), swap(side, "skyx", 1)
     weight_sum = place_weights(row_in_patch, kept_in)
-    coadd = finish(margin, inner, top, bottom, left, right)
+    coadd = finish(margin, at, inner, first, second, near, far)
     return (coadd, weight_sum)
 
 

time: 88.8 us -> 85.4 us (0.962)
  starting transfers between devices: 31.8 us -> 27.3 us
  Pallas kernels: 15.8 us -> 17.2 us
    ppermute x4, starting transfers between devices: 14.3 us -> 10.4 us  [swap(): return lax.ppermute(value, axis, pairs + [(j, i) for i, j in pairs])]
    pallas_call x1, Pallas kernels: 4.91 us -> 6.77 us  [convolve_sum(): pl.pallas_call(functools.partial(coadd_kernel, margin), out_shape=tuple((...]
    ppermute x4, waiting for transfers between devices: 13.4 us -> 15.2 us  [swap(): return lax.ppermute(value, axis, pairs + [(j, i) for i, j in pairs])]
    pallas_call x1, Pallas kernels: 2.72 us -> 1.13 us  [place_weights(): pl.pallas_call(weight_kernel, out_shape=jax.ShapeDtypeStruct((RS * rows,...]
    all_to_all x1, waiting for transfers between devices: 22.5 us -> 21.1 us  [body(): lax.all_to_all(weighted, BOTH, split_axis=0, concat_axis=0, tiled=True)]
    all_to_all x1, starting transfers between devices: 6.61 us -> 5.63 us  [body(): lax.all_to_all(kept, BOTH, split_axis=0, concat_axis=0, tiled=True)]
    unnamed x20 -> x16, local copies, waits for them, and re-layouts: 2.58 us -> 1.91 us
  transfers between devices with their start and end apart: 6 -> 6, of which waited for: 2 -> 4; matrix products, arithmetic and copies ran while one was open for 1% -> 2% of each run, Pallas kernels for 13% -> 15%
where the time goes in v3:
time: 85.4 us; the launch traced here: 84.9 us
  waiting for transfers between devices  36.3 us (43%)
  starting transfers between devices  27.3 us (32%)
  Pallas kernels  17.2 us (20%)
  local copies, waits for them, and re-layouts  2.4 us (3%)
  between operations  0.91 us (1%)
    all_to_all x1, waiting for transfers between devices, body(): lax.all_to_all(weighted, BOTH, split_axis=0, concat_axis=0, tiled=True)  21.1 us
    ppermute x4, waiting for transfers between devices, swap(): return lax.ppermute(value, axis, pairs + [(j, i) for i, j in pairs])  15.2 us
    all_to_all x1, starting transfers between devices, body(): lax.all_to_all(weighted, BOTH, split_axis=0, concat_axis=0, tiled=True)  11.3 us
    ppermute x4, starting transfers between devices, swap(): return lax.ppermute(value, axis, pairs + [(j, i) for i, j in pairs])  10.4 us
    pallas_call x2, Pallas kernels, pack(): pl.pallas_call(functools.partial(pack_kernel, len(planes)), out_shape=jax...  6.97 us
    pallas_call x1, Pallas kernels, convolve_sum(): pl.pallas_call(functools.partial(coadd_kernel, margin), out_shape=tuple((...  6.77 us
    all_to_all x1, starting transfers between devices, body(): lax.all_to_all(kept, BOTH, split_axis=0, concat_axis=0, tiled=True)  5.63 us
    unnamed x16, local copies, waits for them, and re-layouts  1.91 us
  transfers between devices with their start and end apart: 6, of which 4 were waited for; matrix products, arithmetic and copies ran while one was open for 2% of the time, Pallas kernels for 15%

profile of v3, /device:TPU:3, one launch (start us, length us, event | category | flops | bytes accessed | tf_op | source)
XLA Modules:
  0.0 84.9 jit_solution(8832453001719678693)
XLA Ops:
  0.6 0.0 copy-start
  0.7 3.5 %pack.2 = bf16[128,16,512]{2,1,0:T(8,128)(2,1)} custom-call(s32[1]{0:T(128)} %bitcast.2.me, s32[8192]{0:T(1024)} %bitcast.10, s32[8192]{0:T(1024)} %valid.3, bf16[64,16,512]{2,1,0:T(8,128)(2,1)} %refs_0_.3, bf16[64,16,512]{2,1,0:T(8,128)(2,1)} %refs_1_.1), custom_call_target="tpu_custom_call" | custom-call | flops 1048576 | bytes 4194304 | tf_op jit(solution)/shard_map/pack/pallas_call | solution.py:59
  4.2 0.0 copy-start.3
  4.2 0.0 copy-start.4
  4.2 0.0 copy-start.5
  4.2 0.0 copy-start.6
  4.2 11.3 %all-to-all-start = ((bf16[128,16,512]{2,1,0:T(8,128)(2,1)}), bf16[128,16,512]{2,1,0:T(8,128)(2,1)}, u32[]{:S(2)}, u32[]{:S(2)}) async-start(bf16[128,16,512]{2,1,0:T(8,128)(2,1)} %pack.2), calls=%async_computation | async-start | bytes 4194304 | tf_op jit(solution)/shard_map/all_to_all | solution.py:308
  15.5 0.0 copy-done.3
  15.5 0.0 copy-start.7
  15.6 0.1 compare_reduce_fusion
  15.7 0.1 eq.43
  15.8 0.0 copy-done.4
  15.8 0.1 slice.7
  15.8 0.1 rev.3
  15.9 0.0 copy-done.5
  15.9 0.1 reshape.141
  16.0 0.1 select_reduce_fusion
  16.1 0.1 add_select_fusion
  16.2 0.1 select_n.53.row_in_patch
  16.3 0.0 copy-done.6
  16.4 0.1 pad.10.clone
  16.5 0.1 pad_maximum_fusion.down_taps
  16.5 0.5 band_tables.1
  17.1 0.0 copy-start.1
  17.1 1.0 %copy-done.1 = bf16[20,256,128]{2,1,0:T(8,128)(2,1)} copy-done((bf16[20,256,128]{2,1,0:T(8,128)(2,1)}, bf16[20,256,128]{2,1,0:T(8,128)(2,1)S(1)}, u32[]{:S(2)}) %copy-start.1) | copy-done | bytes 1310744
  18.1 0.0 copy-start.2
  18.1 0.8 copy-done.2
  18.9 3.5 %pack.3 = bf16[128,16,512]{2,1,0:T(8,128)(2,1)} custom-call(s32[1]{0:T(128)} %bitcast.2.me, s32[8192]{0:T(1024)} %bitcast.11, s32[8192]{0:T(1024)} %valid.3, bf16[64,16,512]{2,1,0:T(8,128)(2,1)} %refs_0_.3), custom_call_target="tpu_custom_call" | custom-call | flops 1048576 | bytes 3145728 | tf_op jit(solution)/shard_map/pack/pallas_call | solution.py:59
  22.4 0.0 copy-done
  22.4 0.0 copy-done.7
  22.4 0.2 convolution_bitcast_fusion
  22.8 21.1 %all-to-all-done.flux_far = bf16[128,16,512]{2,1,0:T(8,128)(2,1)} async-done(((bf16[128,16,512]{2,1,0:T(8,128)(2,1)}), bf16[128,16,512]{2,1,0:T(8,128)(2,1)}, u32[]{:S(2)}, u32[]{:S(2)}) %all-to-all-start) | async-done | bytes 2097184 | tf_op jit(solution)/shard_map/all_to_all | solution.py:308
  43.9 5.6 %all-to-all-start.1 = ((bf16[128,16,512]{2,1,0:T(8,128)(2,1)}), bf16[128,16,512]{2,1,0:T(8,128)(2,1)S(1)}, u32[]{:S(2)}, u32[]{:S(2)}) async-start(bf16[128,16,512]{2,1,0:T(8,128)(2,1)} %pack.3), calls=%async_computation.1 | async-start | bytes 4194304 | tf_op jit(solution)/shard_map/all_to_all | solution.py:333
  49.5 0.1 pad_add_fusion.here.at
  49.6 6.8 %convolve_sum.1 = (f32[64,640]{1,0:T(8,128)S(1)}, f32[24,640]{1,0:T(8,128)S(1)}, f32[24,640]{1,0:T(8,128)S(1)}) custom-call(s32[2]{0:T(128)S(1)} %pad_add_fusion.here.at, bf16[128,16,512]{2,1,0:T(8,128)(2,1)} %all-to-all-done.flux_far, bf16[160,256]{1,0:T(8,128)(2,1)S(1)} %fusion.3.choose, bf16[20,112,64]{2,1,0:T(8,128)(2,1)} %copy-done.2, ...), custom_call_target="tpu_custom_call" | custom-call | flops 734003200 | bytes 2383872 | tf_op jit(solution)/shard_map/convolve_sum/pallas_call | solution.py:183
  56.4 1.5 %collective-permute-start = (f32[24,640]{1,0:T(8,128)S(1)}, f32[24,640]{1,0:T(8,128)S(1)}, u32[]{:S(2)}, u32[]{:S(2)}) collective-permute-start(f32[24,640]{1,0:T(8,128)S(1)} %get-tuple-element.18), channel_id=1, source_target_pairs={{0,1},{2,3},{4,5},{6,7},{8,9},{10,11},{12,13},{14,15},{1,0},{3,2},... | collective-permute-start | bytes 184328 | tf_op jit(solution)/shard_map/ppermute | solution.py:290
  57.8 3.9 %collective-permute-start.1 = (f32[24,640]{1,0:T(8,128)S(1)}, f32[24,640]{1,0:T(8,128)S(1)}, u32[]{:S(2)}, u32[]{:S(2)}) collective-permute-start(f32[24,640]{1,0:T(8,128)S(1)} %get-tuple-element.19), channel_id=1, source_target_pairs={{1,2},{3,4},{5,6},{7,8},{9,10},{11,12},{13,14},{2,1},{4,3},{6,5},{... | collective-permute-start | bytes 184328 | tf_op jit(solution)/shard_map/ppermute | solution.py:290
  61.7 13.5 %collective-permute-done.first = f32[24,640]{1,0:T(8,128)S(1)} collective-permute-done((f32[24,640]{1,0:T(8,128)S(1)}, f32[24,640]{1,0:T(8,128)S(1)}, u32[]{:S(2)}, u32[]{:S(2)}) %collective-permute-start) | collective-permute-done | bytes 61472 | tf_op jit(solution)/shard_map/ppermute | solution.py:290
  75.3 1.4 %collective-permute-done.1.second = f32[24,640]{1,0:T(8,128)S(1)} collective-permute-done((f32[24,640]{1,0:T(8,128)S(1)}, f32[24,640]{1,0:T(8,128)S(1)}, u32[]{:S(2)}, u32[]{:S(2)}) %collective-permute-start.1) | collective-permute-done | bytes 61472 | tf_op jit(solution)/shard_map/ppermute | solution.py:290
  76.6 0.6 add_beside.1
  77.2 4.9 %collective-permute-start.3 = (f32[64,128]{1,0:T(8,128)S(1)}, f32[64,128]{1,0:T(8,128)S(1)}, u32[]{:S(2)}, u32[]{:S(2)}) collective-permute-start(f32[64,128]{1,0:T(8,128)S(1)} %add_beside.1), channel_id=1, source_target_pairs={{16,32},{48,64},{80,96},{32,16},{64,48},{96,80},{17,33},{49,65},{8... | collective-permute-start | bytes 98312 | tf_op jit(solution)/shard_map/ppermute | solution.py:290
  82.1 0.1 collective-permute-start.2
  82.2 0.0 all-to-all-done.1.kept
  82.2 1.1 %place_weights.1 = f32[64,512]{1,0:T(8,128)} custom-call(s32[1,2048]{1,0:T(1,128)S(1)} %select_n.53.row_in_patch, bf16[128,16,512]{2,1,0:T(8,128)(2,1)S(1)} %all-to-all-done.1.kept), custom_call_target="tpu_custom_call" | custom-call | flops 134217728 | bytes 2097152 | tf_op jit(solution)/shard_map/place_weights/pallas_call | solution.py:222
  83.3 0.3 collective-permute-done.3.far
  83.7 0.0 collective-permute-done.2.near
  83.7 1.2 %finish.1 = f32[64,512]{1,0:T(8,128)} custom-call(s32[2]{0:T(128)S(1)} %pad_add_fusion.here.at, f32[64,640]{1,0:T(8,128)S(1)} %get-tuple-element.17.inner, f32[24,640]{1,0:T(8,128)S(1)} %collective-permute-done.first, f32[24,640]{1,0:T(8,128)S(1)} %collective-permute-done.1.second, f32[64,128]{1,0:T(8,128)S(1)} %collective-permute-done.2.near, ...), custom_call_target="tpu_custom_call" | custom-call | tf_op jit(solution)/shard_map/finish/pallas_call | solution.py:278
  (8 shorter events, 0.1 us)
Async XLA Ops:
  0.6 21.8 %copy-start = (f32[64,20]{0,1:T(8,128)S(1)}, f32[64,20]{0,1:T(8,128)}, u32[]{:S(2)}) copy-start(f32[64,20]{0,1:T(8,128)} %param.15) | copy-start | bytes 15364
  4.2 11.4 %copy-start.3 = (s32[8192,1]{0,1:T(1,128)S(1)}, s32[8192,1]{0,1:T(1,128)}, u32[]{:S(2)}) copy-start(s32[8192,1]{0,1:T(1,128)} %param.11) | copy-start | bytes 98308
  4.2 11.6 %copy-start.4 = (f32[20,41]{1,0:T(8,128)S(1)}, f32[20,41]{1,0:T(8,128)}, u32[]{:S(2)}) copy-start(f32[20,41]{1,0:T(8,128)} %param.17) | copy-start | bytes 9844
  4.2 11.7 %copy-start.5 = (s32[8192]{0:T(1024)S(1)}, s32[8192]{0:T(1024)}, u32[]{:S(2)}) copy-start(s32[8192]{0:T(1024)} %param.12) | copy-start | bytes 98308
  4.2 12.1 %copy-start.6 = (f32[20,41]{1,0:T(8,128)S(1)}, f32[20,41]{1,0:T(8,128)}, u32[]{:S(2)}) copy-start(f32[20,41]{1,0:T(8,128)} %param.16) | copy-start | bytes 9844
  4.2 39.6 %all-to-all-start = ((bf16[128,16,512]{2,1,0:T(8,128)(2,1)}), bf16[128,16,512]{2,1,0:T(8,128)(2,1)}, u32[]{:S(2)}, u32[]{:S(2)}) async-start(bf16[128,16,512]{2,1,0:T(8,128)(2,1)} %pack.2), calls=%async_computation | async-start | bytes 4194304 | tf_op jit(solution)/shard_map/all_to_all | solution.py:308
  15.5 6.9 %copy-start.7 = (s32[128]{0:T(128)S(1)}, s32[128]{0:T(128)}, u32[]{:S(2)}) copy-start(s32[128]{0:T(128)} %param.14) | copy-start | bytes 1540
  17.1 1.1 %copy-start.1 = (bf16[20,256,128]{2,1,0:T(8,128)(2,1)}, bf16[20,256,128]{2,1,0:T(8,128)(2,1)S(1)}, u32[]{:S(2)}) copy-start(bf16[20,256,128]{2,1,0:T(8,128)(2,1)S(1)} %get-tuple-element.16.across_far) | copy-start | bytes 3932164
  18.1 0.8 copy-start.2
  43.9 38.3 %all-to-all-start.1 = ((bf16[128,16,512]{2,1,0:T(8,128)(2,1)}), bf16[128,16,512]{2,1,0:T(8,128)(2,1)S(1)}, u32[]{:S(2)}, u32[]{:S(2)}) async-start(bf16[128,16,512]{2,1,0:T(8,128)(2,1)} %pack.3), calls=%async_computation.1 | async-start | bytes 4194304 | tf_op jit(solution)/shard_map/all_to_all | solution.py:333
  56.4 18.9 %collective-permute-start = (f32[24,640]{1,0:T(8,128)S(1)}, f32[24,640]{1,0:T(8,128)S(1)}, u32[]{:S(2)}, u32[]{:S(2)}) collective-permute-start(f32[24,640]{1,0:T(8,128)S(1)} %get-tuple-element.18), channel_id=1, source_target_pairs={{0,1},{2,3},{4,5},{6,7},{8,9},{10,11},{12,13},{14,15},{1,0},{3,2},... | collective-permute-start | bytes 184328 | tf_op jit(solution)/shard_map/ppermute | solution.py:290
  57.8 18.8 %collective-permute-start.1 = (f32[24,640]{1,0:T(8,128)S(1)}, f32[24,640]{1,0:T(8,128)S(1)}, u32[]{:S(2)}, u32[]{:S(2)}) collective-permute-start(f32[24,640]{1,0:T(8,128)S(1)} %get-tuple-element.19), channel_id=1, source_target_pairs={{1,2},{3,4},{5,6},{7,8},{9,10},{11,12},{13,14},{2,1},{4,3},{6,5},{... | collective-permute-start | bytes 184328 | tf_op jit(solution)/shard_map/ppermute | solution.py:290
  77.2 6.5 %collective-permute-start.3 = (f32[64,128]{1,0:T(8,128)S(1)}, f32[64,128]{1,0:T(8,128)S(1)}, u32[]{:S(2)}, u32[]{:S(2)}) collective-permute-start(f32[64,128]{1,0:T(8,128)S(1)} %add_beside.1), channel_id=1, source_target_pairs={{16,32},{48,64},{80,96},{32,16},{64,48},{96,80},{17,33},{49,65},{8... | collective-permute-start | bytes 98312 | tf_op jit(solution)/shard_map/ppermute | solution.py:290
  82.1 1.6 %collective-permute-start.2 = (f32[64,128]{1,0:T(8,128)S(1)}, f32[64,128]{1,0:T(8,128)S(1)}, u32[]{:S(2)}, u32[]{:S(2)}) collective-permute-start(f32[64,128]{1,0:T(8,128)S(1)} %add_beside.1), channel_id=1, source_target_pairs={{0,16},{32,48},{64,80},{96,112},{16,0},{48,32},{80,64},{112,96},{1... | collective-permute-start | bytes 98312 | tf_op jit(solution)/shard_map/ppermute | solution.py:290

commit v4 on v3

--- a/solution.py
+++ b/solution.py
@@ -23,7 +23,13 @@
         at = pl.ds(chunk * group, group)
         return pltpu.make_async_copy(sources[index].at[at], rooms[index].at[at], arrived.at[index, chunk])
 
-    notes = [pltpu.make_async_copy(patch_of, targets, noted.at[0]), pltpu.make_async_copy(valid, usable, noted.at[1])]
+    listed = targets.shape[0]
+    devices_listed = listed // blocks
+    some = pl.ds(pl.multiple_of(me[0] // devices_listed * listed, listed), listed)
+    notes = [
+        pltpu.make_async_copy(patch_of.at[some], targets, noted.at[0]),
+        pltpu.make_async_copy(valid.at[some], usable, noted.at[1]),
+    ]
     for note in notes:
         note.start()
     for chunk in range(chunks):
@@ -32,7 +38,7 @@
     packed[...] = jnp.zeros_like(packed)
     for note in notes:
         note.wait()
-    first = me[0] * blocks
+    first = me[0] % devices_listed * blocks
     for chunk in range(chunks):
         for index in range(planes):
             fetch(index, chunk).wait()
@@ -64,8 +70,8 @@
         scratch_shapes=[pltpu.VMEM((blocks, rows, width), jnp.bfloat16) for _ in planes]
         + [
             pltpu.VMEM((devices, rows, width), jnp.bfloat16),
-            pltpu.SMEM(patch_of.shape, jnp.int32),
-            pltpu.SMEM(valid.shape, jnp.int32),
+            pltpu.SMEM((1024,), jnp.int32),
+            pltpu.SMEM((1024,), jnp.int32),
             pltpu.SemaphoreType.DMA((len(planes), chunks)),
             pltpu.SemaphoreType.DMA((2,)),
             pltpu.SemaphoreType.DMA((pieces,)),

time: 85.4 us -> 84.8 us (level)
  Pallas kernels: 17.2 us -> 15.9 us
    pallas_call x2, Pallas kernels: 6.97 us -> 5.67 us  [pack(): pl.pallas_call(functools.partial(pack_kernel, len(planes)), out_shape=jax...]
  transfers between devices with their start and end apart: 6 -> 6, of which waited for: 4 -> 4; matrix products, arithmetic and copies ran while one was open for 2% -> 2% of each run, Pallas kernels for 15% -> 14%
where the time goes in v4:
time: 84.8 us; the launch traced here: 84.4 us
  waiting for transfers between devices  37.1 us (44%)
  starting transfers between devices  27.3 us (32%)
  Pallas kernels  15.9 us (19%)
  local copies, waits for them, and re-layouts  2.4 us (3%)
  between operations  0.91 us (1%)
    all_to_all x1, waiting for transfers between devices, body(): lax.all_to_all(weighted, BOTH, split_axis=0, concat_axis=0, tiled=True)  21.9 us
    ppermute x4, waiting for transfers between devices, swap(): return lax.ppermute(value, axis, pairs + [(j, i) for i, j in pairs])  15.2 us
    all_to_all x1, starting transfers between devices, body(): lax.all_to_all(weighted, BOTH, split_axis=0, concat_axis=0, tiled=True)  11.3 us
    ppermute x4, starting transfers between devices, swap(): return lax.ppermute(value, axis, pairs + [(j, i) for i, j in pairs])  10.4 us
    pallas_call x1, Pallas kernels, convolve_sum(): pl.pallas_call(functools.partial(coadd_kernel, margin), out_shape=tuple((...  6.77 us
    pallas_call x2, Pallas kernels, pack(): pl.pallas_call(functools.partial(pack_kernel, len(planes)), out_shape=jax...  5.67 us
    all_to_all x1, starting transfers between devices, body(): lax.all_to_all(kept, BOTH, split_axis=0, concat_axis=0, tiled=True)  5.63 us
    unnamed x16, local copies, waits for them, and re-layouts  1.91 us
  transfers between devices with their start and end apart: 6, of which 4 were waited for; matrix products, arithmetic and copies ran while one was open for 2% of the time, Pallas kernels for 14%

profile of v4, /device:TPU:3, one launch (start us, length us, event | category | flops | bytes accessed | tf_op | source)
XLA Modules:
  0.0 84.4 jit_solution(22343520436332469)
XLA Ops:
  0.6 0.0 copy-start
  0.7 3.0 %pack.2 = bf16[128,16,512]{2,1,0:T(8,128)(2,1)} custom-call(s32[1]{0:T(128)} %bitcast.2.me, s32[8192]{0:T(1024)} %bitcast.10, s32[8192]{0:T(1024)} %valid.3, bf16[64,16,512]{2,1,0:T(8,128)(2,1)} %refs_0_.3, bf16[64,16,512]{2,1,0:T(8,128)(2,1)} %refs_1_.1), custom_call_target="tpu_custom_call" | custom-call | flops 1048576 | bytes 4194304 | tf_op jit(solution)/shard_map/pack/pallas_call | solution.py:65
  3.7 0.0 copy-start.3
  3.7 0.0 copy-start.4
  3.7 0.0 copy-start.5
  3.7 0.0 copy-start.6
  3.7 11.3 %all-to-all-start = ((bf16[128,16,512]{2,1,0:T(8,128)(2,1)}), bf16[128,16,512]{2,1,0:T(8,128)(2,1)}, u32[]{:S(2)}, u32[]{:S(2)}) async-start(bf16[128,16,512]{2,1,0:T(8,128)(2,1)} %pack.2), calls=%async_computation | async-start | bytes 4194304 | tf_op jit(solution)/shard_map/all_to_all | solution.py:314
  15.0 0.0 copy-done.3
  15.1 0.0 copy-start.7
  15.1 0.1 compare_reduce_fusion
  15.2 0.1 eq.43
  15.3 0.0 copy-done.4
  15.3 0.1 slice.7
  15.3 0.1 rev.3
  15.4 0.0 copy-done.5
  15.4 0.1 reshape.141
  15.5 0.1 select_reduce_fusion
  15.6 0.1 add_select_fusion
  15.7 0.1 select_n.53.row_in_patch
  15.8 0.0 copy-done.6
  15.9 0.1 pad.10.clone
  16.0 0.1 pad_maximum_fusion.down_taps
  16.0 0.5 band_tables.1
  16.6 0.0 copy-start.1
  16.6 1.0 %copy-done.1 = bf16[20,256,128]{2,1,0:T(8,128)(2,1)} copy-done((bf16[20,256,128]{2,1,0:T(8,128)(2,1)}, bf16[20,256,128]{2,1,0:T(8,128)(2,1)S(1)}, u32[]{:S(2)}) %copy-start.1) | copy-done | bytes 1310744
  17.6 0.0 copy-start.2
  17.6 0.8 copy-done.2
  18.4 2.7 %pack.3 = bf16[128,16,512]{2,1,0:T(8,128)(2,1)} custom-call(s32[1]{0:T(128)} %bitcast.2.me, s32[8192]{0:T(1024)} %bitcast.11, s32[8192]{0:T(1024)} %valid.3, bf16[64,16,512]{2,1,0:T(8,128)(2,1)} %refs_0_.3), custom_call_target="tpu_custom_call" | custom-call | flops 1048576 | bytes 3145728 | tf_op jit(solution)/shard_map/pack/pallas_call | solution.py:65
  21.1 0.0 copy-done
  21.1 0.0 copy-done.7
  21.1 0.2 convolution_bitcast_fusion
  21.5 21.9 %all-to-all-done.flux_far = bf16[128,16,512]{2,1,0:T(8,128)(2,1)} async-done(((bf16[128,16,512]{2,1,0:T(8,128)(2,1)}), bf16[128,16,512]{2,1,0:T(8,128)(2,1)}, u32[]{:S(2)}, u32[]{:S(2)}) %all-to-all-start) | async-done | bytes 2097184 | tf_op jit(solution)/shard_map/all_to_all | solution.py:314
  43.4 5.6 %all-to-all-start.1 = ((bf16[128,16,512]{2,1,0:T(8,128)(2,1)}), bf16[128,16,512]{2,1,0:T(8,128)(2,1)S(1)}, u32[]{:S(2)}, u32[]{:S(2)}) async-start(bf16[128,16,512]{2,1,0:T(8,128)(2,1)} %pack.3), calls=%async_computation.1 | async-start | bytes 4194304 | tf_op jit(solution)/shard_map/all_to_all | solution.py:339
  49.0 0.1 pad_add_fusion.here.at
  49.1 6.8 %convolve_sum.1 = (f32[64,640]{1,0:T(8,128)S(1)}, f32[24,640]{1,0:T(8,128)S(1)}, f32[24,640]{1,0:T(8,128)S(1)}) custom-call(s32[2]{0:T(128)S(1)} %pad_add_fusion.here.at, bf16[128,16,512]{2,1,0:T(8,128)(2,1)} %all-to-all-done.flux_far, bf16[160,256]{1,0:T(8,128)(2,1)S(1)} %fusion.3.choose, bf16[20,112,64]{2,1,0:T(8,128)(2,1)} %copy-done.2, ...), custom_call_target="tpu_custom_call" | custom-call | flops 734003200 | bytes 2383872 | tf_op jit(solution)/shard_map/convolve_sum/pallas_call | solution.py:189
  55.9 1.5 %collective-permute-start = (f32[24,640]{1,0:T(8,128)S(1)}, f32[24,640]{1,0:T(8,128)S(1)}, u32[]{:S(2)}, u32[]{:S(2)}) collective-permute-start(f32[24,640]{1,0:T(8,128)S(1)} %get-tuple-element.18), channel_id=1, source_target_pairs={{0,1},{2,3},{4,5},{6,7},{8,9},{10,11},{12,13},{14,15},{1,0},{3,2},... | collective-permute-start | bytes 184328 | tf_op jit(solution)/shard_map/ppermute | solution.py:296
  57.3 3.9 %collective-permute-start.1 = (f32[24,640]{1,0:T(8,128)S(1)}, f32[24,640]{1,0:T(8,128)S(1)}, u32[]{:S(2)}, u32[]{:S(2)}) collective-permute-start(f32[24,640]{1,0:T(8,128)S(1)} %get-tuple-element.19), channel_id=1, source_target_pairs={{1,2},{3,4},{5,6},{7,8},{9,10},{11,12},{13,14},{2,1},{4,3},{6,5},{... | collective-permute-start | bytes 184328 | tf_op jit(solution)/shard_map/ppermute | solution.py:296
  61.2 13.5 %collective-permute-done.first = f32[24,640]{1,0:T(8,128)S(1)} collective-permute-done((f32[24,640]{1,0:T(8,128)S(1)}, f32[24,640]{1,0:T(8,128)S(1)}, u32[]{:S(2)}, u32[]{:S(2)}) %collective-permute-start) | collective-permute-done | bytes 61472 | tf_op jit(solution)/shard_map/ppermute | solution.py:296
  74.8 1.4 %collective-permute-done.1.second = f32[24,640]{1,0:T(8,128)S(1)} collective-permute-done((f32[24,640]{1,0:T(8,128)S(1)}, f32[24,640]{1,0:T(8,128)S(1)}, u32[]{:S(2)}, u32[]{:S(2)}) %collective-permute-start.1) | collective-permute-done | bytes 61472 | tf_op jit(solution)/shard_map/ppermute | solution.py:296
  76.1 0.6 add_beside.1
  76.7 4.9 %collective-permute-start.3 = (f32[64,128]{1,0:T(8,128)S(1)}, f32[64,128]{1,0:T(8,128)S(1)}, u32[]{:S(2)}, u32[]{:S(2)}) collective-permute-start(f32[64,128]{1,0:T(8,128)S(1)} %add_beside.1), channel_id=1, source_target_pairs={{16,32},{48,64},{80,96},{32,16},{64,48},{96,80},{17,33},{49,65},{8... | collective-permute-start | bytes 98312 | tf_op jit(solution)/shard_map/ppermute | solution.py:296
  81.6 0.1 collective-permute-start.2
  81.7 0.0 all-to-all-done.1.kept
  81.7 1.1 %place_weights.1 = f32[64,512]{1,0:T(8,128)} custom-call(s32[1,2048]{1,0:T(1,128)S(1)} %select_n.53.row_in_patch, bf16[128,16,512]{2,1,0:T(8,128)(2,1)S(1)} %all-to-all-done.1.kept), custom_call_target="tpu_custom_call" | custom-call | flops 134217728 | bytes 2097152 | tf_op jit(solution)/shard_map/place_weights/pallas_call | solution.py:228
  82.8 0.3 collective-permute-done.3.far
  83.2 0.0 collective-permute-done.2.near
  83.2 1.2 %finish.1 = f32[64,512]{1,0:T(8,128)} custom-call(s32[2]{0:T(128)S(1)} %pad_add_fusion.here.at, f32[64,640]{1,0:T(8,128)S(1)} %get-tuple-element.17.inner, f32[24,640]{1,0:T(8,128)S(1)} %collective-permute-done.first, f32[24,640]{1,0:T(8,128)S(1)} %collective-permute-done.1.second, f32[64,128]{1,0:T(8,128)S(1)} %collective-permute-done.2.near, ...), custom_call_target="tpu_custom_call" | custom-call | tf_op jit(solution)/shard_map/finish/pallas_call | solution.py:284
  (8 shorter events, 0.1 us)
Async XLA Ops:
  0.6 20.5 %copy-start = (f32[64,20]{0,1:T(8,128)S(1)}, f32[64,20]{0,1:T(8,128)}, u32[]{:S(2)}) copy-start(f32[64,20]{0,1:T(8,128)} %param.15) | copy-start | bytes 15364
  3.7 11.4 %copy-start.3 = (s32[8192,1]{0,1:T(1,128)S(1)}, s32[8192,1]{0,1:T(1,128)}, u32[]{:S(2)}) copy-start(s32[8192,1]{0,1:T(1,128)} %param.11) | copy-start | bytes 98308
  3.7 11.6 %copy-start.4 = (f32[20,41]{1,0:T(8,128)S(1)}, f32[20,41]{1,0:T(8,128)}, u32[]{:S(2)}) copy-start(f32[20,41]{1,0:T(8,128)} %param.17) | copy-start | bytes 9844
  3.7 11.7 %copy-start.5 = (s32[8192]{0:T(1024)S(1)}, s32[8192]{0:T(1024)}, u32[]{:S(2)}) copy-start(s32[8192]{0:T(1024)} %param.12) | copy-start | bytes 98308
  3.7 12.1 %copy-start.6 = (f32[20,41]{1,0:T(8,128)S(1)}, f32[20,41]{1,0:T(8,128)}, u32[]{:S(2)}) copy-start(f32[20,41]{1,0:T(8,128)} %param.16) | copy-start | bytes 9844
  3.7 39.6 %all-to-all-start = ((bf16[128,16,512]{2,1,0:T(8,128)(2,1)}), bf16[128,16,512]{2,1,0:T(8,128)(2,1)}, u32[]{:S(2)}, u32[]{:S(2)}) async-start(bf16[128,16,512]{2,1,0:T(8,128)(2,1)} %pack.2), calls=%async_computation | async-start | bytes 4194304 | tf_op jit(solution)/shard_map/all_to_all | solution.py:314
  15.1 6.1 %copy-start.7 = (s32[128]{0:T(128)S(1)}, s32[128]{0:T(128)}, u32[]{:S(2)}) copy-start(s32[128]{0:T(128)} %param.14) | copy-start | bytes 1540
  16.6 1.1 %copy-start.1 = (bf16[20,256,128]{2,1,0:T(8,128)(2,1)}, bf16[20,256,128]{2,1,0:T(8,128)(2,1)S(1)}, u32[]{:S(2)}) copy-start(bf16[20,256,128]{2,1,0:T(8,128)(2,1)S(1)} %get-tuple-element.16.across_far) | copy-start | bytes 3932164
  17.6 0.8 copy-start.2
  43.4 38.3 %all-to-all-start.1 = ((bf16[128,16,512]{2,1,0:T(8,128)(2,1)}), bf16[128,16,512]{2,1,0:T(8,128)(2,1)S(1)}, u32[]{:S(2)}, u32[]{:S(2)}) async-start(bf16[128,16,512]{2,1,0:T(8,128)(2,1)} %pack.3), calls=%async_computation.1 | async-start | bytes 4194304 | tf_op jit(solution)/shard_map/all_to_all | solution.py:339
  55.9 18.9 %collective-permute-start = (f32[24,640]{1,0:T(8,128)S(1)}, f32[24,640]{1,0:T(8,128)S(1)}, u32[]{:S(2)}, u32[]{:S(2)}) collective-permute-start(f32[24,640]{1,0:T(8,128)S(1)} %get-tuple-element.18), channel_id=1, source_target_pairs={{0,1},{2,3},{4,5},{6,7},{8,9},{10,11},{12,13},{14,15},{1,0},{3,2},... | collective-permute-start | bytes 184328 | tf_op jit(solution)/shard_map/ppermute | solution.py:296
  57.3 18.8 %collective-permute-start.1 = (f32[24,640]{1,0:T(8,128)S(1)}, f32[24,640]{1,0:T(8,128)S(1)}, u32[]{:S(2)}, u32[]{:S(2)}) collective-permute-start(f32[24,640]{1,0:T(8,128)S(1)} %get-tuple-element.19), channel_id=1, source_target_pairs={{1,2},{3,4},{5,6},{7,8},{9,10},{11,12},{13,14},{2,1},{4,3},{6,5},{... | collective-permute-start | bytes 184328 | tf_op jit(solution)/shard_map/ppermute | solution.py:296
  76.7 6.5 %collective-permute-start.3 = (f32[64,128]{1,0:T(8,128)S(1)}, f32[64,128]{1,0:T(8,128)S(1)}, u32[]{:S(2)}, u32[]{:S(2)}) collective-permute-start(f32[64,128]{1,0:T(8,128)S(1)} %add_beside.1), channel_id=1, source_target_pairs={{16,32},{48,64},{80,96},{32,16},{64,48},{96,80},{17,33},{49,65},{8... | collective-permute-start | bytes 98312 | tf_op jit(solution)/shard_map/ppermute | solution.py:296
  81.6 1.6 %collective-permute-start.2 = (f32[64,128]{1,0:T(8,128)S(1)}, f32[64,128]{1,0:T(8,128)S(1)}, u32[]{:S(2)}, u32[]{:S(2)}) collective-permute-start(f32[64,128]{1,0:T(8,128)S(1)} %add_beside.1), channel_id=1, source_target_pairs={{0,16},{32,48},{64,80},{96,112},{16,0},{48,32},{80,64},{112,96},{1... | collective-permute-start | bytes 98312 | tf_op jit(solution)/shard_map/ppermute | solution.py:296

commit v5 on v4

--- a/solution.py
+++ b/solution.py
@@ -35,6 +35,7 @@
     for chunk in range(chunks):
         for index in range(planes):
             fetch(index, chunk).start()
+    unsent = packed.shape[0] - 1
     packed[...] = jnp.zeros_like(packed)
     for note in notes:
         note.wait()
@@ -46,10 +47,10 @@
             value = rooms[0][block]
             for room in rooms[1:]:
                 value = value * room[block]
-            place = targets[first + block]
-            packed[place] = jnp.where(usable[first + block] != 0, value, jnp.zeros_like(value))
+            place = jnp.where(usable[first + block] != 0, targets[first + block], unsent)
+            packed[place] = value
     pieces = sent.shape[0]
-    share = packed.shape[0] // pieces
+    share = unsent // pieces
     copies = []
     for piece in range(pieces):
         at = pl.ds(piece * share, share)
@@ -61,7 +62,7 @@
 
 def pack(devices, me, patch_of, valid, *planes):
     blocks, rows, width = planes[0].shape
-    chunks, pieces = 4, 8
+    chunks, pieces = 2, 2
     return pl.pallas_call(
         functools.partial(pack_kernel, len(planes)),
         out_shape=jax.ShapeDtypeStruct((devices, rows, width), jnp.bfloat16),
@@ -69,7 +70,7 @@
         out_specs=pl.BlockSpec(memory_space=pl.ANY),
         scratch_shapes=[pltpu.VMEM((blocks, rows, width), jnp.bfloat16) for _ in planes]
         + [
-            pltpu.VMEM((devices, rows, width), jnp.bfloat16),
+            pltpu.VMEM((devices + 1, rows, width), jnp.bfloat16),
             pltpu.SMEM((1024,), jnp.int32),
             pltpu.SMEM((1024,), jnp.int32),
             pltpu.SemaphoreType.DMA((len(planes), chunks)),
@@ -175,8 +176,8 @@
     inner[...] = whole[edge : edge + tall]
     top, bottom = whole[:edge], whole[edge + tall :]
     even = lax.rem(here[1], 2) == 0
-    first[...] = jnp.where(even, bottom, top)
-    second[...] = jnp.where(even, top, bottom)
+    first[...] = jnp.where(even, bottom, top).astype(first.dtype)
+    second[...] = jnp.where(even, top, bottom).astype(second.dtype)
 
 
 def convolve_sum(margin, at, flux, choose, down, across):
@@ -186,9 +187,10 @@
     tall = RS * rows
     edge = (ext - tall) // 2
     sizes = [(tall, tiles * LANES), (edge, tiles * LANES), (edge, tiles * LANES)]
+    types = (jnp.float32, jnp.bfloat16, jnp.bfloat16)
     return pl.pallas_call(
         functools.partial(coadd_kernel, margin),
-        out_shape=tuple(jax.ShapeDtypeStruct(size, jnp.float32) for size in sizes),
+        out_shape=tuple(jax.ShapeDtypeStruct(*array) for array in zip(sizes, types)),
         in_specs=[
             pl.BlockSpec(memory_space=pltpu.SMEM),
             pl.BlockSpec(memory_space=pltpu.HBM),
@@ -242,6 +244,7 @@
 
 def by_parity(place, first, second):
     even = lax.rem(place, 2) == 0
+    first, second = first.astype(jnp.float32), second.astype(jnp.float32)
     return jnp.where(even, second, first), jnp.where(even, first, second)
 
 
@@ -250,15 +253,15 @@
     edge = first.shape[0]
     lanes = slice(wide - LANES, wide)
     above, below = by_parity(at[1], first[:, lanes], second[:, lanes])
-    out[:edge, :] = inner[:edge, lanes] + above
-    out[edge : tall - edge, :] = inner[edge : tall - edge, lanes]
-    out[tall - edge :, :] = inner[tall - edge :, lanes] + below
+    out[:edge, :] = (inner[:edge, lanes] + above).astype(out.dtype)
+    out[edge : tall - edge, :] = inner[edge : tall - edge, lanes].astype(out.dtype)
+    out[tall - edge :, :] = (inner[tall - edge :, lanes] + below).astype(out.dtype)
 
 
 def add_beside(at, inner, first, second):
     return pl.pallas_call(
         side_kernel,
-        out_shape=jax.ShapeDtypeStruct((inner.shape[0], LANES), jnp.float32),
+        out_shape=jax.ShapeDtypeStruct((inner.shape[0], LANES), jnp.bfloat16),
         in_specs=[pl.BlockSpec(memory_space=pltpu.SMEM)] + [pl.BlockSpec(memory_space=pltpu.VMEM)] * 3,
         out_specs=pl.BlockSpec(memory_space=pltpu.VMEM),
         compiler_params=pltpu.CompilerParams(vmem_limit_bytes=4 << 20),

time: 84.8 us -> 83.6 us (0.986)
  waiting for transfers between devices: 37.1 us -> 36.2 us
    ppermute x4, waiting for transfers between devices: 15.2 us -> 14.2 us  [swap(): return lax.ppermute(value, axis, pairs + [(j, i) for i, j in pairs])]
where the time goes in v5:
time: 83.6 us; the launch traced here: 82.9 us
  waiting for transfers between devices  36.2 us (43%)
  starting transfers between devices  26.8 us (32%)
  Pallas kernels  15.8 us (19%)
  local copies, waits for them, and re-layouts  2.4 us (3%)
  between operations  0.9 us (1%)
    all_to_all x1, waiting for transfers between devices, body(): lax.all_to_all(weighted, BOTH, split_axis=0, concat_axis=0, tiled=True)  21.9 us
    ppermute x4, waiting for transfers between devices, swap(): return lax.ppermute(value, axis, pairs + [(j, i) for i, j in pairs])  14.2 us
    all_to_all x1, starting transfers between devices, body(): lax.all_to_all(weighted, BOTH, split_axis=0, concat_axis=0, tiled=True)  11.3 us
    ppermute x4, starting transfers between devices, swap(): return lax.ppermute(value, axis, pairs + [(j, i) for i, j in pairs])  9.88 us
    pallas_call x1, Pallas kernels, convolve_sum(): pl.pallas_call(functools.partial(coadd_kernel, margin), out_shape=tuple((...  6.77 us
    all_to_all x1, starting transfers between devices, body(): lax.all_to_all(kept, BOTH, split_axis=0, concat_axis=0, tiled=True)  5.63 us
    pallas_call x2, Pallas kernels, pack(): pl.pallas_call(functools.partial(pack_kernel, len(planes)), out_shape=jax...  5.6 us
    unnamed x16, local copies, waits for them, and re-layouts  1.91 us
  transfers between devices with their start and end apart: 6, of which 4 were waited for; matrix products, arithmetic and copies ran while one was open for 2% of the time, Pallas kernels for 14%

profile of v5, /device:TPU:3, one launch (start us, length us, event | category | flops | bytes accessed | tf_op | source)
XLA Modules:
  0.0 82.9 jit_solution(6964214442818210315)
XLA Ops:
  0.6 0.0 copy-start
  0.7 3.0 %pack.2 = bf16[128,16,512]{2,1,0:T(8,128)(2,1)} custom-call(s32[1]{0:T(128)} %bitcast.2.me, s32[8192]{0:T(1024)} %bitcast.10, s32[8192]{0:T(1024)} %valid.3, bf16[64,16,512]{2,1,0:T(8,128)(2,1)} %refs_0_.3, bf16[64,16,512]{2,1,0:T(8,128)(2,1)} %refs_1_.1), custom_call_target="tpu_custom_call" | custom-call | flops 1048576 | bytes 4194304 | tf_op jit(solution)/shard_map/pack/pallas_call | solution.py:66
  3.6 0.0 copy-start.3
  3.6 0.0 copy-start.4
  3.6 0.0 copy-start.5
  3.7 0.0 copy-start.6
  3.7 11.3 %all-to-all-start = ((bf16[128,16,512]{2,1,0:T(8,128)(2,1)}), bf16[128,16,512]{2,1,0:T(8,128)(2,1)}, u32[]{:S(2)}, u32[]{:S(2)}) async-start(bf16[128,16,512]{2,1,0:T(8,128)(2,1)} %pack.2), calls=%async_computation | async-start | bytes 4194304 | tf_op jit(solution)/shard_map/all_to_all | solution.py:317
  15.0 0.0 copy-done.3
  15.0 0.0 copy-start.7
  15.0 0.1 compare_reduce_fusion
  15.1 0.1 eq.43
  15.2 0.0 copy-done.4
  15.2 0.1 slice.7
  15.3 0.1 rev.3
  15.4 0.0 copy-done.5
  15.4 0.1 reshape.141
  15.4 0.1 select_reduce_fusion
  15.6 0.1 add_select_fusion
  15.7 0.1 select_n.53.row_in_patch
  15.8 0.0 copy-done.6
  15.8 0.1 pad.10.clone
  15.9 0.1 pad_maximum_fusion.down_taps
  16.0 0.5 band_tables.1
  16.5 0.0 copy-start.1
  16.5 1.0 %copy-done.1 = bf16[20,256,128]{2,1,0:T(8,128)(2,1)} copy-done((bf16[20,256,128]{2,1,0:T(8,128)(2,1)}, bf16[20,256,128]{2,1,0:T(8,128)(2,1)S(1)}, u32[]{:S(2)}) %copy-start.1) | copy-done | bytes 1310744
  17.6 0.0 copy-start.2
  17.6 0.8 copy-done.2
  18.4 2.6 %pack.3 = bf16[128,16,512]{2,1,0:T(8,128)(2,1)} custom-call(s32[1]{0:T(128)} %bitcast.2.me, s32[8192]{0:T(1024)} %bitcast.11, s32[8192]{0:T(1024)} %valid.3, bf16[64,16,512]{2,1,0:T(8,128)(2,1)} %refs_0_.3), custom_call_target="tpu_custom_call" | custom-call | flops 1048576 | bytes 3145728 | tf_op jit(solution)/shard_map/pack/pallas_call | solution.py:66
  21.0 0.0 copy-done
  21.1 0.0 copy-done.7
  21.1 0.2 convolution_bitcast_fusion
  21.4 21.9 %all-to-all-done.flux_far = bf16[128,16,512]{2,1,0:T(8,128)(2,1)} async-done(((bf16[128,16,512]{2,1,0:T(8,128)(2,1)}), bf16[128,16,512]{2,1,0:T(8,128)(2,1)}, u32[]{:S(2)}, u32[]{:S(2)}) %all-to-all-start) | async-done | bytes 2097184 | tf_op jit(solution)/shard_map/all_to_all | solution.py:317
  43.3 5.6 %all-to-all-start.1 = ((bf16[128,16,512]{2,1,0:T(8,128)(2,1)}), bf16[128,16,512]{2,1,0:T(8,128)(2,1)S(1)}, u32[]{:S(2)}, u32[]{:S(2)}) async-start(bf16[128,16,512]{2,1,0:T(8,128)(2,1)} %pack.3), calls=%async_computation.1 | async-start | bytes 4194304 | tf_op jit(solution)/shard_map/all_to_all | solution.py:342
  48.9 0.1 pad_add_fusion.here.at
  49.0 6.8 %convolve_sum.1 = (f32[64,640]{1,0:T(8,128)S(1)}, bf16[24,640]{1,0:T(8,128)(2,1)S(1)}, bf16[24,640]{1,0:T(8,128)(2,1)S(1)}) custom-call(s32[2]{0:T(128)S(1)} %pad_add_fusion.here.at, bf16[128,16,512]{2,1,0:T(8,128)(2,1)} %all-to-all-done.flux_far, bf16[160,256]{1,0:T(8,128)(2,1)S(1)} %fusion.3.choose, bf16[20,112,64]{2,1,0:T(8,128)(2,1)} %copy-done.2, ...), custom_call_target="tpu_custom_call" | custom-call | flops 734003200 | bytes 2383872 | tf_op jit(solution)/shard_map/convolve_sum/pallas_call | solution.py:191
  55.8 1.5 %collective-permute-start = (bf16[24,640]{1,0:T(8,128)(2,1)S(1)}, bf16[24,640]{1,0:T(8,128)(2,1)S(1)}, u32[]{:S(2)}, u32[]{:S(2)}) collective-permute-start(bf16[24,640]{1,0:T(8,128)(2,1)S(1)} %get-tuple-element.18), channel_id=1, source_target_pairs={{0,1},{2,3},{4,5},{6,7},{8,9},{10,11},{12,13},{14,15},{1,0},{3,2},... | collective-permute-start | bytes 92168 | tf_op jit(solution)/shard_map/ppermute | solution.py:299
  57.3 4.0 %collective-permute-start.1 = (bf16[24,640]{1,0:T(8,128)(2,1)S(1)}, bf16[24,640]{1,0:T(8,128)(2,1)S(1)}, u32[]{:S(2)}, u32[]{:S(2)}) collective-permute-start(bf16[24,640]{1,0:T(8,128)(2,1)S(1)} %get-tuple-element.19), channel_id=1, source_target_pairs={{1,2},{3,4},{5,6},{7,8},{9,10},{11,12},{13,14},{2,1},{4,3},{6,5},{... | collective-permute-start | bytes 92168 | tf_op jit(solution)/shard_map/ppermute | solution.py:299
  61.2 8.1 %collective-permute-done.first = bf16[24,640]{1,0:T(8,128)(2,1)S(1)} collective-permute-done((bf16[24,640]{1,0:T(8,128)(2,1)S(1)}, bf16[24,640]{1,0:T(8,128)(2,1)S(1)}, u32[]{:S(2)}, u32[]{:S(2)}) %collective-permute-start) | collective-permute-done | bytes 30752 | tf_op jit(solution)/shard_map/ppermute | solution.py:299
  69.3 6.0 %collective-permute-done.1.second = bf16[24,640]{1,0:T(8,128)(2,1)S(1)} collective-permute-done((bf16[24,640]{1,0:T(8,128)(2,1)S(1)}, bf16[24,640]{1,0:T(8,128)(2,1)S(1)}, u32[]{:S(2)}, u32[]{:S(2)}) %collective-permute-start.1) | collective-permute-done | bytes 30752 | tf_op jit(solution)/shard_map/ppermute | solution.py:299
  75.3 0.6 add_beside.1
  75.8 4.4 %collective-permute-start.3 = (bf16[64,128]{1,0:T(8,128)(2,1)S(1)}, bf16[64,128]{1,0:T(8,128)(2,1)S(1)}, u32[]{:S(2)}, u32[]{:S(2)}) collective-permute-start(bf16[64,128]{1,0:T(8,128)(2,1)S(1)} %add_beside.1), channel_id=1, source_target_pairs={{16,32},{48,64},{80,96},{32,16},{64,48},{96,80},{17,33},{49,65},{8... | collective-permute-start | bytes 49160 | tf_op jit(solution)/shard_map/ppermute | solution.py:299
  80.2 0.1 collective-permute-start.2
  80.3 0.0 all-to-all-done.1.kept
  80.3 1.1 %place_weights.1 = f32[64,512]{1,0:T(8,128)} custom-call(s32[1,2048]{1,0:T(1,128)S(1)} %select_n.53.row_in_patch, bf16[128,16,512]{2,1,0:T(8,128)(2,1)S(1)} %all-to-all-done.1.kept), custom_call_target="tpu_custom_call" | custom-call | flops 134217728 | bytes 2097152 | tf_op jit(solution)/shard_map/place_weights/pallas_call | solution.py:230
  81.5 0.2 collective-permute-done.3.far
  81.6 0.0 collective-permute-done.2.near
  81.7 1.2 %finish.1 = f32[64,512]{1,0:T(8,128)} custom-call(s32[2]{0:T(128)S(1)} %pad_add_fusion.here.at, f32[64,640]{1,0:T(8,128)S(1)} %get-tuple-element.17.inner, bf16[24,640]{1,0:T(8,128)(2,1)S(1)} %collective-permute-done.first, bf16[24,640]{1,0:T(8,128)(2,1)S(1)} %collective-permute-done.1.second, bf16[64,128]{1,0:T(8,128)(2,1)S(1)} %collective-permute-done.2.near, ...), custom_call_target="tpu_custom_call" | custom-call | tf_op jit(solution)/shard_map/finish/pallas_call | solution.py:287
  (8 shorter events, 0.1 us)
Async XLA Ops:
  0.6 20.4 %copy-start = (f32[64,20]{0,1:T(8,128)S(1)}, f32[64,20]{0,1:T(8,128)}, u32[]{:S(2)}) copy-start(f32[64,20]{0,1:T(8,128)} %param.15) | copy-start | bytes 15364
  3.6 11.4 %copy-start.3 = (s32[8192,1]{0,1:T(1,128)S(1)}, s32[8192,1]{0,1:T(1,128)}, u32[]{:S(2)}) copy-start(s32[8192,1]{0,1:T(1,128)} %param.11) | copy-start | bytes 98308
  3.6 11.6 %copy-start.4 = (f32[20,41]{1,0:T(8,128)S(1)}, f32[20,41]{1,0:T(8,128)}, u32[]{:S(2)}) copy-start(f32[20,41]{1,0:T(8,128)} %param.17) | copy-start | bytes 9844
  3.6 11.7 %copy-start.5 = (s32[8192]{0:T(1024)S(1)}, s32[8192]{0:T(1024)}, u32[]{:S(2)}) copy-start(s32[8192]{0:T(1024)} %param.12) | copy-start | bytes 98308
  3.7 12.1 %copy-start.6 = (f32[20,41]{1,0:T(8,128)S(1)}, f32[20,41]{1,0:T(8,128)}, u32[]{:S(2)}) copy-start(f32[20,41]{1,0:T(8,128)} %param.16) | copy-start | bytes 9844
  3.7 39.6 %all-to-all-start = ((bf16[128,16,512]{2,1,0:T(8,128)(2,1)}), bf16[128,16,512]{2,1,0:T(8,128)(2,1)}, u32[]{:S(2)}, u32[]{:S(2)}) async-start(bf16[128,16,512]{2,1,0:T(8,128)(2,1)} %pack.2), calls=%async_computation | async-start | bytes 4194304 | tf_op jit(solution)/shard_map/all_to_all | solution.py:317
  15.0 6.1 %copy-start.7 = (s32[128]{0:T(128)S(1)}, s32[128]{0:T(128)}, u32[]{:S(2)}) copy-start(s32[128]{0:T(128)} %param.14) | copy-start | bytes 1540
  16.5 1.1 %copy-start.1 = (bf16[20,256,128]{2,1,0:T(8,128)(2,1)}, bf16[20,256,128]{2,1,0:T(8,128)(2,1)S(1)}, u32[]{:S(2)}) copy-start(bf16[20,256,128]{2,1,0:T(8,128)(2,1)S(1)} %get-tuple-element.16.across_far) | copy-start | bytes 3932164
  17.6 0.8 copy-start.2
  43.3 37.0 %all-to-all-start.1 = ((bf16[128,16,512]{2,1,0:T(8,128)(2,1)}), bf16[128,16,512]{2,1,0:T(8,128)(2,1)S(1)}, u32[]{:S(2)}, u32[]{:S(2)}) async-start(bf16[128,16,512]{2,1,0:T(8,128)(2,1)} %pack.3), calls=%async_computation.1 | async-start | bytes 4194304 | tf_op jit(solution)/shard_map/all_to_all | solution.py:342
  55.8 13.5 %collective-permute-start = (bf16[24,640]{1,0:T(8,128)(2,1)S(1)}, bf16[24,640]{1,0:T(8,128)(2,1)S(1)}, u32[]{:S(2)}, u32[]{:S(2)}) collective-permute-start(bf16[24,640]{1,0:T(8,128)(2,1)S(1)} %get-tuple-element.18), channel_id=1, source_target_pairs={{0,1},{2,3},{4,5},{6,7},{8,9},{10,11},{12,13},{14,15},{1,0},{3,2},... | collective-permute-start | bytes 92168 | tf_op jit(solution)/shard_map/ppermute | solution.py:299
  57.3 18.0 %collective-permute-start.1 = (bf16[24,640]{1,0:T(8,128)(2,1)S(1)}, bf16[24,640]{1,0:T(8,128)(2,1)S(1)}, u32[]{:S(2)}, u32[]{:S(2)}) collective-permute-start(bf16[24,640]{1,0:T(8,128)(2,1)S(1)} %get-tuple-element.19), channel_id=1, source_target_pairs={{1,2},{3,4},{5,6},{7,8},{9,10},{11,12},{13,14},{2,1},{4,3},{6,5},{... | collective-permute-start | bytes 92168 | tf_op jit(solution)/shard_map/ppermute | solution.py:299
  75.8 5.8 %collective-permute-start.3 = (bf16[64,128]{1,0:T(8,128)(2,1)S(1)}, bf16[64,128]{1,0:T(8,128)(2,1)S(1)}, u32[]{:S(2)}, u32[]{:S(2)}) collective-permute-start(bf16[64,128]{1,0:T(8,128)(2,1)S(1)} %add_beside.1), channel_id=1, source_target_pairs={{16,32},{48,64},{80,96},{32,16},{64,48},{96,80},{17,33},{49,65},{8... | collective-permute-start | bytes 49160 | tf_op jit(solution)/shard_map/ppermute | solution.py:299
  80.2 1.4 %collective-permute-start.2 = (bf16[64,128]{1,0:T(8,128)(2,1)S(1)}, bf16[64,128]{1,0:T(8,128)(2,1)S(1)}, u32[]{:S(2)}, u32[]{:S(2)}) collective-permute-start(bf16[64,128]{1,0:T(8,128)(2,1)S(1)} %add_beside.1), channel_id=1, source_target_pairs={{0,16},{32,48},{64,80},{96,112},{16,0},{48,32},{80,64},{112,96},{1... | collective-permute-start | bytes 49160 | tf_op jit(solution)/shard_map/ppermute | solution.py:299

commit v6 on v5

--- a/solution.py
+++ b/solution.py
@@ -12,7 +12,8 @@
 BOTH = ("skyx", "skyy")
 
 
-def pack_kernel(planes, me, patch_of, valid, *refs):
+def pack_kernel(planes, patch_of, valid, *refs):
+    me = lax.axis_index(BOTH)
     sources, refs = refs[:planes], refs[planes:]
     out, *rooms, packed, targets, usable, arrived, noted, sent = refs
     blocks = rooms[0].shape[0]
@@ -25,7 +26,7 @@
 
     listed = targets.shape[0]
     devices_listed = listed // blocks
-    some = pl.ds(pl.multiple_of(me[0] // devices_listed * listed, listed), listed)
+    some = pl.ds(pl.multiple_of(me // devices_listed * listed, listed), listed)
     notes = [
         pltpu.make_async_copy(patch_of.at[some], targets, noted.at[0]),
         pltpu.make_async_copy(valid.at[some], usable, noted.at[1]),
@@ -39,7 +40,7 @@
     packed[...] = jnp.zeros_like(packed)
     for note in notes:
         note.wait()
-    first = me[0] % devices_listed * blocks
+    first = me % devices_listed * blocks
     for chunk in range(chunks):
         for index in range(planes):
             fetch(index, chunk).wait()
@@ -60,13 +61,13 @@
         copy.wait()
 
 
-def pack(devices, me, patch_of, valid, *planes):
+def pack(devices, patch_of, valid, *planes):
     blocks, rows, width = planes[0].shape
     chunks, pieces = 2, 2
     return pl.pallas_call(
         functools.partial(pack_kernel, len(planes)),
         out_shape=jax.ShapeDtypeStruct((devices, rows, width), jnp.bfloat16),
-        in_specs=[pl.BlockSpec(memory_space=pltpu.SMEM)] + [pl.BlockSpec(memory_space=pl.ANY)] * (2 + len(planes)),
+        in_specs=[pl.BlockSpec(memory_space=pl.ANY)] * (2 + len(planes)),
         out_specs=pl.BlockSpec(memory_space=pl.ANY),
         scratch_shapes=[pltpu.VMEM((blocks, rows, width), jnp.bfloat16) for _ in planes]
         + [
@@ -84,7 +85,7 @@
         ),
         compiler_params=pltpu.CompilerParams(vmem_limit_bytes=63 << 20),
         name="pack",
-    )(me, patch_of, valid, *planes)
+    )(patch_of, valid, *planes)
 
 
 def table_kernel(across_taps, down_taps, row_at, across, down):
@@ -123,7 +124,7 @@
 
 
 def coadd_kernel(
-    margin, here, flux_far, choose, down_far, across_far, inner, first, second,
+    margin, flux_far, choose, down_far, across_far, inner, first, second,
     flux, down, across, wide, channels, mixed, arrived,
 ):
     sources, rows, width = flux.shape
@@ -175,12 +176,12 @@
     whole = pltpu.roll(whole, tiles * LANES - margin, 1)
     inner[...] = whole[edge : edge + tall]
     top, bottom = whole[:edge], whole[edge + tall :]
-    even = lax.rem(here[1], 2) == 0
+    even = lax.rem(lax.axis_index("skyy"), 2) == 0
     first[...] = jnp.where(even, bottom, top).astype(first.dtype)
     second[...] = jnp.where(even, top, bottom).astype(second.dtype)
 
 
-def convolve_sum(margin, at, flux, choose, down, across):
+def convolve_sum(margin, flux, choose, down, across):
     sources, rows, width = flux.shape
     count, ext, _ = down.shape
     tiles = width // LANES + 1
@@ -192,7 +193,6 @@
         functools.partial(coadd_kernel, margin),
         out_shape=tuple(jax.ShapeDtypeStruct(*array) for array in zip(sizes, types)),
         in_specs=[
-            pl.BlockSpec(memory_space=pltpu.SMEM),
             pl.BlockSpec(memory_space=pltpu.HBM),
             pl.BlockSpec(memory_space=pltpu.VMEM),
             pl.BlockSpec(memory_space=pltpu.HBM),
@@ -215,7 +215,7 @@
             transcendentals=0,
         ),
         name="convolve_sum",
-    )(at, flux, choose, down, across)
+    )(flux, choose, down, across)
 
 
 def weight_kernel(row_in_patch, kept, out):
@@ -242,56 +242,56 @@
     )(row_in_patch, kept)
 
 
-def by_parity(place, first, second):
-    even = lax.rem(place, 2) == 0
+def by_parity(axis, first, second):
+    even = lax.rem(lax.axis_index(axis), 2) == 0
     first, second = first.astype(jnp.float32), second.astype(jnp.float32)
     return jnp.where(even, second, first), jnp.where(even, first, second)
 
 
-def side_kernel(at, inner, first, second, out):
+def side_kernel(inner, first, second, out):
     tall, wide = inner.shape
     edge = first.shape[0]
     lanes = slice(wide - LANES, wide)
-    above, below = by_parity(at[1], first[:, lanes], second[:, lanes])
+    above, below = by_parity("skyy", first[:, lanes], second[:, lanes])
     out[:edge, :] = (inner[:edge, lanes] + above).astype(out.dtype)
     out[edge : tall - edge, :] = inner[edge : tall - edge, lanes].astype(out.dtype)
     out[tall - edge :, :] = (inner[tall - edge :, lanes] + below).astype(out.dtype)
 
 
-def add_beside(at, inner, first, second):
+def add_beside(inner, first, second):
     return pl.pallas_call(
         side_kernel,
         out_shape=jax.ShapeDtypeStruct((inner.shape[0], LANES), jnp.bfloat16),
-        in_specs=[pl.BlockSpec(memory_space=pltpu.SMEM)] + [pl.BlockSpec(memory_space=pltpu.VMEM)] * 3,
+        in_specs=[pl.BlockSpec(memory_space=pltpu.VMEM)] * 3,
         out_specs=pl.BlockSpec(memory_space=pltpu.VMEM),
         compiler_params=pltpu.CompilerParams(vmem_limit_bytes=4 << 20),
         name="add_beside",
-    )(at, inner, first, second)
-
-
-def finish_kernel(margin, at, inner, first, second, near, far, out):
+    )(inner, first, second)
+
+
+def finish_kernel(margin, inner, first, second, near, far, out):
     tall, width = out.shape
     edge = first.shape[0]
-    above, below = by_parity(at[1], first[:, :width], second[:, :width])
+    above, below = by_parity("skyy", first[:, :width], second[:, :width])
     out[:edge, :] = inner[:edge, :width] + above
     out[edge : tall - edge, :] = inner[edge : tall - edge, :width]
     out[tall - edge :, :] = inner[tall - edge :, :width] + below
     lane = lax.broadcasted_iota(jnp.int32, (1, LANES), 1)
-    left, right = by_parity(at[0], near[...], far[...])
+    left, right = by_parity("skyx", near[...], far[...])
     out[:, :LANES] += jnp.where(lane < margin, left, 0.0)
     out[:, width - LANES :] += jnp.where(lane >= LANES - margin, right, 0.0)
 
 
-def finish(margin, at, inner, first, second, near, far):
+def finish(margin, inner, first, second, near, far):
     tall, wide = inner.shape
     return pl.pallas_call(
         functools.partial(finish_kernel, margin),
         out_shape=jax.ShapeDtypeStruct((tall, wide - LANES), jnp.float32),
-        in_specs=[pl.BlockSpec(memory_space=pltpu.SMEM)] + [pl.BlockSpec(memory_space=pltpu.VMEM)] * 5,
+        in_specs=[pl.BlockSpec(memory_space=pltpu.VMEM)] * 5,
         out_specs=pl.BlockSpec(memory_space=pltpu.VMEM),
         compiler_params=pltpu.CompilerParams(vmem_limit_bytes=4 << 20),
         name="finish",
-    )(at, inner, first, second, near, far)
+    )(inner, first, second, near, far)
 
 
 def swap(value, axis, first):
@@ -311,11 +311,10 @@
     my_column, my_line = lax.axis_index("skyx"), lax.axis_index("skyy")
     my_patch = my_column * lines + my_line
     patches = patch_of[:, 0]
-    me = my_patch.astype(jnp.int32).reshape(1)
-
-    weighted = pack(devices, me, patches, valid, inverse_var, image)
+
+    weighted = pack(devices, patches, valid, inverse_var, image)
     weighted_in = lax.all_to_all(weighted, BOTH, split_axis=0, concat_axis=0, tiled=True)
-    kept = pack(devices, me, patches, valid, inverse_var)
+    kept = pack(devices, patches, valid, inverse_var)
 
     choose = (
         coef_index[:, None] == jnp.arange(coef_table.shape[0], dtype=jnp.int32)[None, :]
@@ -340,14 +339,13 @@
     row_in_patch = row_in_patch.reshape(1, devices * row_count)
     kept, table, down, across, row_in_patch = lax.optimization_barrier((kept, table, down, across, row_in_patch))
     kept_in = lax.all_to_all(kept, BOTH, split_axis=0, concat_axis=0, tiled=True)
-    at = jnp.stack([my_column, my_line]).astype(jnp.int32)
     down, across = (pltpu.with_memory_space_constraint(x, pltpu.HBM) for x in (down, across))
-    inner, first, second = convolve_sum(margin, at, weighted_in, table, down, across)
+    inner, first, second = convolve_sum(margin, weighted_in, table, down, across)
     first, second = swap(first, "skyy", 0), swap(second, "skyy", 1)
-    side = add_beside(at, inner, first, second)
+    side = add_beside(inner, first, second)
     near, far = swap(side, "skyx", 0), swap(side, "skyx", 1)
     weight_sum = place_weights(row_in_patch, kept_in)
-    coadd = finish(margin, at, inner, first, second, near, far)
+    coadd = finish(margin, inner, first, second, near, far)
     return (coadd, weight_sum)
 
 

time: 83.6 us -> 82.6 us (0.988)
  Pallas kernels: 15.8 us -> 14.2 us
  transfers between devices with their start and end apart: 6 -> 6, of which waited for: 4 -> 4; matrix products, arithmetic and copies ran while one was open for 2% -> 1% of each run, Pallas kernels for 14% -> 13%
where the time goes in v6:
time: 82.6 us; the launch traced here: 81.8 us
  waiting for transfers between devices  36.8 us (45%)
  starting transfers between devices  26.8 us (32%)
  Pallas kernels  14.2 us (17%)
  local copies, waits for them, and re-layouts  2.4 us (3%)
  between operations  0.9 us (1%)
    all_to_all x1, waiting for transfers between devices, body(): lax.all_to_all(weighted, BOTH, split_axis=0, concat_axis=0, tiled=True)  21.9 us
    ppermute x4, waiting for transfers between devices, swap(): return lax.ppermute(value, axis, pairs + [(j, i) for i, j in pairs])  14.9 us
    all_to_all x1, starting transfers between devices, body(): lax.all_to_all(weighted, BOTH, split_axis=0, concat_axis=0, tiled=True)  11.3 us
    ppermute x4, starting transfers between devices, swap(): return lax.ppermute(value, axis, pairs + [(j, i) for i, j in pairs])  9.88 us
    pallas_call x1, Pallas kernels, convolve_sum(): pl.pallas_call(functools.partial(coadd_kernel, margin), out_shape=tuple((...  6.23 us
    all_to_all x1, starting transfers between devices, body(): lax.all_to_all(kept, BOTH, split_axis=0, concat_axis=0, tiled=True)  5.63 us
    pallas_call x2, Pallas kernels, pack(): pl.pallas_call(functools.partial(pack_kernel, len(planes)), out_shape=jax...  5.59 us
    unnamed x16, local copies, waits for them, and re-layouts  1.91 us
  transfers between devices with their start and end apart: 6, of which 4 were waited for; matrix products, arithmetic and copies ran while one was open for 1% of the time, Pallas kernels for 13%

profile of v6, /device:TPU:3, one launch (start us, length us, event | category | flops | bytes accessed | tf_op | source)
XLA Modules:
  0.0 81.8 jit_solution(1026703596547019620)
XLA Ops:
  0.6 0.0 copy-start
  0.6 3.0 %pack.2 = bf16[128,16,512]{2,1,0:T(8,128)(2,1)} custom-call(s32[8192]{0:T(1024)} %bitcast.7, s32[8192]{0:T(1024)} %valid.3, bf16[64,16,512]{2,1,0:T(8,128)(2,1)} %refs_0_.3, bf16[64,16,512]{2,1,0:T(8,128)(2,1)} %refs_1_.1), custom_call_target="tpu_custom_call" | custom-call | flops 1048576 | bytes 4194304 | tf_op jit(solution)/shard_map/pack/pallas_call | solution.py:67
  3.6 0.0 copy-start.3
  3.6 0.0 copy-start.4
  3.6 0.0 copy-start.5
  3.7 0.0 copy-start.6
  3.7 11.3 %all-to-all-start = ((bf16[128,16,512]{2,1,0:T(8,128)(2,1)}), bf16[128,16,512]{2,1,0:T(8,128)(2,1)}, u32[]{:S(2)}, u32[]{:S(2)}) async-start(bf16[128,16,512]{2,1,0:T(8,128)(2,1)} %pack.2), calls=%async_computation | async-start | bytes 4194304 | tf_op jit(solution)/shard_map/all_to_all | solution.py:316
  15.0 0.0 copy-start.7
  15.0 0.0 copy-done.3
  15.0 0.1 compare_reduce_fusion
  15.1 0.1 eq.43
  15.2 0.0 copy-done.4
  15.2 0.1 slice.7
  15.3 0.1 rev.3
  15.4 0.0 copy-done.5
  15.4 0.1 reshape.137
  15.4 0.1 select_reduce_fusion
  15.6 0.1 add_select_fusion
  15.7 0.1 select_n.53.row_in_patch
  15.8 0.0 copy-done.6
  15.8 0.1 pad.10.clone
  15.9 0.1 pad_maximum_fusion.down_taps
  16.0 0.5 band_tables.1
  16.5 0.0 copy-start.1
  16.5 1.0 %copy-done.1 = bf16[20,256,128]{2,1,0:T(8,128)(2,1)} copy-done((bf16[20,256,128]{2,1,0:T(8,128)(2,1)}, bf16[20,256,128]{2,1,0:T(8,128)(2,1)S(1)}, u32[]{:S(2)}) %copy-start.1) | copy-done | bytes 1310744
  17.6 0.0 copy-start.2
  17.6 0.8 %copy-done.2 = bf16[20,112,64]{2,1,0:T(8,128)(2,1)} copy-done((bf16[20,112,64]{2,1,0:T(8,128)(2,1)}, bf16[20,112,64]{2,1,0:T(8,128)(2,1)S(1)}, u32[]{:S(2)}) %copy-start.2) | copy-done | bytes 286744
  18.4 2.6 %pack.3 = bf16[128,16,512]{2,1,0:T(8,128)(2,1)} custom-call(s32[8192]{0:T(1024)} %bitcast.8, s32[8192]{0:T(1024)} %valid.3, bf16[64,16,512]{2,1,0:T(8,128)(2,1)} %refs_0_.3), custom_call_target="tpu_custom_call" | custom-call | flops 1048576 | bytes 3145728 | tf_op jit(solution)/shard_map/pack/pallas_call | solution.py:67
  21.0 0.0 copy-done
  21.0 0.0 copy-done.7
  21.1 0.2 convolution_bitcast_fusion
  21.4 21.9 %all-to-all-done.flux_far = bf16[128,16,512]{2,1,0:T(8,128)(2,1)} async-done(((bf16[128,16,512]{2,1,0:T(8,128)(2,1)}), bf16[128,16,512]{2,1,0:T(8,128)(2,1)}, u32[]{:S(2)}, u32[]{:S(2)}) %all-to-all-start) | async-done | bytes 2097184 | tf_op jit(solution)/shard_map/all_to_all | solution.py:316
  43.3 5.6 %all-to-all-start.1 = ((bf16[128,16,512]{2,1,0:T(8,128)(2,1)}), bf16[128,16,512]{2,1,0:T(8,128)(2,1)S(1)}, u32[]{:S(2)}, u32[]{:S(2)}) async-start(bf16[128,16,512]{2,1,0:T(8,128)(2,1)} %pack.3), calls=%async_computation.1 | async-start | bytes 4194304 | tf_op jit(solution)/shard_map/all_to_all | solution.py:341
  48.9 6.2 %convolve_sum.1 = (f32[64,640]{1,0:T(8,128)S(1)}, bf16[24,640]{1,0:T(8,128)(2,1)S(1)}, bf16[24,640]{1,0:T(8,128)(2,1)S(1)}) custom-call(bf16[128,16,512]{2,1,0:T(8,128)(2,1)} %all-to-all-done.flux_far, bf16[160,256]{1,0:T(8,128)(2,1)S(1)} %fusion.3.choose, bf16[20,112,64]{2,1,0:T(8,128)(2,1)} %copy-done.2, bf16[20,256,128]{2,1,0:T(8,128)(2,1)} %copy-done.1), custom_call_target="tpu_custom_call" | custom-call | flops 734003200 | bytes 2383872 | tf_op jit(solution)/shard_map/convolve_sum/pallas_call | solution.py:192
  55.2 1.5 %collective-permute-start = (bf16[24,640]{1,0:T(8,128)(2,1)S(1)}, bf16[24,640]{1,0:T(8,128)(2,1)S(1)}, u32[]{:S(2)}, u32[]{:S(2)}) collective-permute-start(bf16[24,640]{1,0:T(8,128)(2,1)S(1)} %get-tuple-element.18), channel_id=1, source_target_pairs={{0,1},{2,3},{4,5},{6,7},{8,9},{10,11},{12,13},{14,15},{1,0},{3,2},... | collective-permute-start | bytes 92168 | tf_op jit(solution)/shard_map/ppermute | solution.py:299
  56.6 4.0 %collective-permute-start.1 = (bf16[24,640]{1,0:T(8,128)(2,1)S(1)}, bf16[24,640]{1,0:T(8,128)(2,1)S(1)}, u32[]{:S(2)}, u32[]{:S(2)}) collective-permute-start(bf16[24,640]{1,0:T(8,128)(2,1)S(1)} %get-tuple-element.19), channel_id=1, source_target_pairs={{1,2},{3,4},{5,6},{7,8},{9,10},{11,12},{13,14},{2,1},{4,3},{6,5},{... | collective-permute-start | bytes 92168 | tf_op jit(solution)/shard_map/ppermute | solution.py:299
  60.6 3.9 %collective-permute-done.first = bf16[24,640]{1,0:T(8,128)(2,1)S(1)} collective-permute-done((bf16[24,640]{1,0:T(8,128)(2,1)S(1)}, bf16[24,640]{1,0:T(8,128)(2,1)S(1)}, u32[]{:S(2)}, u32[]{:S(2)}) %collective-permute-start) | collective-permute-done | bytes 30752 | tf_op jit(solution)/shard_map/ppermute | solution.py:299
  64.5 10.8 %collective-permute-done.1.second = bf16[24,640]{1,0:T(8,128)(2,1)S(1)} collective-permute-done((bf16[24,640]{1,0:T(8,128)(2,1)S(1)}, bf16[24,640]{1,0:T(8,128)(2,1)S(1)}, u32[]{:S(2)}, u32[]{:S(2)}) %collective-permute-start.1) | collective-permute-done | bytes 30752 | tf_op jit(solution)/shard_map/ppermute | solution.py:299
  75.3 4.4 %collective-permute-start.3 = (bf16[64,128]{1,0:T(8,128)(2,1)S(1)}, bf16[64,128]{1,0:T(8,128)(2,1)S(1)}, u32[]{:S(2)}, u32[]{:S(2)}) collective-permute-start(bf16[64,128]{1,0:T(8,128)(2,1)S(1)} %add_beside.1), channel_id=1, source_target_pairs={{16,32},{48,64},{80,96},{32,16},{64,48},{96,80},{17,33},{49,65},{8... | collective-permute-start | bytes 49160 | tf_op jit(solution)/shard_map/ppermute | solution.py:299
  79.7 0.1 collective-permute-start.2
  79.8 0.0 all-to-all-done.1.kept
  79.8 1.1 %place_weights.1 = f32[64,512]{1,0:T(8,128)} custom-call(s32[1,2048]{1,0:T(1,128)S(1)} %select_n.53.row_in_patch, bf16[128,16,512]{2,1,0:T(8,128)(2,1)S(1)} %all-to-all-done.1.kept), custom_call_target="tpu_custom_call" | custom-call | flops 134217728 | bytes 2097152 | tf_op jit(solution)/shard_map/place_weights/pallas_call | solution.py:230
  80.9 0.2 collective-permute-done.3.far
  81.1 0.0 collective-permute-done.2.near
  81.1 0.7 finish.1
  (9 shorter events, 0.1 us)
Async XLA Ops:
  0.6 20.4 %copy-start = (f32[64,20]{0,1:T(8,128)S(1)}, f32[64,20]{0,1:T(8,128)}, u32[]{:S(2)}) copy-start(f32[64,20]{0,1:T(8,128)} %param.15) | copy-start | bytes 15364
  3.6 11.4 %copy-start.3 = (s32[8192,1]{0,1:T(1,128)S(1)}, s32[8192,1]{0,1:T(1,128)}, u32[]{:S(2)}) copy-start(s32[8192,1]{0,1:T(1,128)} %param.11) | copy-start | bytes 98308
  3.6 11.6 %copy-start.4 = (f32[20,41]{1,0:T(8,128)S(1)}, f32[20,41]{1,0:T(8,128)}, u32[]{:S(2)}) copy-start(f32[20,41]{1,0:T(8,128)} %param.17) | copy-start | bytes 9844
  3.6 11.7 %copy-start.5 = (s32[8192]{0:T(1024)S(1)}, s32[8192]{0:T(1024)}, u32[]{:S(2)}) copy-start(s32[8192]{0:T(1024)} %param.12) | copy-start | bytes 98308
  3.7 12.1 %copy-start.6 = (f32[20,41]{1,0:T(8,128)S(1)}, f32[20,41]{1,0:T(8,128)}, u32[]{:S(2)}) copy-start(f32[20,41]{1,0:T(8,128)} %param.16) | copy-start | bytes 9844
  3.7 39.6 %all-to-all-start = ((bf16[128,16,512]{2,1,0:T(8,128)(2,1)}), bf16[128,16,512]{2,1,0:T(8,128)(2,1)}, u32[]{:S(2)}, u32[]{:S(2)}) async-start(bf16[128,16,512]{2,1,0:T(8,128)(2,1)} %pack.2), calls=%async_computation | async-start | bytes 4194304 | tf_op jit(solution)/shard_map/all_to_all | solution.py:316
  15.0 6.1 %copy-start.7 = (s32[128]{0:T(128)S(1)}, s32[128]{0:T(128)}, u32[]{:S(2)}) copy-start(s32[128]{0:T(128)} %param.14) | copy-start | bytes 1540
  16.5 1.1 %copy-start.1 = (bf16[20,256,128]{2,1,0:T(8,128)(2,1)}, bf16[20,256,128]{2,1,0:T(8,128)(2,1)S(1)}, u32[]{:S(2)}) copy-start(bf16[20,256,128]{2,1,0:T(8,128)(2,1)S(1)} %get-tuple-element.16.across_far) | copy-start | bytes 3932164
  17.6 0.8 %copy-start.2 = (bf16[20,112,64]{2,1,0:T(8,128)(2,1)}, bf16[20,112,64]{2,1,0:T(8,128)(2,1)S(1)}, u32[]{:S(2)}) copy-start(bf16[20,112,64]{2,1,0:T(8,128)(2,1)S(1)} %get-tuple-element.15.down_far) | copy-start | bytes 860164
  43.3 36.5 %all-to-all-start.1 = ((bf16[128,16,512]{2,1,0:T(8,128)(2,1)}), bf16[128,16,512]{2,1,0:T(8,128)(2,1)S(1)}, u32[]{:S(2)}, u32[]{:S(2)}) async-start(bf16[128,16,512]{2,1,0:T(8,128)(2,1)} %pack.3), calls=%async_computation.1 | async-start | bytes 4194304 | tf_op jit(solution)/shard_map/all_to_all | solution.py:341
  55.2 9.3 %collective-permute-start = (bf16[24,640]{1,0:T(8,128)(2,1)S(1)}, bf16[24,640]{1,0:T(8,128)(2,1)S(1)}, u32[]{:S(2)}, u32[]{:S(2)}) collective-permute-start(bf16[24,640]{1,0:T(8,128)(2,1)S(1)} %get-tuple-element.18), channel_id=1, source_target_pairs={{0,1},{2,3},{4,5},{6,7},{8,9},{10,11},{12,13},{14,15},{1,0},{3,2},... | collective-permute-start | bytes 92168 | tf_op jit(solution)/shard_map/ppermute | solution.py:299
  56.6 18.6 %collective-permute-start.1 = (bf16[24,640]{1,0:T(8,128)(2,1)S(1)}, bf16[24,640]{1,0:T(8,128)(2,1)S(1)}, u32[]{:S(2)}, u32[]{:S(2)}) collective-permute-start(bf16[24,640]{1,0:T(8,128)(2,1)S(1)} %get-tuple-element.19), channel_id=1, source_target_pairs={{1,2},{3,4},{5,6},{7,8},{9,10},{11,12},{13,14},{2,1},{4,3},{6,5},{... | collective-permute-start | bytes 92168 | tf_op jit(solution)/shard_map/ppermute | solution.py:299
  75.3 5.8 %collective-permute-start.3 = (bf16[64,128]{1,0:T(8,128)(2,1)S(1)}, bf16[64,128]{1,0:T(8,128)(2,1)S(1)}, u32[]{:S(2)}, u32[]{:S(2)}) collective-permute-start(bf16[64,128]{1,0:T(8,128)(2,1)S(1)} %add_beside.1), channel_id=1, source_target_pairs={{16,32},{48,64},{80,96},{32,16},{64,48},{96,80},{17,33},{49,65},{8... | collective-permute-start | bytes 49160 | tf_op jit(solution)/shard_map/ppermute | solution.py:299
  79.7 1.4 %collective-permute-start.2 = (bf16[64,128]{1,0:T(8,128)(2,1)S(1)}, bf16[64,128]{1,0:T(8,128)(2,1)S(1)}, u32[]{:S(2)}, u32[]{:S(2)}) collective-permute-start(bf16[64,128]{1,0:T(8,128)(2,1)S(1)} %add_beside.1), channel_id=1, source_target_pairs={{0,16},{32,48},{64,80},{96,112},{16,0},{48,32},{80,64},{112,96},{1... | collective-permute-start | bytes 49160 | tf_op jit(solution)/shard_map/ppermute | solution.py:299

commit v7 on v6

--- a/solution.py
+++ b/solution.py
@@ -218,14 +218,12 @@
     )(flux, choose, down, across)
 
 
-def weight_kernel(row_in_patch, kept, out):
+def weight_kernel(chosen, kept, out):
     sources, rows, width = kept.shape
-    line = lax.broadcasted_iota(jnp.int32, (out.shape[0], sources * rows), 0)
-    chosen = (line == row_in_patch[...]).astype(jnp.bfloat16)
-    out[...] = jnp.dot(chosen, kept[...].reshape(sources * rows, width), preferred_element_type=jnp.float32)
-
-
-def place_weights(row_in_patch, kept):
+    out[...] = jnp.dot(chosen[...], kept[...].reshape(sources * rows, width), preferred_element_type=jnp.float32)
+
+
+def place_weights(chosen, kept):
     sources, rows, width = kept.shape
     return pl.pallas_call(
         weight_kernel,
@@ -239,7 +237,7 @@
             transcendentals=0,
         ),
         name="place_weights",
-    )(row_in_patch, kept)
+    )(chosen, kept)
 
 
 def by_parity(axis, first, second):
@@ -337,14 +335,15 @@
     received_rows = jnp.arange(row_count, dtype=jnp.int32)[None, :]
     row_in_patch = jnp.where(slot[:, None] >= 0, slot[:, None] * row_count + received_rows, -1)
     row_in_patch = row_in_patch.reshape(1, devices * row_count)
-    kept, table, down, across, row_in_patch = lax.optimization_barrier((kept, table, down, across, row_in_patch))
+    chosen = (places[:, None] == row_in_patch).astype(jnp.bfloat16)
+    kept, table, down, across, chosen = lax.optimization_barrier((kept, table, down, across, chosen))
     kept_in = lax.all_to_all(kept, BOTH, split_axis=0, concat_axis=0, tiled=True)
     down, across = (pltpu.with_memory_space_constraint(x, pltpu.HBM) for x in (down, across))
     inner, first, second = convolve_sum(margin, weighted_in, table, down, across)
     first, second = swap(first, "skyy", 0), swap(second, "skyy", 1)
     side = add_beside(inner, first, second)
     near, far = swap(side, "skyx", 0), swap(side, "skyx", 1)
-    weight_sum = place_weights(row_in_patch, kept_in)
+    weight_sum = place_weights(chosen, kept_in)
     coadd = finish(margin, inner, first, second, near, far)
     return (coadd, weight_sum)
 

time: 82.6 us -> 82.6 us (level)
  transfers between devices with their start and end apart: 6 -> 6, of which waited for: 4 -> 4; matrix products, arithmetic and copies ran while one was open for 1% -> 2% of each run, Pallas kernels for 13% -> 13%
where the time goes in v7:
time: 82.6 us; the launch traced here: 81.8 us
  waiting for transfers between devices  36.7 us (44%)
  starting transfers between devices  26.8 us (32%)
  Pallas kernels  14.2 us (17%)
  local copies, waits for them, and re-layouts  2.39 us (3%)
  between operations  0.9 us (1%)
    all_to_all x1, waiting for transfers between devices, body(): lax.all_to_all(weighted, BOTH, split_axis=0, concat_axis=0, tiled=True)  21.9 us
    ppermute x4, waiting for transfers between devices, swap(): return lax.ppermute(value, axis, pairs + [(j, i) for i, j in pairs])  14.9 us
    all_to_all x1, starting transfers between devices, body(): lax.all_to_all(weighted, BOTH, split_axis=0, concat_axis=0, tiled=True)  11.3 us
    ppermute x4, starting transfers between devices, swap(): return lax.ppermute(value, axis, pairs + [(j, i) for i, j in pairs])  9.88 us
    pallas_call x1, Pallas kernels, convolve_sum(): pl.pallas_call(functools.partial(coadd_kernel, margin), out_shape=tuple((...  6.23 us
    all_to_all x1, starting transfers between devices, body(): lax.all_to_all(kept, BOTH, split_axis=0, concat_axis=0, tiled=True)  5.63 us
    pallas_call x2, Pallas kernels, pack(): pl.pallas_call(functools.partial(pack_kernel, len(planes)), out_shape=jax...  5.59 us
    unnamed x16, local copies, waits for them, and re-layouts  1.91 us
  transfers between devices with their start and end apart: 6, of which 4 were waited for; matrix products, arithmetic and copies ran while one was open for 2% of the time, Pallas kernels for 13%

profile of v7, /device:TPU:3, one launch (start us, length us, event | category | flops | bytes accessed | tf_op | source)
XLA Modules:
  0.0 81.8 jit_solution(12569572006623321616)
XLA Ops:
  0.6 0.0 copy-start
  0.6 3.0 %pack.2 = bf16[128,16,512]{2,1,0:T(8,128)(2,1)} custom-call(s32[8192]{0:T(1024)} %bitcast.7, s32[8192]{0:T(1024)} %valid.3, bf16[64,16,512]{2,1,0:T(8,128)(2,1)} %refs_0_.3, bf16[64,16,512]{2,1,0:T(8,128)(2,1)} %refs_1_.1), custom_call_target="tpu_custom_call" | custom-call | flops 1048576 | bytes 4194304 | tf_op jit(solution)/shard_map/pack/pallas_call | solution.py:67
  3.6 0.0 copy-start.3
  3.6 0.0 copy-start.5
  3.6 0.0 copy-start.4
  3.7 0.0 copy-start.6
  3.7 11.3 %all-to-all-start = ((bf16[128,16,512]{2,1,0:T(8,128)(2,1)}), bf16[128,16,512]{2,1,0:T(8,128)(2,1)}, u32[]{:S(2)}, u32[]{:S(2)}) async-start(bf16[128,16,512]{2,1,0:T(8,128)(2,1)} %pack.2), calls=%async_computation | async-start | bytes 4194304 | tf_op jit(solution)/shard_map/all_to_all | solution.py:314
  15.0 0.0 copy-start.7
  15.0 0.0 copy-done.3
  15.0 0.1 compare_reduce_fusion
  15.1 0.1 eq.56
  15.2 0.0 copy-done.5
  15.2 0.1 reshape.124
  15.3 0.1 select_reduce_fusion
  15.4 0.0 copy-done.4
  15.4 0.1 slice.7
  15.5 0.1 rev.3
  15.6 0.1 add_select_fusion
  15.7 0.1 select_n.50
  15.8 0.0 copy-done.6
  15.8 0.1 pad.10.clone
  15.9 0.1 pad_maximum_fusion.down_taps
  16.0 0.5 band_tables.1
  16.5 0.0 copy-start.1
  16.5 1.0 %copy-done.1 = bf16[20,256,128]{2,1,0:T(8,128)(2,1)} copy-done((bf16[20,256,128]{2,1,0:T(8,128)(2,1)}, bf16[20,256,128]{2,1,0:T(8,128)(2,1)S(1)}, u32[]{:S(2)}) %copy-start.1) | copy-done | bytes 1310744
  17.5 0.0 copy-start.2
  17.5 0.8 %copy-done.2 = bf16[20,112,64]{2,1,0:T(8,128)(2,1)} copy-done((bf16[20,112,64]{2,1,0:T(8,128)(2,1)}, bf16[20,112,64]{2,1,0:T(8,128)(2,1)S(1)}, u32[]{:S(2)}) %copy-start.2) | copy-done | bytes 286744
  18.4 2.6 %pack.3 = bf16[128,16,512]{2,1,0:T(8,128)(2,1)} custom-call(s32[8192]{0:T(1024)} %bitcast.8, s32[8192]{0:T(1024)} %valid.3, bf16[64,16,512]{2,1,0:T(8,128)(2,1)} %refs_0_.3), custom_call_target="tpu_custom_call" | custom-call | flops 1048576 | bytes 3145728 | tf_op jit(solution)/shard_map/pack/pallas_call | solution.py:67
  21.0 0.0 copy-done
  21.0 0.0 copy-done.7
  21.0 0.2 convolution_bitcast_fusion
  21.4 21.9 %all-to-all-done.flux_far = bf16[128,16,512]{2,1,0:T(8,128)(2,1)} async-done(((bf16[128,16,512]{2,1,0:T(8,128)(2,1)}), bf16[128,16,512]{2,1,0:T(8,128)(2,1)}, u32[]{:S(2)}, u32[]{:S(2)}) %all-to-all-start) | async-done | bytes 2097184 | tf_op jit(solution)/shard_map/all_to_all | solution.py:314
  43.3 5.6 %all-to-all-start.1 = ((bf16[128,16,512]{2,1,0:T(8,128)(2,1)}), bf16[128,16,512]{2,1,0:T(8,128)(2,1)S(1)}, u32[]{:S(2)}, u32[]{:S(2)}) async-start(bf16[128,16,512]{2,1,0:T(8,128)(2,1)} %pack.3), calls=%async_computation.1 | async-start | bytes 4194304 | tf_op jit(solution)/shard_map/all_to_all | solution.py:340
  48.9 6.2 %convolve_sum.1 = (f32[64,640]{1,0:T(8,128)S(1)}, bf16[24,640]{1,0:T(8,128)(2,1)S(1)}, bf16[24,640]{1,0:T(8,128)(2,1)S(1)}) custom-call(bf16[128,16,512]{2,1,0:T(8,128)(2,1)} %all-to-all-done.flux_far, bf16[160,256]{1,0:T(8,128)(2,1)S(1)} %fusion.4.choose, bf16[20,112,64]{2,1,0:T(8,128)(2,1)} %copy-done.2, bf16[20,256,128]{2,1,0:T(8,128)(2,1)} %copy-done.1), custom_call_target="tpu_custom_call" | custom-call | flops 734003200 | bytes 2383872 | tf_op jit(solution)/shard_map/convolve_sum/pallas_call | solution.py:192
  55.2 1.5 %collective-permute-start = (bf16[24,640]{1,0:T(8,128)(2,1)S(1)}, bf16[24,640]{1,0:T(8,128)(2,1)S(1)}, u32[]{:S(2)}, u32[]{:S(2)}) collective-permute-start(bf16[24,640]{1,0:T(8,128)(2,1)S(1)} %get-tuple-element.18), channel_id=1, source_target_pairs={{0,1},{2,3},{4,5},{6,7},{8,9},{10,11},{12,13},{14,15},{1,0},{3,2},... | collective-permute-start | bytes 92168 | tf_op jit(solution)/shard_map/ppermute | solution.py:297
  56.6 4.0 %collective-permute-start.1 = (bf16[24,640]{1,0:T(8,128)(2,1)S(1)}, bf16[24,640]{1,0:T(8,128)(2,1)S(1)}, u32[]{:S(2)}, u32[]{:S(2)}) collective-permute-start(bf16[24,640]{1,0:T(8,128)(2,1)S(1)} %get-tuple-element.19), channel_id=1, source_target_pairs={{1,2},{3,4},{5,6},{7,8},{9,10},{11,12},{13,14},{2,1},{4,3},{6,5},{... | collective-permute-start | bytes 92168 | tf_op jit(solution)/shard_map/ppermute | solution.py:297
  60.6 3.9 %collective-permute-done.first = bf16[24,640]{1,0:T(8,128)(2,1)S(1)} collective-permute-done((bf16[24,640]{1,0:T(8,128)(2,1)S(1)}, bf16[24,640]{1,0:T(8,128)(2,1)S(1)}, u32[]{:S(2)}, u32[]{:S(2)}) %collective-permute-start) | collective-permute-done | bytes 30752 | tf_op jit(solution)/shard_map/ppermute | solution.py:297
  64.5 10.8 %collective-permute-done.1.second = bf16[24,640]{1,0:T(8,128)(2,1)S(1)} collective-permute-done((bf16[24,640]{1,0:T(8,128)(2,1)S(1)}, bf16[24,640]{1,0:T(8,128)(2,1)S(1)}, u32[]{:S(2)}, u32[]{:S(2)}) %collective-permute-start.1) | collective-permute-done | bytes 30752 | tf_op jit(solution)/shard_map/ppermute | solution.py:297
  75.3 4.4 %collective-permute-start.3 = (bf16[64,128]{1,0:T(8,128)(2,1)S(1)}, bf16[64,128]{1,0:T(8,128)(2,1)S(1)}, u32[]{:S(2)}, u32[]{:S(2)}) collective-permute-start(bf16[64,128]{1,0:T(8,128)(2,1)S(1)} %add_beside.1), channel_id=1, source_target_pairs={{16,32},{48,64},{80,96},{32,16},{64,48},{96,80},{17,33},{49,65},{8... | collective-permute-start | bytes 49160 | tf_op jit(solution)/shard_map/ppermute | solution.py:297
  79.7 0.1 collective-permute-start.2
  79.8 0.0 all-to-all-done.1.kept
  79.8 1.1 %place_weights.1 = f32[64,512]{1,0:T(8,128)} custom-call(bf16[64,2048]{1,0:T(8,128)(2,1)S(1)} %fusion.chosen, bf16[128,16,512]{2,1,0:T(8,128)(2,1)S(1)} %all-to-all-done.1.kept), custom_call_target="tpu_custom_call" | custom-call | flops 134217728 | bytes 2097152 | tf_op jit(solution)/shard_map/place_weights/pallas_call | solution.py:228
  80.9 0.2 collective-permute-done.3.far
  81.1 0.0 collective-permute-done.2.near
  81.1 0.7 finish.1
  (10 shorter events, 0.2 us)
Async XLA Ops:
  0.6 20.4 %copy-start = (f32[64,20]{0,1:T(8,128)S(1)}, f32[64,20]{0,1:T(8,128)}, u32[]{:S(2)}) copy-start(f32[64,20]{0,1:T(8,128)} %param.15) | copy-start | bytes 15364
  3.6 11.4 %copy-start.3 = (s32[8192,1]{0,1:T(1,128)S(1)}, s32[8192,1]{0,1:T(1,128)}, u32[]{:S(2)}) copy-start(s32[8192,1]{0,1:T(1,128)} %param.11) | copy-start | bytes 98308
  3.6 11.6 %copy-start.5 = (s32[8192]{0:T(1024)S(1)}, s32[8192]{0:T(1024)}, u32[]{:S(2)}) copy-start(s32[8192]{0:T(1024)} %param.12) | copy-start | bytes 98308
  3.6 11.8 %copy-start.4 = (f32[20,41]{1,0:T(8,128)S(1)}, f32[20,41]{1,0:T(8,128)}, u32[]{:S(2)}) copy-start(f32[20,41]{1,0:T(8,128)} %param.17) | copy-start | bytes 9844
  3.7 12.1 %copy-start.6 = (f32[20,41]{1,0:T(8,128)S(1)}, f32[20,41]{1,0:T(8,128)}, u32[]{:S(2)}) copy-start(f32[20,41]{1,0:T(8,128)} %param.16) | copy-start | bytes 9844
  3.7 39.6 %all-to-all-start = ((bf16[128,16,512]{2,1,0:T(8,128)(2,1)}), bf16[128,16,512]{2,1,0:T(8,128)(2,1)}, u32[]{:S(2)}, u32[]{:S(2)}) async-start(bf16[128,16,512]{2,1,0:T(8,128)(2,1)} %pack.2), calls=%async_computation | async-start | bytes 4194304 | tf_op jit(solution)/shard_map/all_to_all | solution.py:314
  15.0 6.1 %copy-start.7 = (s32[128]{0:T(128)S(1)}, s32[128]{0:T(128)}, u32[]{:S(2)}) copy-start(s32[128]{0:T(128)} %param.14) | copy-start | bytes 1540
  16.5 1.1 %copy-start.1 = (bf16[20,256,128]{2,1,0:T(8,128)(2,1)}, bf16[20,256,128]{2,1,0:T(8,128)(2,1)S(1)}, u32[]{:S(2)}) copy-start(bf16[20,256,128]{2,1,0:T(8,128)(2,1)S(1)} %get-tuple-element.16.across_far) | copy-start | bytes 3932164
  17.5 0.8 %copy-start.2 = (bf16[20,112,64]{2,1,0:T(8,128)(2,1)}, bf16[20,112,64]{2,1,0:T(8,128)(2,1)S(1)}, u32[]{:S(2)}) copy-start(bf16[20,112,64]{2,1,0:T(8,128)(2,1)S(1)} %get-tuple-element.15.down_far) | copy-start | bytes 860164
  43.3 36.5 %all-to-all-start.1 = ((bf16[128,16,512]{2,1,0:T(8,128)(2,1)}), bf16[128,16,512]{2,1,0:T(8,128)(2,1)S(1)}, u32[]{:S(2)}, u32[]{:S(2)}) async-start(bf16[128,16,512]{2,1,0:T(8,128)(2,1)} %pack.3), calls=%async_computation.1 | async-start | bytes 4194304 | tf_op jit(solution)/shard_map/all_to_all | solution.py:340
  55.2 9.3 %collective-permute-start = (bf16[24,640]{1,0:T(8,128)(2,1)S(1)}, bf16[24,640]{1,0:T(8,128)(2,1)S(1)}, u32[]{:S(2)}, u32[]{:S(2)}) collective-permute-start(bf16[24,640]{1,0:T(8,128)(2,1)S(1)} %get-tuple-element.18), channel_id=1, source_target_pairs={{0,1},{2,3},{4,5},{6,7},{8,9},{10,11},{12,13},{14,15},{1,0},{3,2},... | collective-permute-start | bytes 92168 | tf_op jit(solution)/shard_map/ppermute | solution.py:297
  56.6 18.6 %collective-permute-start.1 = (bf16[24,640]{1,0:T(8,128)(2,1)S(1)}, bf16[24,640]{1,0:T(8,128)(2,1)S(1)}, u32[]{:S(2)}, u32[]{:S(2)}) collective-permute-start(bf16[24,640]{1,0:T(8,128)(2,1)S(1)} %get-tuple-element.19), channel_id=1, source_target_pairs={{1,2},{3,4},{5,6},{7,8},{9,10},{11,12},{13,14},{2,1},{4,3},{6,5},{... | collective-permute-start | bytes 92168 | tf_op jit(solution)/shard_map/ppermute | solution.py:297
  75.3 5.8 %collective-permute-start.3 = (bf16[64,128]{1,0:T(8,128)(2,1)S(1)}, bf16[64,128]{1,0:T(8,128)(2,1)S(1)}, u32[]{:S(2)}, u32[]{:S(2)}) collective-permute-start(bf16[64,128]{1,0:T(8,128)(2,1)S(1)} %add_beside.1), channel_id=1, source_target_pairs={{16,32},{48,64},{80,96},{32,16},{64,48},{96,80},{17,33},{49,65},{8... | collective-permute-start | bytes 49160 | tf_op jit(solution)/shard_map/ppermute | solution.py:297
  79.7 1.4 %collective-permute-start.2 = (bf16[64,128]{1,0:T(8,128)(2,1)S(1)}, bf16[64,128]{1,0:T(8,128)(2,1)S(1)}, u32[]{:S(2)}, u32[]{:S(2)}) collective-permute-start(bf16[64,128]{1,0:T(8,128)(2,1)S(1)} %add_beside.1), channel_id=1, source_target_pairs={{0,16},{32,48},{64,80},{96,112},{16,0},{48,32},{80,64},{112,96},{1... | collective-permute-start | bytes 49160 | tf_op jit(solution)/shard_map/ppermute | solution.py:297
